TPU v7x, 32 devices: a whole 2x2x4 slice. The times are simulated.
32 devices in a mesh: gx: 2 (over core), gy: 4 (over z), gz: 4 (over y, x).
Axes of the slice: x: 2, y: 2, z: 4, core: 2. Of those that a mesh axis runs over, the one named last changes fastest.
Arguments:
- positions: float32 [2, 4, 4, 2, 3, 128], P('gx', 'gy', 'gz'), may hold values from 0 to 12, as said below
- features: bfloat16 [2, 4, 4, 2, 128, 128], P('gx', 'gy', 'gz'), may hold values from -6 to 6
- counts: int32 [2, 4, 4, 2], P('gx', 'gy', 'gz'), may hold values from 0 to 128, as said below
- neighbours: int32 [2, 4, 4, 2, 8], P('gx', 'gy', 'gz'), may hold values from -1 to 53, as said below
- mix_weight: bfloat16 [1024, 128], replicated, may hold values from -0.1875 to 0.1875
- readout: float32 [128], replicated, may hold values from -4 to 4
- radial_rates: float32 [4], replicated, may hold values from 0.03 to 0.6
Outputs:
- forces: float32 [2, 4, 4, 2, 3, 128], P('gx', 'gy', 'gz')
- feature_grads: float32 [2, 4, 4, 2, 128, 128], P('gx', 'gy', 'gz')
Inputs may be any that keep to these rules, and one draw needn't show every extreme that they name: The atoms of a tile fill its first counts slots; a count of 0 marks a tile slot that its device doesn't own; every draw has a tile with 128 atoms. neighbours[.., t, s] names a tile of the device's neighbourhood as ((dx + 1) * 9 + (dy + 1) * 3 + (dz + 1)) * 2 + u, dx, dy, dz in -1..1 being the device offsets along gx, gy, gz and u the tile slot; slot 0 names tile t itself, every other used slot names a tile with one or more atoms, the entries of a row differ, and -1 marks unused slots, which come after the used ones. `positions`: the atoms of device (a, b, c) lie in the cube of side 3 whose lowest corner is 3 (a, b, c).
All inputs are finite; a program needn't handle non-finite values.
Results may differ from a plain program's by a relative error of at most 0.0008.
Values may be sent and summed in bfloat16 or wider, within the bound.
No kernel may reach another device: no remote copies, remote signals or barrier semaphores. Data moves between devices by JAX's collectives and lax.ppermute only.
A program may use at most 64 MiB of HBM per device.

v0:
```python
import functools

import jax
import jax.numpy as jnp
from jax import lax
from jax.experimental import pallas as pl
from jax.experimental.pallas import tpu as pltpu
from jax.sharding import PartitionSpec as P


ROWS = 32
EXTRA = 8
TOP = 14.0
TINY = 1e-30
GROUP = 8
LOG2E = 1.4426950408889634
SMALL = 8 << 20
LARGE = 30 << 20
NT = (((1,), (1,)), ((), ()))


def swaps(axis):
    count = lax.axis_size(axis)
    result = []
    for first in (0, 1):
        pairs = [(i, i + 1) for i in range(first, count - 1, 2)]
        if pairs:
            result.append(pairs + [(b, a) for a, b in pairs])
    return result


def side_of(step, parity, sides):
    side = jnp.where((step == 1) == (parity == 0), 1, 2)
    return jnp.minimum(jnp.where(step == 0, 0, side), sides)


def pack_kernel(
    counts_ref,
    neighbours_ref,
    rates_ref,
    readout_ref,
    features_ref,
    points_ref,
    packed_ref,
    out_neighbours_ref,
    out_rates_ref,
    out_readout_ref,
    buffer_ref,
    place_ref,
    extra_ref,
    sems,
):
    loads = [
        pltpu.make_async_copy(features_ref, buffer_ref, sems.at[0]),
        pltpu.make_async_copy(points_ref, place_ref, sems.at[1]),
    ]
    for load in loads:
        load.start()
    tiles, atoms, _ = features_ref.shape
    for t in range(tiles):
        for k in range(neighbours_ref.shape[1]):
            out_neighbours_ref[t, k] = neighbours_ref[t, k]
    for r in range(rates_ref.shape[0]):
        out_rates_ref[r] = rates_ref[r]
    out_readout_ref[...] = readout_ref[...]
    extra_ref[...] = jnp.zeros_like(extra_ref)
    for load in loads:
        load.wait()
    for t in range(tiles):
        count = counts_ref[t]
        rows = lax.broadcasted_iota(jnp.int32, features_ref.shape[1:], 0)
        values = buffer_ref[t].astype(jnp.float32)
        packed_ref[t, :atoms] = jnp.where(rows < count, values, 0.0).astype(jnp.bfloat16)
        rest = place_ref[:, t, :]
        for term in range(3):
            part = rest.astype(jnp.bfloat16).astype(jnp.float32)
            extra_ref[t, 3 * term : 3 * term + 3] = part
            rest = rest - part
        packed_ref[t, atoms:] = extra_ref[t].astype(jnp.bfloat16)


def join_kernel(groups, *refs):
    inputs = refs[: -len(groups)]
    for group, out_ref in zip(groups, refs[-len(groups) :]):
        at = 0
        for k in group:
            count = inputs[k].shape[0]
            out_ref[at : at + count] = inputs[k][...]
            at += count


def join(groups, *arrays):
    shapes = [
        jax.ShapeDtypeStruct(
            (sum(arrays[k].shape[0] for k in group),) + arrays[0].shape[1:], arrays[0].dtype
        )
        for group in groups
    ]
    vmem = pl.BlockSpec(memory_space=pltpu.VMEM)
    return pl.pallas_call(
        functools.partial(join_kernel, groups),
        out_shape=shapes,
        in_specs=[vmem] * len(arrays),
        out_specs=[vmem] * len(groups),
        compiler_params=pltpu.CompilerParams(vmem_limit_bytes=SMALL),
        name="join",
    )(*arrays)


def decoded(ref, rows):
    value = ref[rows]
    channels = value.shape[1] - EXTRA
    grads = value[:, :channels] * jnp.exp2(value[:, channels + 3 : channels + 4] - TOP)
    forces = value[:, channels : channels + 3] * jnp.exp2(
        value[:, channels + 4 : channels + 5] - TOP
    )
    return grads, forces


def fold_kernel(cuts, plain, coded, *refs):
    plain_refs, coded_refs = refs[:plain], refs[plain : plain + coded]
    for (low, high, code), out_ref in zip(cuts, refs[plain + coded :]):
        channels = out_ref.shape[1] - EXTRA
        rows = slice(low, high)
        grads = forces = None
        for ref in plain_refs:
            part = ref[rows]
            grads = part[:, :channels] if grads is None else grads + part[:, :channels]
            part = part[:, channels : channels + 3]
            forces = part if forces is None else forces + part
        for ref in coded_refs:
            one, two = decoded(ref, rows)
            grads, forces = grads + one, forces + two
        if not code:
            out_ref[:, :channels] = grads
            out_ref[:, channels : channels + 3] = forces
            continue
        for first, value, at in ((0, grads, 3), (channels, forces, 4)):
            bound = jnp.max(jnp.abs(value), axis=1, keepdims=True)
            exponent = jnp.ceil(jnp.log2(jnp.maximum(bound, TINY)))
            out_ref[:, first : first + value.shape[1]] = value * jnp.exp2(TOP - exponent)
            out_ref[:, channels + at : channels + at + 1] = exponent


def fold(cuts, plain, coded):
    arrays = list(plain) + list(coded)
    shapes = [
        jax.ShapeDtypeStruct((high - low,) + arrays[0].shape[1:], jnp.float32)
        for low, high, _ in cuts
    ]
    vmem = pl.BlockSpec(memory_space=pltpu.VMEM)
    return pl.pallas_call(
        functools.partial(fold_kernel, cuts, len(plain), len(coded)),
        out_shape=shapes,
        in_specs=[vmem] * len(arrays),
        out_specs=[vmem] * len(cuts),
        compiler_params=pltpu.CompilerParams(vmem_limit_bytes=SMALL),
        name="fold",
    )(*arrays)


def send(value, axis, pairs):
    return lax.ppermute(value.astype(jnp.float16), axis, pairs).astype(jnp.float32)


def main_kernel(
    pieces,
    sides,
    slots,
    axis_ref,
    counts_ref,
    neighbours_ref,
    rates_ref,
    points_ref,
    mixing_ref,
    readout_ref,
    *refs,
):
    piece_refs = refs[:pieces]
    ghost_refs = refs[pieces : 2 * pieces]
    (
        near_ref,
        own_ref,
        other_ref,
        features_ref,
        basis_ref,
        sum_ref,
        seed_ref,
        seed_t_ref,
        near_grad_ref,
        near_force_ref,
        own_force_ref,
        ghost_ref,
        in_sems,
        out_sems,
        *grad_refs,
    ) = refs[2 * pieces :]
    _, tiles, atoms = points_ref.shape
    channels = readout_ref.shape[1]
    radials = rates_ref.shape[0]
    bases = 4 * radials
    group_rows = bases * GROUP
    groups = ROWS // GROUP
    chunk_rows = bases * ROWS
    couples = (slots + 1) // 2
    scaling = (slots * atoms) ** (-0.5)
    starts = [sum(ref.shape[0] for ref in piece_refs[:k]) for k in range(pieces)]
    cross = 1 + sides[1] + sides[2]
    blocks = (sides[1] + 1) * (sides[2] + 1)

    loads = [
        pltpu.make_async_copy(
            piece_refs[k], near_ref.at[pl.ds(starts[k], piece_refs[k].shape[0])], in_sems.at[k]
        )
        for k in range(pieces)
    ]
    for load in loads:
        load.start()

    for t in range(tiles):
        lines = [points_ref[m, t : t + 1, :] for m in range(3)]
        lines.append(jnp.zeros((atoms - 3, atoms), jnp.float32))
        columns = jnp.transpose(jnp.concatenate(lines, axis=0))
        for m in range(3):
            own_ref[t, m] = jnp.broadcast_to(columns[:, m : m + 1], (atoms, atoms))
    ghost_ref[...] = jnp.zeros_like(ghost_ref)
    own_force_ref[...] = jnp.zeros_like(own_force_ref)

    for load in loads:
        load.wait()

    def located(target):
        target = jnp.maximum(target, 0)
        block = lax.div(target, tiles)
        steps = (lax.div(block, 9), lax.rem(lax.div(block, 3), 3), lax.rem(block, 3))
        x, y, z = (side_of(steps[k] - 1, axis_ref[k], sides[k]) for k in range(3))
        diagonal = cross + (y - 1) * sides[2] + (z - 1)
        straight = jnp.where(y == 0, z, sides[2] + y)
        block = jnp.where((y > 0) & (z > 0), diagonal, straight)
        return (x * blocks + block) * tiles + lax.rem(target, tiles)

    rates = [rates_ref[r] for r in range(radials)]
    powers = [-rate * LOG2E for rate in rates]

    def geometry(t, slot, where):
        offset = [other_ref[t, slot, m] - own_ref[t, m, where, :] for m in range(3)]
        square = offset[0] * offset[0] + offset[1] * offset[1] + offset[2] * offset[2]
        return offset, [jnp.exp2(power * square) for power in powers]

    for t in range(tiles):
        count = counts_ref[t]
        chunks = (count + (ROWS - 1)) // ROWS

        def work(t=t, count=count, chunks=chunks):
            live = 0
            for k in range(slots):
                target = neighbours_ref[t, k]
                live = live + jnp.where(target >= 0, 1, 0)
                tile = located(target)
                values = near_ref[tile, :atoms, :]
                features_ref[t, k * atoms : (k + 1) * atoms] = jnp.where(
                    target >= 0, values, jnp.zeros_like(values)
                )
                extra = near_ref[tile, atoms:, :].astype(jnp.float32)
                total = extra[0:3] + extra[3:6] + extra[6:9]
                for m in range(3):
                    other_ref[t, k, m] = jnp.broadcast_to(total[m : m + 1, :], (GROUP, atoms))
            for k in range(slots, 2 * couples + 2):
                features_ref[t, k * atoms : (k + 1) * atoms] = jnp.zeros((atoms, channels), jnp.bfloat16)
                for m in range(3):
                    other_ref[t, k, m] = jnp.zeros((GROUP, atoms), jnp.float32)

            def forward(chunk, carry):
                start = pl.multiple_of(chunk * ROWS, ROWS)
                base = pl.multiple_of(chunk * chunk_rows, chunk_rows)
                for slot in range(2 * couples):
                    for g in range(groups):
                        offset, radial = geometry(t, slot, pl.ds(start + g * GROUP, GROUP))
                        for r in range(radials):
                            values = [radial[r]] + [radial[r] * offset[m] for m in range(3)]
                            for k in range(2):
                                pair = jnp.concatenate(values[2 * k : 2 * k + 2], axis=0)
                                row = base + g * group_rows + (4 * r + 2 * k) * GROUP
                                basis_ref[t, slot, pl.ds(row, 2 * GROUP), :] = pair.astype(
                                    jnp.bfloat16
                                )
                where = pl.ds(base, chunk_rows)
                basis = [basis_ref[t, slot, where, :] for slot in range(2 * couples)]
                sum_ref[t, where, :] = (
                    jnp.dot(
                        jnp.concatenate(basis, axis=1),
                        features_ref[t, : 2 * couples * atoms],
                        preferred_element_type=jnp.float32,
                    )
                    * scaling
                )
                return carry

            lax.fori_loop(0, chunks, forward, 0)

            def clear(chunk, carry):
                where = pl.ds(pl.multiple_of(chunk * chunk_rows, chunk_rows), chunk_rows)
                sum_ref[t, where, :] = jnp.zeros((chunk_rows, channels), jnp.float32)
                return carry

            lax.fori_loop(chunks, atoms // ROWS, clear, 0)

            def sums(r, m):
                first = (4 * r + m) * GROUP
                return jnp.concatenate(
                    [
                        sum_ref[t, g * group_rows + first : g * group_rows + first + GROUP, :]
                        for g in range(atoms // GROUP)
                    ],
                    axis=0,
                )

            parts = [sums(r, 0) for r in range(radials)]
            for r in range(radials):
                norm = None
                for m in range(1, 4):
                    value = sums(r, m)
                    norm = value * value if norm is None else norm + value * value
                parts.append(norm)
            invariant = jnp.concatenate([part.astype(jnp.bfloat16) for part in parts], axis=1)
            preact = jnp.dot(invariant, mixing_ref[...], preferred_element_type=jnp.float32)
            sigmoid = jax.nn.sigmoid(preact)
            row = lax.broadcasted_iota(jnp.int32, (atoms, channels), 0)
            valid = (row < count).astype(jnp.float32)
            grad_pre = valid * readout_ref[...] * sigmoid * (1.0 + preact * (1.0 - sigmoid))
            grad = lax.dot_general(
                grad_pre.astype(jnp.bfloat16),
                mixing_ref[...],
                NT,
                preferred_element_type=jnp.float32,
            )
            for r in range(radials):
                scalar = grad[:, r * channels : (r + 1) * channels] * scaling
                square = grad[:, (radials + r) * channels : (radials + r + 1) * channels]
                square = square * (2.0 * scaling)
                values = [scalar] + [square * sums(r, m) for m in range(1, 4)]
                for g in range(atoms // GROUP):
                    rows = slice(g * GROUP, (g + 1) * GROUP)
                    for k in range(2):
                        pair = jnp.concatenate(
                            [value[rows] for value in values[2 * k : 2 * k + 2]], axis=0
                        )
                        first = g * group_rows + (4 * r + 2 * k) * GROUP
                        seed_ref[t, first : first + 2 * GROUP, :] = pair.astype(jnp.bfloat16)
            for chunk in range(atoms // ROWS):
                rows = slice(chunk * chunk_rows, (chunk + 1) * chunk_rows)
                seed_t_ref[t, chunk] = jnp.transpose(seed_ref[t, rows, :])

            near_grad_ref[...] = jnp.zeros_like(near_grad_ref)
            near_force_ref[...] = jnp.zeros_like(near_force_ref)
            active = (live + 1) // 2
            steps = active * chunks

            def following(place):
                couple, chunk = place
                wrap = chunk + 1 >= chunks
                couple = jnp.where(wrap, couple + 1, couple)
                return jnp.where(couple < active, couple, couples), jnp.where(wrap, 0, chunk + 1)

            def multiply(place, grad_ref):
                couple, chunk = place
                base = pl.multiple_of(chunk * chunk_rows, chunk_rows)
                where = pl.ds(base, chunk_rows)
                grad_ref[...] = lax.dot_general(
                    seed_ref[t, where, :],
                    features_ref[
                        t, pl.ds(pl.multiple_of(couple * 2 * atoms, 2 * atoms), 2 * atoms), :
                    ],
                    NT,
                    preferred_element_type=jnp.float32,
                )
                stored = jnp.minimum(couple, couples - 1)
                basis = [basis_ref[t, 2 * stored + half, where, :] for half in range(2)]
                near_grad_ref[couple] += jnp.dot(
                    seed_t_ref[t, chunk],
                    jnp.concatenate(basis, axis=1),
                    preferred_element_type=jnp.float32,
                )

            def pull(place, grad_ref):
                couple, chunk = place
                start = pl.multiple_of(chunk * ROWS, ROWS)
                pulled = [[None] * 3 for _ in range(2)]
                for g in range(groups):
                    rows = pl.ds(start + g * GROUP, GROUP)
                    total = [None] * 3
                    for half in range(2):
                        lanes = slice(half * atoms, (half + 1) * atoms)
                        offset, radial = geometry(t, 2 * couple + half, rows)
                        direct = [None] * 3
                        inner = None
                        for r in range(radials):
                            row = g * group_rows + 4 * r * GROUP
                            grad = [
                                grad_ref[row + m * GROUP : row + (m + 1) * GROUP, lanes]
                                for m in range(4)
                            ]
                            along = grad[0]
                            for m in range(3):
                                along = along + grad[m + 1] * offset[m]
                                part = radial[r] * grad[m + 1]
                                direct[m] = part if r == 0 else direct[m] + part
                            part = (radial[r] * (2.0 * rates[r])) * along
                            inner = part if r == 0 else inner + part
                        for m in range(3):
                            force = direct[m] - offset[m] * inner
                            total[m] = force if half == 0 else total[m] + force
                            old = pulled[half][m]
                            pulled[half][m] = force if g == 0 else old + force
                    for m in range(3):
                        own_force_ref[t, m, rows, :] += total[m]
                for half in range(2):
                    for m in range(3):
                        near_force_ref[couple, half, m] += pulled[half][m]

            zero = jnp.zeros((), jnp.int32)
            first = (zero, zero)
            places = (first, following(first))
            multiply(places[0], grad_refs[0])
            multiply(places[1], grad_refs[1])

            def backward(k, places):
                one, two = places
                three = following(two)
                four = following(three)
                five = following(four)
                six = following(five)
                pull(one, grad_refs[0])
                multiply(three, grad_refs[2])
                pull(two, grad_refs[1])
                multiply(four, grad_refs[3])
                pull(three, grad_refs[2])
                multiply(five, grad_refs[0])
                pull(four, grad_refs[3])
                multiply(six, grad_refs[1])
                return five, six

            lax.fori_loop(0, (steps + 3) // 4, backward, places)

            for slot in range(slots):
                target = neighbours_ref[t, slot]

                def give(slot=slot, target=target):
                    tile = located(target)
                    couple, half = divmod(slot, 2)
                    lanes = slice(half * atoms, (half + 1) * atoms)
                    ghost_ref[tile, :channels, :] += near_grad_ref[couple, :, lanes]
                    for m in range(3):
                        ghost_ref[tile, channels + m : channels + m + 1, :] -= jnp.sum(
                            near_force_ref[couple, half, m], axis=0, keepdims=True
                        )

                pl.when(target >= 0)(give)
            for m in range(3):
                ghost_ref[t, channels + m : channels + m + 1, :] += jnp.sum(
                    jnp.transpose(own_force_ref[t, m]), axis=0, keepdims=True
                )

        pl.when(count > 0)(work)

    stores = [
        pltpu.make_async_copy(
            ghost_ref.at[pl.ds(starts[k], piece_refs[k].shape[0])], ghost_refs[k], out_sems.at[k]
        )
        for k in range(pieces)
    ]
    for store in stores:
        store.start()
    for store in stores:
        store.wait()


def final_kernel(counts_ref, center_ref, *refs):
    coded_refs = refs[:-2]
    forces_ref, grads_ref = refs[-2:]
    tiles, channels, atoms = grads_ref.shape
    for t in range(tiles):
        rows = slice(t, t + 1)
        grads = center_ref[rows, :channels]
        forces = center_ref[rows, channels : channels + 3]
        for ref in coded_refs:
            one, two = decoded(ref, rows)
            grads, forces = grads + one, forces + two
        forces_ref[:, t, :] = forces[0]
        column = lax.broadcasted_iota(jnp.int32, (channels, atoms), 1)
        masked = jnp.where(column < counts_ref[t], grads[0], 0.0)
        grads_ref[t] = jnp.transpose(masked)


def step(positions, features, counts, neighbours, mix_weight, readout, radial_rates):
    tiles, atoms = positions.shape[3], positions.shape[5]
    channels = features.shape[5]
    slots = neighbours.shape[4]
    radials = radial_rates.shape[0]
    vmem = pl.BlockSpec(memory_space=pltpu.VMEM)
    smem = pl.BlockSpec(memory_space=pltpu.SMEM)
    hbm = pl.BlockSpec(memory_space=pl.ANY)
    far = pl.BlockSpec(memory_space=pltpu.HBM)
    small = pltpu.CompilerParams(vmem_limit_bytes=SMALL)

    def swap(value, axis):
        return [lax.ppermute(value, axis, pairs) for pairs in swaps(axis)]

    sides = tuple(len(swaps(axis)) for axis in ("gx", "gy", "gz"))
    own_counts = counts.reshape(tiles)
    points = jnp.transpose(positions, (0, 1, 2, 4, 3, 5)).reshape(3, tiles, atoms)
    packed, neighbours, rates, readout = pl.pallas_call(
        pack_kernel,
        out_shape=[
            jax.ShapeDtypeStruct((tiles, atoms + 16, channels), jnp.bfloat16),
            jax.ShapeDtypeStruct((tiles, slots), jnp.int32),
            jax.ShapeDtypeStruct((radials,), jnp.float32),
            jax.ShapeDtypeStruct((1, channels), jnp.float32),
        ],
        in_specs=[smem, smem, smem, vmem, far, far],
        out_specs=[vmem, smem, smem, vmem],
        scratch_shapes=[
            pltpu.VMEM((tiles, atoms, channels), jnp.bfloat16),
            pltpu.VMEM((3, tiles, atoms), jnp.float32),
            pltpu.VMEM((tiles, 16, channels), jnp.float32),
            pltpu.SemaphoreType.DMA((2,)),
        ],
        compiler_params=pltpu.CompilerParams(vmem_limit_bytes=60 << 20),
        name="pack",
    )(
        own_counts,
        neighbours.reshape(tiles, slots),
        radial_rates,
        readout.reshape(1, channels),
        features.reshape(tiles, atoms, channels),
        points,
    )

    along_z = swap(packed, "gz")
    (line,) = join([list(range(len(along_z)))], *along_z)
    along_y = swap(packed, "gy")
    diagonal = swap(line, "gy")
    (cross,) = join([list(range(2 + len(along_y)))], packed, line, *along_y)
    pieces = [[cross] + diagonal]
    for pairs in swaps("gx"):
        plane = [lax.ppermute(cross, "gx", pairs)]
        pieces.append(plane + [lax.ppermute(piece, "gx", pairs) for piece in diagonal])
    flat = [piece for plane in pieces for piece in plane]

    total = sum(piece.shape[0] for piece in flat)
    couples = (slots + 1) // 2
    bases = 4 * radials
    chunks = atoms // ROWS
    ghost_rows = channels + EXTRA
    position = jnp.stack([lax.axis_index(axis) % 2 for axis in ("gx", "gy", "gz")])
    ghosts = pl.pallas_call(
        functools.partial(main_kernel, len(flat), sides, slots),
        out_shape=[
            jax.ShapeDtypeStruct((piece.shape[0], ghost_rows, atoms), jnp.float32)
            for piece in flat
        ],
        in_specs=[smem] * 4 + [vmem] * 3 + [hbm] * len(flat),
        out_specs=[hbm] * len(flat),
        scratch_shapes=[
            pltpu.VMEM((total, atoms + 16, channels), jnp.bfloat16),
            pltpu.VMEM((tiles, 3, atoms, atoms), jnp.float32),
            pltpu.VMEM((tiles, 2 * couples + 2, 3, GROUP, atoms), jnp.float32),
            pltpu.VMEM((tiles, (2 * couples + 2) * atoms, channels), jnp.bfloat16),
            pltpu.VMEM((tiles, 2 * couples, bases * atoms, atoms), jnp.bfloat16),
            pltpu.VMEM((tiles, bases * atoms, channels), jnp.float32),
            pltpu.VMEM((tiles, bases * atoms, channels), jnp.bfloat16),
            pltpu.VMEM((tiles, chunks, channels, bases * ROWS), jnp.bfloat16),
            pltpu.VMEM((couples + 1, channels, 2 * atoms), jnp.float32),
            pltpu.VMEM((couples + 1, 2, 3, GROUP, atoms), jnp.float32),
            pltpu.VMEM((tiles, 3, atoms, atoms), jnp.float32),
            pltpu.VMEM((total, ghost_rows, atoms), jnp.float32),
            pltpu.SemaphoreType.DMA((len(flat),)),
            pltpu.SemaphoreType.DMA((len(flat),)),
        ]
        + [pltpu.VMEM((bases * ROWS, 2 * atoms), jnp.float32)] * 4,
        compiler_params=pltpu.CompilerParams(vmem_limit_bytes=LARGE),
        name="pairs",
    )(
        position,
        own_counts,
        neighbours,
        rates,
        points,
        mix_weight,
        readout,
        *flat,
    )

    width = len(pieces[0])
    ghosts = [ghosts[k * width : (k + 1) * width] for k in range(len(pieces))]

    def gather(k):
        arrays = [ghosts[0][k]]
        for plane, pairs in zip(ghosts[1:], swaps("gx")):
            arrays.append(lax.ppermute(plane[k], "gx", pairs))
        return arrays

    diagonal = []
    for k, pairs in enumerate(swaps("gy")):
        arrays = gather(k + 1)
        (value,) = fold([(0, arrays[0].shape[0], True)], arrays, [])
        diagonal.append(send(value, "gy", pairs))
    arrays = gather(0)
    line = (sides[2] + 1) * tiles
    cuts = [(0, tiles, False), (tiles, line, False)]
    for k in range(sides[1]):
        cuts.append((line + k * tiles, line + (k + 1) * tiles, True))
    center, along_z, *along_y = fold(cuts, arrays, [])
    cuts = [(k * tiles, (k + 1) * tiles, True) for k in range(sides[2])]
    along_z = fold(cuts, [along_z], diagonal)
    parts = [center]
    for values, axis in ((along_z, "gz"), (along_y, "gy")):
        for value, pairs in zip(values, swaps(axis)):
            parts.append(send(value, axis, pairs))

    forces, grads = pl.pallas_call(
        final_kernel,
        out_shape=[
            jax.ShapeDtypeStruct((3, tiles, atoms), jnp.float32),
            jax.ShapeDtypeStruct((tiles, channels, atoms), jnp.float32),
        ],
        in_specs=[smem] + [vmem] * len(parts),
        out_specs=[vmem, vmem],
        compiler_params=small,
        name="finish",
    )(own_counts, *parts)
    forces = jnp.transpose(forces.reshape(1, 1, 1, 3, tiles, atoms), (0, 1, 2, 4, 3, 5))
    return forces, grads.reshape(1, 1, 1, tiles, atoms, channels)


def solution(mesh):
    in_specs = (
        P("gx", "gy", "gz", None, None, None),
        P("gx", "gy", "gz", None, None, None),
        P("gx", "gy", "gz", None),
        P("gx", "gy", "gz", None, None),
        P(),
        P(),
        P(),
    )
    out_specs = (P("gx", "gy", "gz", None, None, None), P("gx", "gy", "gz", None, None, None))
    return jax.shard_map(step, mesh=mesh, in_specs=in_specs, out_specs=out_specs, check_vma=False)
```

profile of v0, /device:TPU:0, one launch (start us, length us, event | category | flops | bytes accessed | tf_op | source)
XLA Modules:
  0.0 62.7 jit_solution(6894589565499387160)
XLA Ops:
  0.6 2.2 %pack.1 = (bf16[2,144,128]{2,1,0:T(8,128)(2,1)}, s32[2,8]{1,0:T(2,128)}, f32[4]{0:T(128)}, f32[1,128]{1,0:T(1,128)}) custom-call(s32[2]{0:T(128)} %bitcast.16, s32[2,8]{1,0:T(2,128)} %bitcast.20, f32[4]{0:T(128)} %rates_ref.1, f32[1,128]{1,0:T(1,128)} %bitcast.21, bf16[2,128,128]{2,1,0:T(8,128)(2,1)} %bitcast.19, f32[3,2,128]{2,1,0:T(2,128)} %bitcast.14), custom_call_target="tpu_custom_call" | custom-call | tf_op jit(solution)/shard_map/pack/pallas_call | solution.py:512
  2.9 0.8 %collective-permute-start.1 = (bf16[2,144,128]{2,1,0:T(8,128)(2,1)}, bf16[2,144,128]{2,1,0:T(8,128)(2,1)S(1)}, u32[]{:S(2)}, u32[]{:S(2)}) collective-permute-start(bf16[2,144,128]{2,1,0:T(8,128)(2,1)} %get-tuple-element.23.refs_0_), channel_id=1, source_target_pairs={{1,2},{2,1},{5,6},{6,5},{9,10},{10,9},{13,14},{14,13},{17,18},{18,... | collective-permute-start | bytes 221192 | tf_op jit(solution)/shard_map/ppermute | solution.py:507
  3.7 5.8 %collective-permute-start = (bf16[2,144,128]{2,1,0:T(8,128)(2,1)}, bf16[2,144,128]{2,1,0:T(8,128)(2,1)S(1)}, u32[]{:S(2)}, u32[]{:S(2)}) collective-permute-start(bf16[2,144,128]{2,1,0:T(8,128)(2,1)} %get-tuple-element.23.refs_0_), channel_id=1, source_target_pairs={{0,1},{2,3},{1,0},{3,2},{4,5},{6,7},{5,4},{7,6},{8,9},{10,11},{9,8... | collective-permute-start | bytes 221192 | tf_op jit(solution)/shard_map/ppermute | solution.py:507
  9.5 0.7 %collective-permute-start.3 = (bf16[2,144,128]{2,1,0:T(8,128)(2,1)}, bf16[2,144,128]{2,1,0:T(8,128)(2,1)S(1)}, u32[]{:S(2)}, u32[]{:S(2)}) collective-permute-start(bf16[2,144,128]{2,1,0:T(8,128)(2,1)} %get-tuple-element.23.refs_0_), channel_id=1, source_target_pairs={{4,8},{8,4},{5,9},{9,5},{6,10},{10,6},{7,11},{11,7},{20,24},{24,20... | collective-permute-start | bytes 221192 | tf_op jit(solution)/shard_map/ppermute | solution.py:507
  10.1 4.5 %collective-permute-start.2 = (bf16[2,144,128]{2,1,0:T(8,128)(2,1)}, bf16[2,144,128]{2,1,0:T(8,128)(2,1)S(1)}, u32[]{:S(2)}, u32[]{:S(2)}) collective-permute-start(bf16[2,144,128]{2,1,0:T(8,128)(2,1)} %get-tuple-element.23.refs_0_), channel_id=1, source_target_pairs={{0,4},{8,12},{4,0},{12,8},{1,5},{9,13},{5,1},{13,9},{2,6},{10,14},... | collective-permute-start | bytes 221192 | tf_op jit(solution)/shard_map/ppermute | solution.py:507
  14.6 2.5 %collective-permute-done.2.refs_2_ = bf16[2,144,128]{2,1,0:T(8,128)(2,1)S(1)} collective-permute-done((bf16[2,144,128]{2,1,0:T(8,128)(2,1)}, bf16[2,144,128]{2,1,0:T(8,128)(2,1)S(1)}, u32[]{:S(2)}, u32[]{:S(2)}) %collective-permute-start.2) | collective-permute-done | bytes 73760 | tf_op jit(solution)/shard_map/ppermute | solution.py:507
  17.2 0.1 collective-permute-start.6
  17.2 0.7 %collective-permute-start.5 = (bf16[4,144,128]{2,1,0:T(8,128)(2,1)S(1)}, bf16[4,144,128]{2,1,0:T(8,128)(2,1)S(1)}, u32[]{:S(2)}, u32[]{:S(2)}) collective-permute-start(bf16[4,144,128]{2,1,0:T(8,128)(2,1)S(1)} %join.2.refs_1_), channel_id=1, source_target_pairs={{4,8},{8,4},{5,9},{9,5},{6,10},{10,6},{7,11},{11,7},{20,24},{24,20... | collective-permute-start | bytes 442376 | tf_op jit(solution)/shard_map/ppermute | solution.py:507
  17.9 3.8 %collective-permute-start.4 = (bf16[4,144,128]{2,1,0:T(8,128)(2,1)S(1)}, bf16[4,144,128]{2,1,0:T(8,128)(2,1)S(1)}, u32[]{:S(2)}, u32[]{:S(2)}) collective-permute-start(bf16[4,144,128]{2,1,0:T(8,128)(2,1)S(1)} %join.2.refs_1_), channel_id=1, source_target_pairs={{0,4},{8,12},{4,0},{12,8},{1,5},{9,13},{5,1},{13,9},{2,6},{10,14},... | collective-permute-start | bytes 442376 | tf_op jit(solution)/shard_map/ppermute | solution.py:507
  21.7 4.2 %collective-permute-done.4.refs_1_ = bf16[4,144,128]{2,1,0:T(8,128)(2,1)S(1)} collective-permute-done((bf16[4,144,128]{2,1,0:T(8,128)(2,1)S(1)}, bf16[4,144,128]{2,1,0:T(8,128)(2,1)S(1)}, u32[]{:S(2)}, u32[]{:S(2)}) %collective-permute-start.4) | collective-permute-done | bytes 147488 | tf_op jit(solution)/shard_map/ppermute | solution.py:507
  25.9 0.1 pad_add_fusion.axis_ref
  26.0 1.3 %collective-permute-done.7.refs_4_ = bf16[4,144,128]{2,1,0:T(8,128)(2,1)S(1)} collective-permute-done((bf16[4,144,128]{2,1,0:T(8,128)(2,1)S(1)}, bf16[4,144,128]{2,1,0:T(8,128)(2,1)S(1)}, u32[]{:S(2)}, u32[]{:S(2)}) %collective-permute-start.7) | collective-permute-done | bytes 147488 | tf_op jit(solution)/shard_map/ppermute | solution.py:547
  27.3 0.6 copy-done.3
  28.0 3.0 %pairs.1 = (f32[10,136,128]{2,1,0:T(8,128)S(1)}, f32[4,136,128]{2,1,0:T(8,128)S(1)}, f32[4,136,128]{2,1,0:T(8,128)S(1)}, f32[10,136,128]{2,1,0:T(8,128)S(1)}, f3...) custom-call(s32[3]{0:T(128)S(1)} %pad_add_fusion.axis_ref, s32[2]{0:T(128)S(1)} %bitcast.17, s32[2,8]{1,0:T(2,128)S(1)} %copy-done.4, ...), custom_call_target="tpu_custom_call" | custom-call | tf_op jit(solution)/shard_map/pairs/pallas_call | solution.py:556
  31.0 4.1 %collective-permute-start.9 = (f32[10,136,128]{2,1,0:T(8,128)S(1)}, f32[10,136,128]{2,1,0:T(8,128)S(1)}, u32[]{:S(2)}, u32[]{:S(2)}) collective-permute-start(f32[10,136,128]{2,1,0:T(8,128)S(1)} %get-tuple-element.25), channel_id=1, source_target_pairs={{0,16},{16,0},{1,17},{17,1},{2,18},{18,2},{3,19},{19,3},{4,20},{20... | collective-permute-start | bytes 2088968 | tf_op jit(solution)/shard_map/ppermute | solution.py:600
  35.1 0.1 collective-permute-start.10
  35.2 0.4 collective-permute-start.12
  35.6 1.7 %collective-permute-done.10.refs_1_ = f32[4,136,128]{2,1,0:T(8,128)S(1)} collective-permute-done((f32[4,136,128]{2,1,0:T(8,128)S(1)}, f32[4,136,128]{2,1,0:T(8,128)S(1)}, u32[]{:S(2)}, u32[]{:S(2)}) %collective-permute-start.10) | collective-permute-done | bytes 278560 | tf_op jit(solution)/shard_map/ppermute | solution.py:600
  37.3 0.1 fold.5
  37.4 8.3 %collective-permute-start.11 = (f16[4,136,128]{2,1,0:T(8,128)(2,1)S(1)}, f16[4,136,128]{2,1,0:T(8,128)(2,1)S(1)}, u32[]{:S(2)}, u32[]{:S(2)}) collective-permute-start(f16[4,136,128]{2,1,0:T(8,128)(2,1)S(1)} %convert_element_type.36), channel_id=1, source_target_pairs={{0,4},{8,12},{4,0},{12,8},{1,5},{9,13},{5,1},{13,9},{2,6},{10,14},... | collective-permute-start | bytes 417800 | tf_op jit(solution)/shard_map/ppermute | solution.py:163
  45.7 0.1 fold.6
  45.8 0.7 %collective-permute-start.13 = (f16[4,136,128]{2,1,0:T(8,128)(2,1)S(1)}, f16[4,136,128]{2,1,0:T(8,128)(2,1)S(1)}, u32[]{:S(2)}, u32[]{:S(2)}) collective-permute-start(f16[4,136,128]{2,1,0:T(8,128)(2,1)S(1)} %convert_element_type.38), channel_id=1, source_target_pairs={{4,8},{8,4},{5,9},{9,5},{6,10},{10,6},{7,11},{11,7},{20,24},{24,20... | collective-permute-start | bytes 417800 | tf_op jit(solution)/shard_map/ppermute | solution.py:163
  46.5 3.2 %collective-permute-done.11 = f16[4,136,128]{2,1,0:T(8,128)(2,1)S(1)} collective-permute-done((f16[4,136,128]{2,1,0:T(8,128)(2,1)S(1)}, f16[4,136,128]{2,1,0:T(8,128)(2,1)S(1)}, u32[]{:S(2)}, u32[]{:S(2)}) %collective-permute-start.11) | collective-permute-done | bytes 139296 | tf_op jit(solution)/shard_map/ppermute | solution.py:163
  49.8 0.1 fold.4
  49.9 0.1 fold.7
  50.0 0.7 %collective-permute-start.17 = (f16[2,136,128]{2,1,0:T(8,128)(2,1)S(1)}, f16[2,136,128]{2,1,0:T(8,128)(2,1)S(1)}, u32[]{:S(2)}, u32[]{:S(2)}) collective-permute-start(f16[2,136,128]{2,1,0:T(8,128)(2,1)S(1)} %convert_element_type.46), channel_id=1, source_target_pairs={{4,8},{8,4},{5,9},{9,5},{6,10},{10,6},{7,11},{11,7},{20,24},{24,20... | collective-permute-start | bytes 208904 | tf_op jit(solution)/shard_map/ppermute | solution.py:163
  50.7 5.5 %collective-permute-start.16 = (f16[2,136,128]{2,1,0:T(8,128)(2,1)S(1)}, f16[2,136,128]{2,1,0:T(8,128)(2,1)S(1)}, u32[]{:S(2)}, u32[]{:S(2)}) collective-permute-start(f16[2,136,128]{2,1,0:T(8,128)(2,1)S(1)} %convert_element_type.44), channel_id=1, source_target_pairs={{0,4},{8,12},{4,0},{12,8},{1,5},{9,13},{5,1},{13,9},{2,6},{10,14},... | collective-permute-start | bytes 208904 | tf_op jit(solution)/shard_map/ppermute | solution.py:163
  56.3 0.7 %collective-permute-start.15 = (f16[2,136,128]{2,1,0:T(8,128)(2,1)S(1)}, f16[2,136,128]{2,1,0:T(8,128)(2,1)S(1)}, u32[]{:S(2)}, u32[]{:S(2)}) collective-permute-start(f16[2,136,128]{2,1,0:T(8,128)(2,1)S(1)} %convert_element_type.42), channel_id=1, source_target_pairs={{1,2},{2,1},{5,6},{6,5},{9,10},{10,9},{13,14},{14,13},{17,18},{18,... | collective-permute-start | bytes 208904 | tf_op jit(solution)/shard_map/ppermute | solution.py:163
  56.9 0.6 collective-permute-start.14
  57.5 1.0 %collective-permute-done.16 = f16[2,136,128]{2,1,0:T(8,128)(2,1)S(1)} collective-permute-done((f16[2,136,128]{2,1,0:T(8,128)(2,1)S(1)}, f16[2,136,128]{2,1,0:T(8,128)(2,1)S(1)}, u32[]{:S(2)}, u32[]{:S(2)}) %collective-permute-start.16) | collective-permute-done | bytes 69664 | tf_op jit(solution)/shard_map/ppermute | solution.py:163
  58.6 2.7 %collective-permute-done.14 = f16[2,136,128]{2,1,0:T(8,128)(2,1)S(1)} collective-permute-done((f16[2,136,128]{2,1,0:T(8,128)(2,1)S(1)}, f16[2,136,128]{2,1,0:T(8,128)(2,1)S(1)}, u32[]{:S(2)}, u32[]{:S(2)}) %collective-permute-start.14) | collective-permute-done | bytes 69664 | tf_op jit(solution)/shard_map/ppermute | solution.py:163
  61.3 1.3 %finish.1 = (f32[3,2,128]{2,1,0:T(2,128)}, f32[2,128,128]{2,1,0:T(8,128)}) custom-call(s32[2]{0:T(128)S(1)} %bitcast.18, f32[2,136,128]{2,1,0:T(8,128)S(1)} %get-tuple-element.26.center_ref, f32[2,136,128]{2,1,0:T(8,128)S(1)} %convert_element_type.41.refs_0_, f32[2,136,128]{2,1,0:T(8,128)S(1)} %convert_element_type.43.refs_1_, ...), custom_call_target="tpu_custom_call" | custom-call | tf_op jit(solution)/shard_map/finish/pallas_call | solution.py:621
  (40 shorter events, 0.3 us)
Async XLA Ops:
  2.9 14.3 %copy-start.1 = (bf16[2,144,128]{2,1,0:T(8,128)(2,1)S(1)}, bf16[2,144,128]{2,1,0:T(8,128)(2,1)}, u32[]{:S(2)}) copy-start(bf16[2,144,128]{2,1,0:T(8,128)(2,1)} %get-tuple-element.23.refs_0_) | copy-start | bytes 221188
  2.9 11.7 %collective-permute-start.1 = (bf16[2,144,128]{2,1,0:T(8,128)(2,1)}, bf16[2,144,128]{2,1,0:T(8,128)(2,1)S(1)}, u32[]{:S(2)}, u32[]{:S(2)}) collective-permute-start(bf16[2,144,128]{2,1,0:T(8,128)(2,1)} %get-tuple-element.23.refs_0_), channel_id=1, source_target_pairs={{1,2},{2,1},{5,6},{6,5},{9,10},{10,9},{13,14},{14,13},{17,18},{18,... | collective-permute-start | bytes 221192 | tf_op jit(solution)/shard_map/ppermute | solution.py:507
  3.7 10.9 %collective-permute-start = (bf16[2,144,128]{2,1,0:T(8,128)(2,1)}, bf16[2,144,128]{2,1,0:T(8,128)(2,1)S(1)}, u32[]{:S(2)}, u32[]{:S(2)}) collective-permute-start(bf16[2,144,128]{2,1,0:T(8,128)(2,1)} %get-tuple-element.23.refs_0_), channel_id=1, source_target_pairs={{0,1},{2,3},{1,0},{3,2},{4,5},{6,7},{5,4},{7,6},{8,9},{10,11},{9,8... | collective-permute-start | bytes 221192 | tf_op jit(solution)/shard_map/ppermute | solution.py:507
  9.5 5.2 %collective-permute-start.3 = (bf16[2,144,128]{2,1,0:T(8,128)(2,1)}, bf16[2,144,128]{2,1,0:T(8,128)(2,1)S(1)}, u32[]{:S(2)}, u32[]{:S(2)}) collective-permute-start(bf16[2,144,128]{2,1,0:T(8,128)(2,1)} %get-tuple-element.23.refs_0_), channel_id=1, source_target_pairs={{4,8},{8,4},{5,9},{9,5},{6,10},{10,6},{7,11},{11,7},{20,24},{24,20... | collective-permute-start | bytes 221192 | tf_op jit(solution)/shard_map/ppermute | solution.py:507
  10.1 7.0 %collective-permute-start.2 = (bf16[2,144,128]{2,1,0:T(8,128)(2,1)}, bf16[2,144,128]{2,1,0:T(8,128)(2,1)S(1)}, u32[]{:S(2)}, u32[]{:S(2)}) collective-permute-start(bf16[2,144,128]{2,1,0:T(8,128)(2,1)} %get-tuple-element.23.refs_0_), channel_id=1, source_target_pairs={{0,4},{8,12},{4,0},{12,8},{1,5},{9,13},{5,1},{13,9},{2,6},{10,14},... | collective-permute-start | bytes 221192 | tf_op jit(solution)/shard_map/ppermute | solution.py:507
  14.6 12.7 %copy-start = (bf16[1024,128]{1,0:T(8,128)(2,1)S(1)}, bf16[1024,128]{1,0:T(8,128)(2,1)}, u32[]{:S(2)}) copy-start(bf16[1024,128]{1,0:T(8,128)(2,1)} %mixing_ref.1) | copy-start | bytes 786436
  17.2 10.1 %collective-permute-start.6 = (bf16[10,144,128]{2,1,0:T(8,128)(2,1)S(1)}, bf16[10,144,128]{2,1,0:T(8,128)(2,1)S(1)}, u32[]{:S(2)}, u32[]{:S(2)}) collective-permute-start(bf16[10,144,128]{2,1,0:T(8,128)(2,1)S(1)} %join.3.refs_0_), channel_id=1, source_target_pairs={{0,16},{16,0},{1,17},{17,1},{2,18},{18,2},{3,19},{19,3},{4,20},{20... | collective-permute-start | bytes 1105928 | tf_op jit(solution)/shard_map/ppermute | solution.py:546
  17.2 4.5 %collective-permute-start.5 = (bf16[4,144,128]{2,1,0:T(8,128)(2,1)S(1)}, bf16[4,144,128]{2,1,0:T(8,128)(2,1)S(1)}, u32[]{:S(2)}, u32[]{:S(2)}) collective-permute-start(bf16[4,144,128]{2,1,0:T(8,128)(2,1)S(1)} %join.2.refs_1_), channel_id=1, source_target_pairs={{4,8},{8,4},{5,9},{9,5},{6,10},{10,6},{7,11},{11,7},{20,24},{24,20... | collective-permute-start | bytes 442376 | tf_op jit(solution)/shard_map/ppermute | solution.py:507
  17.9 8.0 %collective-permute-start.4 = (bf16[4,144,128]{2,1,0:T(8,128)(2,1)S(1)}, bf16[4,144,128]{2,1,0:T(8,128)(2,1)S(1)}, u32[]{:S(2)}, u32[]{:S(2)}) collective-permute-start(bf16[4,144,128]{2,1,0:T(8,128)(2,1)S(1)} %join.2.refs_1_), channel_id=1, source_target_pairs={{0,4},{8,12},{4,0},{12,8},{1,5},{9,13},{5,1},{13,9},{2,6},{10,14},... | collective-permute-start | bytes 442376 | tf_op jit(solution)/shard_map/ppermute | solution.py:507
  21.7 4.3 %collective-permute-start.8 = (bf16[4,144,128]{2,1,0:T(8,128)(2,1)S(1)}, bf16[4,144,128]{2,1,0:T(8,128)(2,1)S(1)}, u32[]{:S(2)}, u32[]{:S(2)}) collective-permute-start(bf16[4,144,128]{2,1,0:T(8,128)(2,1)S(1)} %collective-permute-done.5.refs_2_), channel_id=1, source_target_pairs={{0,16},{16,0},{1,17},{17,1},{2,18},{18,2},{3,19},{19,3},{4,20},{20... | collective-permute-start | bytes 442376 | tf_op jit(solution)/shard_map/ppermute | solution.py:547
  25.9 1.4 %collective-permute-start.7 = (bf16[4,144,128]{2,1,0:T(8,128)(2,1)S(1)}, bf16[4,144,128]{2,1,0:T(8,128)(2,1)S(1)}, u32[]{:S(2)}, u32[]{:S(2)}) collective-permute-start(bf16[4,144,128]{2,1,0:T(8,128)(2,1)S(1)} %collective-permute-done.4.refs_1_), channel_id=1, source_target_pairs={{0,16},{16,0},{1,17},{17,1},{2,18},{18,2},{3,19},{19,3},{4,20},{20... | collective-permute-start | bytes 442376 | tf_op jit(solution)/shard_map/ppermute | solution.py:547
  25.9 1.4 %copy-start.5 = (f32[4]{0:T(128)S(1)}, f32[4]{0:T(128)}, u32[]{:S(2)}) copy-start(f32[4]{0:T(128)} %get-tuple-element.21.rates_ref) | copy-start | bytes 52
  25.9 1.4 %copy-start.6 = (f32[1,128]{1,0:T(1,128)S(1)}, f32[1,128]{1,0:T(1,128)}, u32[]{:S(2)}) copy-start(f32[1,128]{1,0:T(1,128)} %get-tuple-element.22.readout_ref) | copy-start | bytes 1540
  26.0 1.3 %copy-start.2 = (f32[1,1,1,2,3,128]{5,3,4,2,1,0:T(2,128)S(1)}, f32[1,1,1,2,3,128]{5,3,4,2,1,0:T(2,128)}, u32[]{:S(2)}) copy-start(f32[1,1,1,2,3,128]{5,3,4,2,1,0:T(2,128)} %param.7) | copy-start | bytes 9220
  27.3 0.7 %copy-start.3 = (s32[1,1,1,2]{3,2,1,0:T(1,128)S(1)}, s32[1,1,1,2]{3,2,1,0:T(1,128)}, u32[]{:S(2)}) copy-start(s32[1,1,1,2]{3,2,1,0:T(1,128)} %param.9) | copy-start | bytes 28
  27.3 0.7 %copy-start.4 = (s32[2,8]{1,0:T(2,128)S(1)}, s32[2,8]{1,0:T(2,128)}, u32[]{:S(2)}) copy-start(s32[2,8]{1,0:T(2,128)} %get-tuple-element.20.neighbours_ref) | copy-start | bytes 196
  31.0 18.7 %collective-permute-start.9 = (f32[10,136,128]{2,1,0:T(8,128)S(1)}, f32[10,136,128]{2,1,0:T(8,128)S(1)}, u32[]{:S(2)}, u32[]{:S(2)}) collective-permute-start(f32[10,136,128]{2,1,0:T(8,128)S(1)} %get-tuple-element.25), channel_id=1, source_target_pairs={{0,16},{16,0},{1,17},{17,1},{2,18},{18,2},{3,19},{19,3},{4,20},{20... | collective-permute-start | bytes 2088968 | tf_op jit(solution)/shard_map/ppermute | solution.py:600
  35.1 2.2 %collective-permute-start.10 = (f32[4,136,128]{2,1,0:T(8,128)S(1)}, f32[4,136,128]{2,1,0:T(8,128)S(1)}, u32[]{:S(2)}, u32[]{:S(2)}) collective-permute-start(f32[4,136,128]{2,1,0:T(8,128)S(1)} %get-tuple-element.29), channel_id=1, source_target_pairs={{0,16},{16,0},{1,17},{17,1},{2,18},{18,2},{3,19},{19,3},{4,20},{20... | collective-permute-start | bytes 835592 | tf_op jit(solution)/shard_map/ppermute | solution.py:600
  35.2 10.5 %collective-permute-start.12 = (f32[4,136,128]{2,1,0:T(8,128)S(1)}, f32[4,136,128]{2,1,0:T(8,128)S(1)}, u32[]{:S(2)}, u32[]{:S(2)}) collective-permute-start(f32[4,136,128]{2,1,0:T(8,128)S(1)} %get-tuple-element.31), channel_id=1, source_target_pairs={{0,16},{16,0},{1,17},{17,1},{2,18},{18,2},{3,19},{19,3},{4,20},{20... | collective-permute-start | bytes 835592 | tf_op jit(solution)/shard_map/ppermute | solution.py:600
  37.4 12.3 %collective-permute-start.11 = (f16[4,136,128]{2,1,0:T(8,128)(2,1)S(1)}, f16[4,136,128]{2,1,0:T(8,128)(2,1)S(1)}, u32[]{:S(2)}, u32[]{:S(2)}) collective-permute-start(f16[4,136,128]{2,1,0:T(8,128)(2,1)S(1)} %convert_element_type.36), channel_id=1, source_target_pairs={{0,4},{8,12},{4,0},{12,8},{1,5},{9,13},{5,1},{13,9},{2,6},{10,14},... | collective-permute-start | bytes 417800 | tf_op jit(solution)/shard_map/ppermute | solution.py:163
  45.8 3.9 %collective-permute-start.13 = (f16[4,136,128]{2,1,0:T(8,128)(2,1)S(1)}, f16[4,136,128]{2,1,0:T(8,128)(2,1)S(1)}, u32[]{:S(2)}, u32[]{:S(2)}) collective-permute-start(f16[4,136,128]{2,1,0:T(8,128)(2,1)S(1)} %convert_element_type.38), channel_id=1, source_target_pairs={{4,8},{8,4},{5,9},{9,5},{6,10},{10,6},{7,11},{11,7},{20,24},{24,20... | collective-permute-start | bytes 417800 | tf_op jit(solution)/shard_map/ppermute | solution.py:163
  50.0 7.5 %collective-permute-start.17 = (f16[2,136,128]{2,1,0:T(8,128)(2,1)S(1)}, f16[2,136,128]{2,1,0:T(8,128)(2,1)S(1)}, u32[]{:S(2)}, u32[]{:S(2)}) collective-permute-start(f16[2,136,128]{2,1,0:T(8,128)(2,1)S(1)} %convert_element_type.46), channel_id=1, source_target_pairs={{4,8},{8,4},{5,9},{9,5},{6,10},{10,6},{7,11},{11,7},{20,24},{24,20... | collective-permute-start | bytes 208904 | tf_op jit(solution)/shard_map/ppermute | solution.py:163
  50.7 7.8 %collective-permute-start.16 = (f16[2,136,128]{2,1,0:T(8,128)(2,1)S(1)}, f16[2,136,128]{2,1,0:T(8,128)(2,1)S(1)}, u32[]{:S(2)}, u32[]{:S(2)}) collective-permute-start(f16[2,136,128]{2,1,0:T(8,128)(2,1)S(1)} %convert_element_type.44), channel_id=1, source_target_pairs={{0,4},{8,12},{4,0},{12,8},{1,5},{9,13},{5,1},{13,9},{2,6},{10,14},... | collective-permute-start | bytes 208904 | tf_op jit(solution)/shard_map/ppermute | solution.py:163
  56.3 2.3 %collective-permute-start.15 = (f16[2,136,128]{2,1,0:T(8,128)(2,1)S(1)}, f16[2,136,128]{2,1,0:T(8,128)(2,1)S(1)}, u32[]{:S(2)}, u32[]{:S(2)}) collective-permute-start(f16[2,136,128]{2,1,0:T(8,128)(2,1)S(1)} %convert_element_type.42), channel_id=1, source_target_pairs={{1,2},{2,1},{5,6},{6,5},{9,10},{10,9},{13,14},{14,13},{17,18},{18,... | collective-permute-start | bytes 208904 | tf_op jit(solution)/shard_map/ppermute | solution.py:163
  56.9 4.4 %collective-permute-start.14 = (f16[2,136,128]{2,1,0:T(8,128)(2,1)S(1)}, f16[2,136,128]{2,1,0:T(8,128)(2,1)S(1)}, u32[]{:S(2)}, u32[]{:S(2)}) collective-permute-start(f16[2,136,128]{2,1,0:T(8,128)(2,1)S(1)} %convert_element_type.40), channel_id=1, source_target_pairs={{0,1},{2,3},{1,0},{3,2},{4,5},{6,7},{5,4},{7,6},{8,9},{10,11},{9,8... | collective-permute-start | bytes 208904 | tf_op jit(solution)/shard_map/ppermute | solution.py:163
where the time goes:
time: 63 us; the launch traced here: 62.7 us
  starting transfers between devices  37.2 us (59%)
  waiting for transfers between devices  16.6 us (26%)
  Pallas kernels  6.98 us (11%)
  between operations  0.91 us (1%)
  local copies, waits for them, and re-layouts  0.68 us (1%)
    ppermute x6, starting transfers between devices, send(): lax.ppermute(value.astype(jnp.float16), axis, pairs).astype(jnp.float32)  16.4 us
    ppermute x6, starting transfers between devices, swap(): return [lax.ppermute(value, axis, pairs) for pairs in swaps(axis)]  16.1 us
    ppermute x6, waiting for transfers between devices, send(): lax.ppermute(value.astype(jnp.float16), axis, pairs).astype(jnp.float32)  6.94 us
    ppermute x6, waiting for transfers between devices, swap(): return [lax.ppermute(value, axis, pairs) for pairs in swaps(axis)]  6.72 us
    ppermute x3, starting transfers between devices, gather(): arrays.append(lax.ppermute(plane[k], 'gx', pairs))  4.65 us
    pallas_call x1, Pallas kernels, step(): pl.pallas_call(functools.partial(main_kernel, len(flat), sides, slots), o...  3.02 us
    pallas_call x1, Pallas kernels, step(): pl.pallas_call(pack_kernel, out_shape=[jax.ShapeDtypeStruct((tiles, atoms...  2.24 us
    ppermute x3, waiting for transfers between devices, gather(): arrays.append(lax.ppermute(plane[k], 'gx', pairs))  1.68 us
  transfers between devices with their start and end apart: 18, of which 7 were waited for; matrix products, arithmetic and copies ran while one was open for 0% of the time, Pallas kernels for 0%

commit v1 on v0

--- a/solution.py
+++ b/solution.py
@@ -34,49 +34,43 @@
     return jnp.minimum(jnp.where(step == 0, 0, side), sides)
 
 
-def pack_kernel(
-    counts_ref,
-    neighbours_ref,
-    rates_ref,
-    readout_ref,
-    features_ref,
-    points_ref,
-    packed_ref,
-    out_neighbours_ref,
-    out_rates_ref,
-    out_readout_ref,
-    buffer_ref,
-    place_ref,
-    extra_ref,
-    sems,
-):
-    loads = [
-        pltpu.make_async_copy(features_ref, buffer_ref, sems.at[0]),
-        pltpu.make_async_copy(points_ref, place_ref, sems.at[1]),
-    ]
-    for load in loads:
-        load.start()
+def pack_kernel(counts_ref, features_ref, points_ref, packed_ref, extra_ref):
     tiles, atoms, _ = features_ref.shape
-    for t in range(tiles):
-        for k in range(neighbours_ref.shape[1]):
-            out_neighbours_ref[t, k] = neighbours_ref[t, k]
-    for r in range(rates_ref.shape[0]):
-        out_rates_ref[r] = rates_ref[r]
-    out_readout_ref[...] = readout_ref[...]
     extra_ref[...] = jnp.zeros_like(extra_ref)
-    for load in loads:
-        load.wait()
     for t in range(tiles):
         count = counts_ref[t]
         rows = lax.broadcasted_iota(jnp.int32, features_ref.shape[1:], 0)
-        values = buffer_ref[t].astype(jnp.float32)
+        values = features_ref[t].astype(jnp.float32)
         packed_ref[t, :atoms] = jnp.where(rows < count, values, 0.0).astype(jnp.bfloat16)
-        rest = place_ref[:, t, :]
+        rest = points_ref[:, t, :]
         for term in range(3):
             part = rest.astype(jnp.bfloat16).astype(jnp.float32)
             extra_ref[t, 3 * term : 3 * term + 3] = part
             rest = rest - part
         packed_ref[t, atoms:] = extra_ref[t].astype(jnp.bfloat16)
+
+
+def side_kernel(
+    counts_ref,
+    neighbours_ref,
+    rates_ref,
+    points_ref,
+    readout_ref,
+    out_counts_ref,
+    out_neighbours_ref,
+    out_rates_ref,
+    out_points_ref,
+    out_readout_ref,
+):
+    tiles, slots = neighbours_ref.shape
+    for t in range(tiles):
+        out_counts_ref[t] = counts_ref[t]
+        for k in range(slots):
+            out_neighbours_ref[t, k] = neighbours_ref[t, k]
+    for r in range(rates_ref.shape[0]):
+        out_rates_ref[r] = rates_ref[r]
+    out_points_ref[...] = points_ref[...]
+    out_readout_ref[...] = readout_ref[...]
 
 
 def join_kernel(groups, *refs):
@@ -500,7 +494,6 @@
     vmem = pl.BlockSpec(memory_space=pltpu.VMEM)
     smem = pl.BlockSpec(memory_space=pltpu.SMEM)
     hbm = pl.BlockSpec(memory_space=pl.ANY)
-    far = pl.BlockSpec(memory_space=pltpu.HBM)
     small = pltpu.CompilerParams(vmem_limit_bytes=SMALL)
 
     def swap(value, axis):
@@ -509,37 +502,39 @@
     sides = tuple(len(swaps(axis)) for axis in ("gx", "gy", "gz"))
     own_counts = counts.reshape(tiles)
     points = jnp.transpose(positions, (0, 1, 2, 4, 3, 5)).reshape(3, tiles, atoms)
-    packed, neighbours, rates, readout = pl.pallas_call(
+    packed = pl.pallas_call(
         pack_kernel,
+        out_shape=jax.ShapeDtypeStruct((tiles, atoms + 16, channels), jnp.bfloat16),
+        in_specs=[smem, vmem, vmem],
+        out_specs=vmem,
+        scratch_shapes=[pltpu.VMEM((tiles, 16, channels), jnp.float32)],
+        compiler_params=pltpu.CompilerParams(vmem_limit_bytes=60 << 20),
+        name="pack",
+    )(own_counts, features.reshape(tiles, atoms, channels), points)
+    along_z = swap(packed, "gz")
+    own_counts, neighbours, rates, points, readout = pl.pallas_call(
+        side_kernel,
         out_shape=[
-            jax.ShapeDtypeStruct((tiles, atoms + 16, channels), jnp.bfloat16),
+            jax.ShapeDtypeStruct((tiles,), jnp.int32),
             jax.ShapeDtypeStruct((tiles, slots), jnp.int32),
             jax.ShapeDtypeStruct((radials,), jnp.float32),
+            jax.ShapeDtypeStruct((3, tiles, atoms), jnp.float32),
             jax.ShapeDtypeStruct((1, channels), jnp.float32),
         ],
-        in_specs=[smem, smem, smem, vmem, far, far],
-        out_specs=[vmem, smem, smem, vmem],
-        scratch_shapes=[
-            pltpu.VMEM((tiles, atoms, channels), jnp.bfloat16),
-            pltpu.VMEM((3, tiles, atoms), jnp.float32),
-            pltpu.VMEM((tiles, 16, channels), jnp.float32),
-            pltpu.SemaphoreType.DMA((2,)),
-        ],
-        compiler_params=pltpu.CompilerParams(vmem_limit_bytes=60 << 20),
-        name="pack",
+        in_specs=[smem, smem, smem, vmem, vmem],
+        out_specs=[smem, smem, smem, vmem, vmem],
+        compiler_params=small,
+        name="sides",
     )(
         own_counts,
         neighbours.reshape(tiles, slots),
         radial_rates,
+        points,
         readout.reshape(1, channels),
-        features.reshape(tiles, atoms, channels),
-        points,
     )
-
-    along_z = swap(packed, "gz")
     (line,) = join([list(range(len(along_z)))], *along_z)
+    diagonal = swap(line, "gy")
     along_y = swap(packed, "gy")
-    diagonal = swap(line, "gy")
     (cross,) = join([list(range(2 + len(along_y)))], packed, line, *along_y)
     pieces = [[cross] + diagonal]
     for pairs in swaps("gx"):
@@ -611,12 +606,13 @@
     for k in range(sides[1]):
         cuts.append((line + k * tiles, line + (k + 1) * tiles, True))
     center, along_z, *along_y = fold(cuts, arrays, [])
+    parts = [center]
+    for value, pairs in zip(along_y, swaps("gy")):
+        parts.append(send(value, "gy", pairs))
     cuts = [(k * tiles, (k + 1) * tiles, True) for k in range(sides[2])]
     along_z = fold(cuts, [along_z], diagonal)
-    parts = [center]
-    for values, axis in ((along_z, "gz"), (along_y, "gy")):
-        for value, pairs in zip(values, swaps(axis)):
-            parts.append(send(value, axis, pairs))
+    for value, pairs in zip(along_z, swaps("gz")):
+        parts.append(send(value, "gz", pairs))
 
     forces, grads = pl.pallas_call(
         final_kernel,

time: 63 us -> 62.5 us (level)
  waiting for transfers between devices: 16.6 us -> 15.3 us
    ppermute x2, waiting for transfers between devices: 1.29 us -> 0.01 us  [step(): lax.ppermute(piece, 'gx', pairs)]
    pallas_call x1 -> x2, Pallas kernels: 2.24 us -> 2.72 us  [the longest x1 1.53 us: step(): pl.pallas_call(pack_kernel, out_shape=jax.ShapeDtypeStruct((tiles, atoms...]
  transfers between devices with their start and end apart: 18 -> 18, of which waited for: 7 -> 6; matrix products, arithmetic and copies ran while one was open for 0% -> 0% of each run, Pallas kernels for 0% -> 2%
where the time goes in v1:
time: 62.5 us; the launch traced here: 62.2 us
  starting transfers between devices  37.6 us (60%)
  waiting for transfers between devices  15.3 us (24%)
  Pallas kernels  7.49 us (12%)
  between operations  0.91 us (1%)
  local copies, waits for them, and re-layouts  0.73 us (1%)
    ppermute x6, starting transfers between devices, send(): lax.ppermute(value.astype(jnp.float16), axis, pairs).astype(jnp.float32)  16.4 us
    ppermute x6, starting transfers between devices, swap(): return [lax.ppermute(value, axis, pairs) for pairs in swaps(axis)]  16.1 us
    ppermute x6, waiting for transfers between devices, send(): lax.ppermute(value.astype(jnp.float16), axis, pairs).astype(jnp.float32)  6.86 us
    ppermute x6, waiting for transfers between devices, swap(): return [lax.ppermute(value, axis, pairs) for pairs in swaps(axis)]  6.72 us
    ppermute x3, starting transfers between devices, gather(): arrays.append(lax.ppermute(plane[k], 'gx', pairs))  5 us
    pallas_call x1, Pallas kernels, step(): pl.pallas_call(functools.partial(main_kernel, len(flat), sides, slots), o...  3.03 us
    ppermute x3, waiting for transfers between devices, gather(): arrays.append(lax.ppermute(plane[k], 'gx', pairs))  1.68 us
    pallas_call x1, Pallas kernels, step(): pl.pallas_call(pack_kernel, out_shape=jax.ShapeDtypeStruct((tiles, atoms...  1.53 us
  transfers between devices with their start and end apart: 18, of which 6 were waited for; matrix products, arithmetic and copies ran while one was open for 0% of the time, Pallas kernels for 2%

profile of v1, /device:TPU:0, one launch (start us, length us, event | category | flops | bytes accessed | tf_op | source)
XLA Modules:
  0.0 62.2 jit_solution(2099050783063837196)
XLA Ops:
  0.6 1.5 %pack.1.refs_0_ = bf16[2,144,128]{2,1,0:T(8,128)(2,1)} custom-call(s32[2]{0:T(128)} %bitcast.16, bf16[2,128,128]{2,1,0:T(8,128)(2,1)} %bitcast.20, f32[3,2,128]{2,1,0:T(2,128)} %bitcast.14), custom_call_target="tpu_custom_call" | custom-call | tf_op jit(solution)/shard_map/pack/pallas_call | solution.py:505
  2.2 0.8 %collective-permute-start.1 = (bf16[2,144,128]{2,1,0:T(8,128)(2,1)}, bf16[2,144,128]{2,1,0:T(8,128)(2,1)S(1)}, u32[]{:S(2)}, u32[]{:S(2)}) collective-permute-start(bf16[2,144,128]{2,1,0:T(8,128)(2,1)} %pack.1.refs_0_), channel_id=1, source_target_pairs={{1,2},{2,1},{5,6},{6,5},{9,10},{10,9},{13,14},{14,13},{17,18},{18,... | collective-permute-start | bytes 221192 | tf_op jit(solution)/shard_map/ppermute | solution.py:500
  3.0 5.8 %collective-permute-start = (bf16[2,144,128]{2,1,0:T(8,128)(2,1)}, bf16[2,144,128]{2,1,0:T(8,128)(2,1)S(1)}, u32[]{:S(2)}, u32[]{:S(2)}) collective-permute-start(bf16[2,144,128]{2,1,0:T(8,128)(2,1)} %pack.1.refs_0_), channel_id=1, source_target_pairs={{0,1},{2,3},{1,0},{3,2},{4,5},{6,7},{5,4},{7,6},{8,9},{10,11},{9,8... | collective-permute-start | bytes 221192 | tf_op jit(solution)/shard_map/ppermute | solution.py:500
  8.7 0.7 %collective-permute-start.3 = (bf16[2,144,128]{2,1,0:T(8,128)(2,1)}, bf16[2,144,128]{2,1,0:T(8,128)(2,1)S(1)}, u32[]{:S(2)}, u32[]{:S(2)}) collective-permute-start(bf16[2,144,128]{2,1,0:T(8,128)(2,1)} %pack.1.refs_0_), channel_id=1, source_target_pairs={{4,8},{8,4},{5,9},{9,5},{6,10},{10,6},{7,11},{11,7},{20,24},{24,20... | collective-permute-start | bytes 221192 | tf_op jit(solution)/shard_map/ppermute | solution.py:500
  9.4 4.5 %collective-permute-start.2 = (bf16[2,144,128]{2,1,0:T(8,128)(2,1)}, bf16[2,144,128]{2,1,0:T(8,128)(2,1)S(1)}, u32[]{:S(2)}, u32[]{:S(2)}) collective-permute-start(bf16[2,144,128]{2,1,0:T(8,128)(2,1)} %pack.1.refs_0_), channel_id=1, source_target_pairs={{0,4},{8,12},{4,0},{12,8},{1,5},{9,13},{5,1},{13,9},{2,6},{10,14},... | collective-permute-start | bytes 221192 | tf_op jit(solution)/shard_map/ppermute | solution.py:500
  13.9 2.5 %collective-permute-done.2.refs_2_ = bf16[2,144,128]{2,1,0:T(8,128)(2,1)S(1)} collective-permute-done((bf16[2,144,128]{2,1,0:T(8,128)(2,1)}, bf16[2,144,128]{2,1,0:T(8,128)(2,1)S(1)}, u32[]{:S(2)}, u32[]{:S(2)}) %collective-permute-start.2) | collective-permute-done | bytes 73760 | tf_op jit(solution)/shard_map/ppermute | solution.py:500
  16.4 0.1 collective-permute-start.6
  16.5 0.7 %collective-permute-start.5 = (bf16[4,144,128]{2,1,0:T(8,128)(2,1)S(1)}, bf16[4,144,128]{2,1,0:T(8,128)(2,1)S(1)}, u32[]{:S(2)}, u32[]{:S(2)}) collective-permute-start(bf16[4,144,128]{2,1,0:T(8,128)(2,1)S(1)} %join.2.refs_1_), channel_id=1, source_target_pairs={{4,8},{8,4},{5,9},{9,5},{6,10},{10,6},{7,11},{11,7},{20,24},{24,20... | collective-permute-start | bytes 442376 | tf_op jit(solution)/shard_map/ppermute | solution.py:500
  17.2 3.8 %collective-permute-start.4 = (bf16[4,144,128]{2,1,0:T(8,128)(2,1)S(1)}, bf16[4,144,128]{2,1,0:T(8,128)(2,1)S(1)}, u32[]{:S(2)}, u32[]{:S(2)}) collective-permute-start(bf16[4,144,128]{2,1,0:T(8,128)(2,1)S(1)} %join.2.refs_1_), channel_id=1, source_target_pairs={{0,4},{8,12},{4,0},{12,8},{1,5},{9,13},{5,1},{13,9},{2,6},{10,14},... | collective-permute-start | bytes 442376 | tf_op jit(solution)/shard_map/ppermute | solution.py:500
  21.0 4.2 %collective-permute-done.4.refs_1_ = bf16[4,144,128]{2,1,0:T(8,128)(2,1)S(1)} collective-permute-done((bf16[4,144,128]{2,1,0:T(8,128)(2,1)S(1)}, bf16[4,144,128]{2,1,0:T(8,128)(2,1)S(1)}, u32[]{:S(2)}, u32[]{:S(2)}) %collective-permute-start.4) | collective-permute-done | bytes 147488 | tf_op jit(solution)/shard_map/ppermute | solution.py:500
  25.2 0.6 copy-done.5
  25.9 1.2 %sides.1 = (s32[2]{0:T(128)S(1)}, s32[2,8]{1,0:T(2,128)S(1)}, f32[4]{0:T(128)S(1)}, f32[3,2,128]{2,1,0:T(2,128)S(1)}, f32[1,128]{1,0:T(1,128)S(1)}) custom-call(s32[2]{0:T(128)S(1)} %bitcast.17, s32[2,8]{1,0:T(2,128)S(1)} %bitcast.18, f32[4]{0:T(128)S(1)} %copy-done.5, f32[3,2,128]{2,1,0:T(2,128)S(1)} %bitcast.15, f32[1,128]{1,0:T(1,128)S(1)} %bitcast.19), custom_call_target="tpu_custom_call" | custom-call | tf_op jit(solution)/shard_map/sides/pallas_call | solution.py:515
  27.1 0.1 pad_add_fusion.axis_ref
  27.2 3.0 %pairs.1 = (f32[10,136,128]{2,1,0:T(8,128)S(1)}, f32[4,136,128]{2,1,0:T(8,128)S(1)}, f32[4,136,128]{2,1,0:T(8,128)S(1)}, f32[10,136,128]{2,1,0:T(8,128)S(1)}, f3...) custom-call(s32[3]{0:T(128)S(1)} %pad_add_fusion.axis_ref, s32[2]{0:T(128)S(1)} %get-tuple-element.21.counts_ref, ...), custom_call_target="tpu_custom_call" | custom-call | tf_op jit(solution)/shard_map/pairs/pallas_call | solution.py:551
  30.2 4.5 %collective-permute-start.9 = (f32[10,136,128]{2,1,0:T(8,128)S(1)}, f32[10,136,128]{2,1,0:T(8,128)S(1)}, u32[]{:S(2)}, u32[]{:S(2)}) collective-permute-start(f32[10,136,128]{2,1,0:T(8,128)S(1)} %get-tuple-element.27), channel_id=1, source_target_pairs={{0,16},{16,0},{1,17},{17,1},{2,18},{18,2},{3,19},{19,3},{4,20},{20... | collective-permute-start | bytes 2088968 | tf_op jit(solution)/shard_map/ppermute | solution.py:595
  34.7 0.1 collective-permute-start.12
  34.8 0.4 collective-permute-start.14
  35.2 1.7 %collective-permute-done.12.refs_1_ = f32[4,136,128]{2,1,0:T(8,128)S(1)} collective-permute-done((f32[4,136,128]{2,1,0:T(8,128)S(1)}, f32[4,136,128]{2,1,0:T(8,128)S(1)}, u32[]{:S(2)}, u32[]{:S(2)}) %collective-permute-start.12) | collective-permute-done | bytes 278560 | tf_op jit(solution)/shard_map/ppermute | solution.py:595
  36.9 0.1 fold.5
  37.0 8.2 %collective-permute-start.13 = (f16[4,136,128]{2,1,0:T(8,128)(2,1)S(1)}, f16[4,136,128]{2,1,0:T(8,128)(2,1)S(1)}, u32[]{:S(2)}, u32[]{:S(2)}) collective-permute-start(f16[4,136,128]{2,1,0:T(8,128)(2,1)S(1)} %convert_element_type.40), channel_id=1, source_target_pairs={{0,4},{8,12},{4,0},{12,8},{1,5},{9,13},{5,1},{13,9},{2,6},{10,14},... | collective-permute-start | bytes 417800 | tf_op jit(solution)/shard_map/ppermute | solution.py:157
  45.2 0.1 fold.6
  45.3 0.7 %collective-permute-start.15 = (f16[4,136,128]{2,1,0:T(8,128)(2,1)S(1)}, f16[4,136,128]{2,1,0:T(8,128)(2,1)S(1)}, u32[]{:S(2)}, u32[]{:S(2)}) collective-permute-start(f16[4,136,128]{2,1,0:T(8,128)(2,1)S(1)} %convert_element_type.42), channel_id=1, source_target_pairs={{4,8},{8,4},{5,9},{9,5},{6,10},{10,6},{7,11},{11,7},{20,24},{24,20... | collective-permute-start | bytes 417800 | tf_op jit(solution)/shard_map/ppermute | solution.py:157
  46.0 3.2 %collective-permute-done.13 = f16[4,136,128]{2,1,0:T(8,128)(2,1)S(1)} collective-permute-done((f16[4,136,128]{2,1,0:T(8,128)(2,1)S(1)}, f16[4,136,128]{2,1,0:T(8,128)(2,1)S(1)}, u32[]{:S(2)}, u32[]{:S(2)}) %collective-permute-start.13) | collective-permute-done | bytes 139296 | tf_op jit(solution)/shard_map/ppermute | solution.py:157
  49.3 0.1 fold.4
  49.4 0.1 fold.7
  49.6 0.7 %collective-permute-start.17 = (f16[2,136,128]{2,1,0:T(8,128)(2,1)S(1)}, f16[2,136,128]{2,1,0:T(8,128)(2,1)S(1)}, u32[]{:S(2)}, u32[]{:S(2)}) collective-permute-start(f16[2,136,128]{2,1,0:T(8,128)(2,1)S(1)} %convert_element_type.46), channel_id=1, source_target_pairs={{1,2},{2,1},{5,6},{6,5},{9,10},{10,9},{13,14},{14,13},{17,18},{18,... | collective-permute-start | bytes 208904 | tf_op jit(solution)/shard_map/ppermute | solution.py:157
  50.3 0.7 %collective-permute-start.11 = (f16[2,136,128]{2,1,0:T(8,128)(2,1)S(1)}, f16[2,136,128]{2,1,0:T(8,128)(2,1)S(1)}, u32[]{:S(2)}, u32[]{:S(2)}) collective-permute-start(f16[2,136,128]{2,1,0:T(8,128)(2,1)S(1)} %convert_element_type.38), channel_id=1, source_target_pairs={{4,8},{8,4},{5,9},{9,5},{6,10},{10,6},{7,11},{11,7},{20,24},{24,20... | collective-permute-start | bytes 208904 | tf_op jit(solution)/shard_map/ppermute | solution.py:157
  50.9 5.5 %collective-permute-start.10 = (f16[2,136,128]{2,1,0:T(8,128)(2,1)S(1)}, f16[2,136,128]{2,1,0:T(8,128)(2,1)S(1)}, u32[]{:S(2)}, u32[]{:S(2)}) collective-permute-start(f16[2,136,128]{2,1,0:T(8,128)(2,1)S(1)} %convert_element_type.36), channel_id=1, source_target_pairs={{0,4},{8,12},{4,0},{12,8},{1,5},{9,13},{5,1},{13,9},{2,6},{10,14},... | collective-permute-start | bytes 208904 | tf_op jit(solution)/shard_map/ppermute | solution.py:157
  56.5 0.6 %collective-permute-start.16 = (f16[2,136,128]{2,1,0:T(8,128)(2,1)S(1)}, f16[2,136,128]{2,1,0:T(8,128)(2,1)S(1)}, u32[]{:S(2)}, u32[]{:S(2)}) collective-permute-start(f16[2,136,128]{2,1,0:T(8,128)(2,1)S(1)} %convert_element_type.44), channel_id=1, source_target_pairs={{0,1},{2,3},{1,0},{3,2},{4,5},{6,7},{5,4},{7,6},{8,9},{10,11},{9,8... | collective-permute-start | bytes 208904 | tf_op jit(solution)/shard_map/ppermute | solution.py:157
  57.2 1.6 %collective-permute-done.10 = f16[2,136,128]{2,1,0:T(8,128)(2,1)S(1)} collective-permute-done((f16[2,136,128]{2,1,0:T(8,128)(2,1)S(1)}, f16[2,136,128]{2,1,0:T(8,128)(2,1)S(1)}, u32[]{:S(2)}, u32[]{:S(2)}) %collective-permute-start.10) | collective-permute-done | bytes 69664 | tf_op jit(solution)/shard_map/ppermute | solution.py:157
  58.8 2.1 %collective-permute-done.16 = f16[2,136,128]{2,1,0:T(8,128)(2,1)S(1)} collective-permute-done((f16[2,136,128]{2,1,0:T(8,128)(2,1)S(1)}, f16[2,136,128]{2,1,0:T(8,128)(2,1)S(1)}, u32[]{:S(2)}, u32[]{:S(2)}) %collective-permute-start.16) | collective-permute-done | bytes 69664 | tf_op jit(solution)/shard_map/ppermute | solution.py:157
  60.9 1.3 %finish.1 = (f32[3,2,128]{2,1,0:T(2,128)}, f32[2,128,128]{2,1,0:T(8,128)}) custom-call(s32[2]{0:T(128)S(1)} %get-tuple-element.21.counts_ref, f32[2,136,128]{2,1,0:T(8,128)S(1)} %get-tuple-element.28.center_ref, f32[2,136,128]{2,1,0:T(8,128)S(1)} %convert_element_type.37.refs_0_, f32[2,136,128]{2,1,0:T(8,128)S(1)} %convert_element_type.39.refs_1_, ...), custom_call_target="tpu_custom_call" | custom-call | tf_op jit(solution)/shard_map/finish/pallas_call | solution.py:617
  (41 shorter events, 0.4 us)
Async XLA Ops:
  2.2 14.2 %copy-start = (bf16[2,144,128]{2,1,0:T(8,128)(2,1)S(1)}, bf16[2,144,128]{2,1,0:T(8,128)(2,1)}, u32[]{:S(2)}) copy-start(bf16[2,144,128]{2,1,0:T(8,128)(2,1)} %pack.1.refs_0_) | copy-start | bytes 221188
  2.2 11.7 %collective-permute-start.1 = (bf16[2,144,128]{2,1,0:T(8,128)(2,1)}, bf16[2,144,128]{2,1,0:T(8,128)(2,1)S(1)}, u32[]{:S(2)}, u32[]{:S(2)}) collective-permute-start(bf16[2,144,128]{2,1,0:T(8,128)(2,1)} %pack.1.refs_0_), channel_id=1, source_target_pairs={{1,2},{2,1},{5,6},{6,5},{9,10},{10,9},{13,14},{14,13},{17,18},{18,... | collective-permute-start | bytes 221192 | tf_op jit(solution)/shard_map/ppermute | solution.py:500
  3.0 10.9 %collective-permute-start = (bf16[2,144,128]{2,1,0:T(8,128)(2,1)}, bf16[2,144,128]{2,1,0:T(8,128)(2,1)S(1)}, u32[]{:S(2)}, u32[]{:S(2)}) collective-permute-start(bf16[2,144,128]{2,1,0:T(8,128)(2,1)} %pack.1.refs_0_), channel_id=1, source_target_pairs={{0,1},{2,3},{1,0},{3,2},{4,5},{6,7},{5,4},{7,6},{8,9},{10,11},{9,8... | collective-permute-start | bytes 221192 | tf_op jit(solution)/shard_map/ppermute | solution.py:500
  8.7 5.2 %collective-permute-start.3 = (bf16[2,144,128]{2,1,0:T(8,128)(2,1)}, bf16[2,144,128]{2,1,0:T(8,128)(2,1)S(1)}, u32[]{:S(2)}, u32[]{:S(2)}) collective-permute-start(bf16[2,144,128]{2,1,0:T(8,128)(2,1)} %pack.1.refs_0_), channel_id=1, source_target_pairs={{4,8},{8,4},{5,9},{9,5},{6,10},{10,6},{7,11},{11,7},{20,24},{24,20... | collective-permute-start | bytes 221192 | tf_op jit(solution)/shard_map/ppermute | solution.py:500
  9.4 7.0 %collective-permute-start.2 = (bf16[2,144,128]{2,1,0:T(8,128)(2,1)}, bf16[2,144,128]{2,1,0:T(8,128)(2,1)S(1)}, u32[]{:S(2)}, u32[]{:S(2)}) collective-permute-start(bf16[2,144,128]{2,1,0:T(8,128)(2,1)} %pack.1.refs_0_), channel_id=1, source_target_pairs={{0,4},{8,12},{4,0},{12,8},{1,5},{9,13},{5,1},{13,9},{2,6},{10,14},... | collective-permute-start | bytes 221192 | tf_op jit(solution)/shard_map/ppermute | solution.py:500
  13.9 13.3 %copy-start.1 = (bf16[1024,128]{1,0:T(8,128)(2,1)S(1)}, bf16[1024,128]{1,0:T(8,128)(2,1)}, u32[]{:S(2)}) copy-start(bf16[1024,128]{1,0:T(8,128)(2,1)} %mixing_ref.1) | copy-start | bytes 786436
  16.4 10.8 %collective-permute-start.6 = (bf16[10,144,128]{2,1,0:T(8,128)(2,1)S(1)}, bf16[10,144,128]{2,1,0:T(8,128)(2,1)S(1)}, u32[]{:S(2)}, u32[]{:S(2)}) collective-permute-start(bf16[10,144,128]{2,1,0:T(8,128)(2,1)S(1)} %join.3.refs_0_), channel_id=1, source_target_pairs={{0,16},{16,0},{1,17},{17,1},{2,18},{18,2},{3,19},{19,3},{4,20},{20... | collective-permute-start | bytes 1105928 | tf_op jit(solution)/shard_map/ppermute | solution.py:541
  16.5 4.5 %collective-permute-start.5 = (bf16[4,144,128]{2,1,0:T(8,128)(2,1)S(1)}, bf16[4,144,128]{2,1,0:T(8,128)(2,1)S(1)}, u32[]{:S(2)}, u32[]{:S(2)}) collective-permute-start(bf16[4,144,128]{2,1,0:T(8,128)(2,1)S(1)} %join.2.refs_1_), channel_id=1, source_target_pairs={{4,8},{8,4},{5,9},{9,5},{6,10},{10,6},{7,11},{11,7},{20,24},{24,20... | collective-permute-start | bytes 442376 | tf_op jit(solution)/shard_map/ppermute | solution.py:500
  17.2 8.0 %collective-permute-start.4 = (bf16[4,144,128]{2,1,0:T(8,128)(2,1)S(1)}, bf16[4,144,128]{2,1,0:T(8,128)(2,1)S(1)}, u32[]{:S(2)}, u32[]{:S(2)}) collective-permute-start(bf16[4,144,128]{2,1,0:T(8,128)(2,1)S(1)} %join.2.refs_1_), channel_id=1, source_target_pairs={{0,4},{8,12},{4,0},{12,8},{1,5},{9,13},{5,1},{13,9},{2,6},{10,14},... | collective-permute-start | bytes 442376 | tf_op jit(solution)/shard_map/ppermute | solution.py:500
  20.9 6.2 %collective-permute-start.8 = (bf16[4,144,128]{2,1,0:T(8,128)(2,1)S(1)}, bf16[4,144,128]{2,1,0:T(8,128)(2,1)S(1)}, u32[]{:S(2)}, u32[]{:S(2)}) collective-permute-start(bf16[4,144,128]{2,1,0:T(8,128)(2,1)S(1)} %collective-permute-done.5.refs_2_), channel_id=1, source_target_pairs={{0,16},{16,0},{1,17},{17,1},{2,18},{18,2},{3,19},{19,3},{4,20},{20... | collective-permute-start | bytes 442376 | tf_op jit(solution)/shard_map/ppermute | solution.py:542
  25.2 2.0 %collective-permute-start.7 = (bf16[4,144,128]{2,1,0:T(8,128)(2,1)S(1)}, bf16[4,144,128]{2,1,0:T(8,128)(2,1)S(1)}, u32[]{:S(2)}, u32[]{:S(2)}) collective-permute-start(bf16[4,144,128]{2,1,0:T(8,128)(2,1)S(1)} %collective-permute-done.4.refs_1_), channel_id=1, source_target_pairs={{0,16},{16,0},{1,17},{17,1},{2,18},{18,2},{3,19},{19,3},{4,20},{20... | collective-permute-start | bytes 442376 | tf_op jit(solution)/shard_map/ppermute | solution.py:542
  25.2 0.7 %copy-start.5 = (f32[4]{0:T(128)S(1)}, f32[4]{0:T(128)}, u32[]{:S(2)}) copy-start(f32[4]{0:T(128)} %rates_ref.1) | copy-start | bytes 52
  25.2 0.7 %copy-start.6 = (f32[128]{0:T(128)S(1)}, f32[128]{0:T(128)}, u32[]{:S(2)}) copy-start(f32[128]{0:T(128)} %param.12) | copy-start | bytes 1540
  25.2 0.7 %copy-start.2 = (f32[1,1,1,2,3,128]{5,3,4,2,1,0:T(2,128)S(1)}, f32[1,1,1,2,3,128]{5,3,4,2,1,0:T(2,128)}, u32[]{:S(2)}) copy-start(f32[1,1,1,2,3,128]{5,3,4,2,1,0:T(2,128)} %param.7) | copy-start | bytes 9220
  25.2 0.7 %copy-start.3 = (s32[1,1,1,2]{3,2,1,0:T(1,128)S(1)}, s32[1,1,1,2]{3,2,1,0:T(1,128)}, u32[]{:S(2)}) copy-start(s32[1,1,1,2]{3,2,1,0:T(1,128)} %param.9) | copy-start | bytes 28
  25.2 0.7 %copy-start.4 = (s32[1,1,1,2,8]{4,3,2,1,0:T(2,128)S(1)}, s32[1,1,1,2,8]{4,3,2,1,0:T(2,128)}, u32[]{:S(2)}) copy-start(s32[1,1,1,2,8]{4,3,2,1,0:T(2,128)} %param.10) | copy-start | bytes 196
  30.2 19.0 %collective-permute-start.9 = (f32[10,136,128]{2,1,0:T(8,128)S(1)}, f32[10,136,128]{2,1,0:T(8,128)S(1)}, u32[]{:S(2)}, u32[]{:S(2)}) collective-permute-start(f32[10,136,128]{2,1,0:T(8,128)S(1)} %get-tuple-element.27), channel_id=1, source_target_pairs={{0,16},{16,0},{1,17},{17,1},{2,18},{18,2},{3,19},{19,3},{4,20},{20... | collective-permute-start | bytes 2088968 | tf_op jit(solution)/shard_map/ppermute | solution.py:595
  34.7 2.2 %collective-permute-start.12 = (f32[4,136,128]{2,1,0:T(8,128)S(1)}, f32[4,136,128]{2,1,0:T(8,128)S(1)}, u32[]{:S(2)}, u32[]{:S(2)}) collective-permute-start(f32[4,136,128]{2,1,0:T(8,128)S(1)} %get-tuple-element.33), channel_id=1, source_target_pairs={{0,16},{16,0},{1,17},{17,1},{2,18},{18,2},{3,19},{19,3},{4,20},{20... | collective-permute-start | bytes 835592 | tf_op jit(solution)/shard_map/ppermute | solution.py:595
  34.8 10.4 %collective-permute-start.14 = (f32[4,136,128]{2,1,0:T(8,128)S(1)}, f32[4,136,128]{2,1,0:T(8,128)S(1)}, u32[]{:S(2)}, u32[]{:S(2)}) collective-permute-start(f32[4,136,128]{2,1,0:T(8,128)S(1)} %get-tuple-element.35), channel_id=1, source_target_pairs={{0,16},{16,0},{1,17},{17,1},{2,18},{18,2},{3,19},{19,3},{4,20},{20... | collective-permute-start | bytes 835592 | tf_op jit(solution)/shard_map/ppermute | solution.py:595
  37.0 12.2 %collective-permute-start.13 = (f16[4,136,128]{2,1,0:T(8,128)(2,1)S(1)}, f16[4,136,128]{2,1,0:T(8,128)(2,1)S(1)}, u32[]{:S(2)}, u32[]{:S(2)}) collective-permute-start(f16[4,136,128]{2,1,0:T(8,128)(2,1)S(1)} %convert_element_type.40), channel_id=1, source_target_pairs={{0,4},{8,12},{4,0},{12,8},{1,5},{9,13},{5,1},{13,9},{2,6},{10,14},... | collective-permute-start | bytes 417800 | tf_op jit(solution)/shard_map/ppermute | solution.py:157
  45.3 3.9 %collective-permute-start.15 = (f16[4,136,128]{2,1,0:T(8,128)(2,1)S(1)}, f16[4,136,128]{2,1,0:T(8,128)(2,1)S(1)}, u32[]{:S(2)}, u32[]{:S(2)}) collective-permute-start(f16[4,136,128]{2,1,0:T(8,128)(2,1)S(1)} %convert_element_type.42), channel_id=1, source_target_pairs={{4,8},{8,4},{5,9},{9,5},{6,10},{10,6},{7,11},{11,7},{20,24},{24,20... | collective-permute-start | bytes 417800 | tf_op jit(solution)/shard_map/ppermute | solution.py:157
  49.6 7.6 %collective-permute-start.17 = (f16[2,136,128]{2,1,0:T(8,128)(2,1)S(1)}, f16[2,136,128]{2,1,0:T(8,128)(2,1)S(1)}, u32[]{:S(2)}, u32[]{:S(2)}) collective-permute-start(f16[2,136,128]{2,1,0:T(8,128)(2,1)S(1)} %convert_element_type.46), channel_id=1, source_target_pairs={{1,2},{2,1},{5,6},{6,5},{9,10},{10,9},{13,14},{14,13},{17,18},{18,... | collective-permute-start | bytes 208904 | tf_op jit(solution)/shard_map/ppermute | solution.py:157
  50.3 6.9 %collective-permute-start.11 = (f16[2,136,128]{2,1,0:T(8,128)(2,1)S(1)}, f16[2,136,128]{2,1,0:T(8,128)(2,1)S(1)}, u32[]{:S(2)}, u32[]{:S(2)}) collective-permute-start(f16[2,136,128]{2,1,0:T(8,128)(2,1)S(1)} %convert_element_type.38), channel_id=1, source_target_pairs={{4,8},{8,4},{5,9},{9,5},{6,10},{10,6},{7,11},{11,7},{20,24},{24,20... | collective-permute-start | bytes 208904 | tf_op jit(solution)/shard_map/ppermute | solution.py:157
  50.9 7.8 %collective-permute-start.10 = (f16[2,136,128]{2,1,0:T(8,128)(2,1)S(1)}, f16[2,136,128]{2,1,0:T(8,128)(2,1)S(1)}, u32[]{:S(2)}, u32[]{:S(2)}) collective-permute-start(f16[2,136,128]{2,1,0:T(8,128)(2,1)S(1)} %convert_element_type.36), channel_id=1, source_target_pairs={{0,4},{8,12},{4,0},{12,8},{1,5},{9,13},{5,1},{13,9},{2,6},{10,14},... | collective-permute-start | bytes 208904 | tf_op jit(solution)/shard_map/ppermute | solution.py:157
  56.5 4.4 %collective-permute-start.16 = (f16[2,136,128]{2,1,0:T(8,128)(2,1)S(1)}, f16[2,136,128]{2,1,0:T(8,128)(2,1)S(1)}, u32[]{:S(2)}, u32[]{:S(2)}) collective-permute-start(f16[2,136,128]{2,1,0:T(8,128)(2,1)S(1)} %convert_element_type.44), channel_id=1, source_target_pairs={{0,1},{2,3},{1,0},{3,2},{4,5},{6,7},{5,4},{7,6},{8,9},{10,11},{9,8... | collective-permute-start | bytes 208904 | tf_op jit(solution)/shard_map/ppermute | solution.py:157

commit v2 on v1

--- a/solution.py
+++ b/solution.py
@@ -199,8 +199,6 @@
     couples = (slots + 1) // 2
     scaling = (slots * atoms) ** (-0.5)
     starts = [sum(ref.shape[0] for ref in piece_refs[:k]) for k in range(pieces)]
-    cross = 1 + sides[1] + sides[2]
-    blocks = (sides[1] + 1) * (sides[2] + 1)
 
     loads = [
         pltpu.make_async_copy(
@@ -228,10 +226,8 @@
         block = lax.div(target, tiles)
         steps = (lax.div(block, 9), lax.rem(lax.div(block, 3), 3), lax.rem(block, 3))
         x, y, z = (side_of(steps[k] - 1, axis_ref[k], sides[k]) for k in range(3))
-        diagonal = cross + (y - 1) * sides[2] + (z - 1)
-        straight = jnp.where(y == 0, z, sides[2] + y)
-        block = jnp.where((y > 0) & (z > 0), diagonal, straight)
-        return (x * blocks + block) * tiles + lax.rem(target, tiles)
+        block = (x * (sides[1] + 1) + y) * (sides[2] + 1) + z
+        return block * tiles + lax.rem(target, tiles)
 
     rates = [rates_ref[r] for r in range(radials)]
     powers = [-rate * LOG2E for rate in rates]
@@ -532,14 +528,12 @@
         points,
         readout.reshape(1, channels),
     )
-    (line,) = join([list(range(len(along_z)))], *along_z)
-    diagonal = swap(line, "gy")
-    along_y = swap(packed, "gy")
-    (cross,) = join([list(range(2 + len(along_y)))], packed, line, *along_y)
-    pieces = [[cross] + diagonal]
+    (line,) = join([list(range(1 + len(along_z)))], packed, *along_z)
+    lines = [line] + swap(line, "gy")
+    pieces = [lines]
     for pairs in swaps("gx"):
-        plane = [lax.ppermute(cross, "gx", pairs)]
-        pieces.append(plane + [lax.ppermute(piece, "gx", pairs) for piece in diagonal])
+        plane = [lax.ppermute(line, "gx", pairs)]
+        pieces.append(plane + [lax.ppermute(piece, "gx", pairs) for piece in lines[1:]])
     flat = [piece for plane in pieces for piece in plane]
 
     total = sum(piece.shape[0] for piece in flat)
@@ -595,22 +589,15 @@
             arrays.append(lax.ppermute(plane[k], "gx", pairs))
         return arrays
 
-    diagonal = []
+    received = []
     for k, pairs in enumerate(swaps("gy")):
         arrays = gather(k + 1)
         (value,) = fold([(0, arrays[0].shape[0], True)], arrays, [])
-        diagonal.append(send(value, "gy", pairs))
+        received.append(send(value, "gy", pairs))
     arrays = gather(0)
-    line = (sides[2] + 1) * tiles
-    cuts = [(0, tiles, False), (tiles, line, False)]
-    for k in range(sides[1]):
-        cuts.append((line + k * tiles, line + (k + 1) * tiles, True))
-    center, along_z, *along_y = fold(cuts, arrays, [])
+    cuts = [(k * tiles, (k + 1) * tiles, k > 0) for k in range(sides[2] + 1)]
+    center, *along_z = fold(cuts, arrays, received)
     parts = [center]
-    for value, pairs in zip(along_y, swaps("gy")):
-        parts.append(send(value, "gy", pairs))
-    cuts = [(k * tiles, (k + 1) * tiles, True) for k in range(sides[2])]
-    along_z = fold(cuts, [along_z], diagonal)
     for value, pairs in zip(along_z, swaps("gz")):
         parts.append(send(value, "gz", pairs))
 

time: 62.5 us -> 57.1 us (0.914)
  the two profiles are of different devices: /device:TPU:0 before, /device:TPU:14 now
where the time goes in v2:
time: 57.1 us; the launch traced here: 56.8 us
  waiting for transfers between devices  22.5 us (39%)
  Pallas kernels  20.6 us (36%)
  starting transfers between devices  11.1 us (19%)
  local copies, waits for them, and re-layouts  1.6 us (3%)
  between operations  0.86 us (2%)
    pallas_call x1, Pallas kernels, step(): pl.pallas_call(functools.partial(main_kernel, len(flat), sides, slots), o...  16.2 us
    ppermute x4, waiting for transfers between devices, send(): lax.ppermute(value.astype(jnp.float16), axis, pairs).astype(jnp.float32)  11.4 us
    ppermute x4, waiting for transfers between devices, swap(): return [lax.ppermute(value, axis, pairs) for pairs in swaps(axis)]  9.52 us
    ppermute x4, starting transfers between devices, swap(): return [lax.ppermute(value, axis, pairs) for pairs in swaps(axis)]  7.62 us
    ppermute x4, starting transfers between devices, send(): lax.ppermute(value.astype(jnp.float16), axis, pairs).astype(jnp.float32)  2.73 us
    unnamed x14, local copies, waits for them, and re-layouts  1.6 us
    ppermute x3, waiting for transfers between devices, gather(): arrays.append(lax.ppermute(plane[k], 'gx', pairs))  1.56 us
    pallas_call x1, Pallas kernels, step(): pl.pallas_call(pack_kernel, out_shape=jax.ShapeDtypeStruct((tiles, atoms...  1.53 us
  transfers between devices with their start and end apart: 14, of which 8 were waited for; matrix products, arithmetic and copies ran while one was open for 0% of the time, Pallas kernels for 2%

profile of v2, /device:TPU:14, one launch (start us, length us, event | category | flops | bytes accessed | tf_op | source)
XLA Modules:
  0.0 56.8 jit_solution(7015424664866320234)
XLA Ops:
  0.6 1.5 %pack.1.refs_0_ = bf16[2,144,128]{2,1,0:T(8,128)(2,1)} custom-call(s32[2]{0:T(128)} %bitcast.16, bf16[2,128,128]{2,1,0:T(8,128)(2,1)} %bitcast.20, f32[3,2,128]{2,1,0:T(2,128)} %bitcast.14), custom_call_target="tpu_custom_call" | custom-call | tf_op jit(solution)/shard_map/pack/pallas_call | solution.py:501
  2.2 0.7 %collective-permute-start.1 = (bf16[2,144,128]{2,1,0:T(8,128)(2,1)}, bf16[2,144,128]{2,1,0:T(8,128)(2,1)S(1)}, u32[]{:S(2)}, u32[]{:S(2)}) collective-permute-start(bf16[2,144,128]{2,1,0:T(8,128)(2,1)} %pack.1.refs_0_), channel_id=1, source_target_pairs={{1,2},{2,1},{5,6},{6,5},{9,10},{10,9},{13,14},{14,13},{17,18},{18,... | collective-permute-start | bytes 221192 | tf_op jit(solution)/shard_map/ppermute | solution.py:496
  2.8 3.3 %collective-permute-start = (bf16[2,144,128]{2,1,0:T(8,128)(2,1)}, bf16[2,144,128]{2,1,0:T(8,128)(2,1)S(1)}, u32[]{:S(2)}, u32[]{:S(2)}) collective-permute-start(bf16[2,144,128]{2,1,0:T(8,128)(2,1)} %pack.1.refs_0_), channel_id=1, source_target_pairs={{0,1},{2,3},{1,0},{3,2},{4,5},{6,7},{5,4},{7,6},{8,9},{10,11},{9,8... | collective-permute-start | bytes 221192 | tf_op jit(solution)/shard_map/ppermute | solution.py:496
  6.1 3.7 %collective-permute-done.refs_1_ = bf16[2,144,128]{2,1,0:T(8,128)(2,1)S(1)} collective-permute-done((bf16[2,144,128]{2,1,0:T(8,128)(2,1)}, bf16[2,144,128]{2,1,0:T(8,128)(2,1)S(1)}, u32[]{:S(2)}, u32[]{:S(2)}) %collective-permute-start) | collective-permute-done | bytes 73760 | tf_op jit(solution)/shard_map/ppermute | solution.py:496
  9.8 0.9 %copy-done = bf16[2,144,128]{2,1,0:T(8,128)(2,1)S(1)} copy-done((bf16[2,144,128]{2,1,0:T(8,128)(2,1)S(1)}, bf16[2,144,128]{2,1,0:T(8,128)(2,1)}, u32[]{:S(2)}) %copy-start) | copy-done | bytes 73752
  10.7 3.6 %collective-permute-start.3 = (bf16[6,144,128]{2,1,0:T(8,128)(2,1)S(1)}, bf16[6,144,128]{2,1,0:T(8,128)(2,1)S(1)}, u32[]{:S(2)}, u32[]{:S(2)}) collective-permute-start(bf16[6,144,128]{2,1,0:T(8,128)(2,1)S(1)} %join.1.refs_0_), channel_id=1, source_target_pairs={{4,8},{8,4},{5,9},{9,5},{6,10},{10,6},{7,11},{11,7},{20,24},{24,20... | collective-permute-start | bytes 663560 | tf_op jit(solution)/shard_map/ppermute | solution.py:496
  14.3 0.1 collective-permute-start.2
  14.4 0.1 collective-permute-start.4
  14.5 4.3 %collective-permute-done.3.refs_2_ = bf16[6,144,128]{2,1,0:T(8,128)(2,1)S(1)} collective-permute-done((bf16[6,144,128]{2,1,0:T(8,128)(2,1)S(1)}, bf16[6,144,128]{2,1,0:T(8,128)(2,1)S(1)}, u32[]{:S(2)}, u32[]{:S(2)}) %collective-permute-start.3) | collective-permute-done | bytes 221216 | tf_op jit(solution)/shard_map/ppermute | solution.py:496
  18.7 1.6 %collective-permute-done.2.refs_1_ = bf16[6,144,128]{2,1,0:T(8,128)(2,1)S(1)} collective-permute-done((bf16[6,144,128]{2,1,0:T(8,128)(2,1)S(1)}, bf16[6,144,128]{2,1,0:T(8,128)(2,1)S(1)}, u32[]{:S(2)}, u32[]{:S(2)}) %collective-permute-start.2) | collective-permute-done | bytes 221216 | tf_op jit(solution)/shard_map/ppermute | solution.py:496
  20.4 0.6 %copy-done.5 = f32[4]{0:T(128)S(1)} copy-done((f32[4]{0:T(128)S(1)}, f32[4]{0:T(128)}, u32[]{:S(2)}) %copy-start.5) | copy-done | bytes 40
  21.0 0.0 copy-done.2
  21.0 0.0 copy-done.4
  21.1 1.2 %sides.1 = (s32[2]{0:T(128)S(1)}, s32[2,8]{1,0:T(2,128)S(1)}, f32[4]{0:T(128)S(1)}, f32[3,2,128]{2,1,0:T(2,128)S(1)}, f32[1,128]{1,0:T(1,128)S(1)}) custom-call(s32[2]{0:T(128)S(1)} %bitcast.17, s32[2,8]{1,0:T(2,128)S(1)} %bitcast.18, f32[4]{0:T(128)S(1)} %copy-done.5, f32[3,2,128]{2,1,0:T(2,128)S(1)} %bitcast.15, f32[1,128]{1,0:T(1,128)S(1)} %bitcast.19), custom_call_target="tpu_custom_call" | custom-call | tf_op jit(solution)/shard_map/sides/pallas_call | solution.py:511
  22.3 0.1 pad_add_fusion.axis_ref
  22.4 16.2 %pairs.1 = (f32[6,136,128]{2,1,0:T(8,128)S(1)}, f32[6,136,128]{2,1,0:T(8,128)S(1)}, f32[6,136,128]{2,1,0:T(8,128)S(1)}, f32[6,136,128]{2,1,0:T(8,128)S(1)}, f32[...) custom-call(s32[3]{0:T(128)S(1)} %pad_add_fusion.axis_ref, s32[2]{0:T(128)S(1)} %get-tuple-element.18.counts_ref, ...), custom_call_target="tpu_custom_call" | custom-call | tf_op jit(solution)/shard_map/pairs/pallas_call | solution.py:545
  38.5 0.1 collective-permute-start.8
  38.6 0.5 collective-permute-start.10
  39.1 0.1 collective-permute-start.7
  39.2 1.2 %collective-permute-done.8.refs_1_ = f32[6,136,128]{2,1,0:T(8,128)S(1)} collective-permute-done((f32[6,136,128]{2,1,0:T(8,128)S(1)}, f32[6,136,128]{2,1,0:T(8,128)S(1)}, u32[]{:S(2)}, u32[]{:S(2)}) %collective-permute-start.8) | collective-permute-done | bytes 417824 | tf_op jit(solution)/shard_map/ppermute | solution.py:589
  40.4 0.1 fold.3
  40.5 0.1 collective-permute-start.9
  40.6 0.4 collective-permute-done.10.refs_1_
  41.0 0.1 fold.4
  41.1 1.9 %collective-permute-start.11 = (f16[6,136,128]{2,1,0:T(8,128)(2,1)S(1)}, f16[6,136,128]{2,1,0:T(8,128)(2,1)S(1)}, u32[]{:S(2)}, u32[]{:S(2)}) collective-permute-start(f16[6,136,128]{2,1,0:T(8,128)(2,1)S(1)} %convert_element_type.26), channel_id=1, source_target_pairs={{4,8},{8,4},{5,9},{9,5},{6,10},{10,6},{7,11},{11,7},{20,24},{24,20... | collective-permute-start | bytes 626696 | tf_op jit(solution)/shard_map/ppermute | solution.py:157
  43.0 4.7 %collective-permute-done.9 = f16[6,136,128]{2,1,0:T(8,128)(2,1)S(1)} collective-permute-done((f16[6,136,128]{2,1,0:T(8,128)(2,1)S(1)}, f16[6,136,128]{2,1,0:T(8,128)(2,1)S(1)}, u32[]{:S(2)}, u32[]{:S(2)}) %collective-permute-start.9) | collective-permute-done | bytes 208928 | tf_op jit(solution)/shard_map/ppermute | solution.py:157
  47.8 2.4 %collective-permute-done.11 = f16[6,136,128]{2,1,0:T(8,128)(2,1)S(1)} collective-permute-done((f16[6,136,128]{2,1,0:T(8,128)(2,1)S(1)}, f16[6,136,128]{2,1,0:T(8,128)(2,1)S(1)}, u32[]{:S(2)}, u32[]{:S(2)}) %collective-permute-start.11) | collective-permute-done | bytes 208928 | tf_op jit(solution)/shard_map/ppermute | solution.py:157
  50.2 0.2 fold.5
  50.4 0.7 %collective-permute-start.13 = (f16[2,136,128]{2,1,0:T(8,128)(2,1)S(1)}, f16[2,136,128]{2,1,0:T(8,128)(2,1)S(1)}, u32[]{:S(2)}, u32[]{:S(2)}) collective-permute-start(f16[2,136,128]{2,1,0:T(8,128)(2,1)S(1)} %convert_element_type.30), channel_id=1, source_target_pairs={{1,2},{2,1},{5,6},{6,5},{9,10},{10,9},{13,14},{14,13},{17,18},{18,... | collective-permute-start | bytes 208904 | tf_op jit(solution)/shard_map/ppermute | solution.py:157
  51.1 0.1 collective-permute-start.12
  51.2 4.3 %collective-permute-done.12 = f16[2,136,128]{2,1,0:T(8,128)(2,1)S(1)} collective-permute-done((f16[2,136,128]{2,1,0:T(8,128)(2,1)S(1)}, f16[2,136,128]{2,1,0:T(8,128)(2,1)S(1)}, u32[]{:S(2)}, u32[]{:S(2)}) %collective-permute-start.12) | collective-permute-done | bytes 69664 | tf_op jit(solution)/shard_map/ppermute | solution.py:157
  55.5 1.3 %finish.1 = (f32[3,2,128]{2,1,0:T(2,128)}, f32[2,128,128]{2,1,0:T(8,128)}) custom-call(s32[2]{0:T(128)S(1)} %get-tuple-element.18.counts_ref, f32[2,136,128]{2,1,0:T(8,128)S(1)} %get-tuple-element.29.center_ref, f32[2,136,128]{2,1,0:T(8,128)S(1)} %convert_element_type.29.refs_0_, f32[2,136,128]{2,1,0:T(8,128)S(1)} %convert_element_type.31.refs_1_), custom_call_target="tpu_custom_call" | custom-call | tf_op jit(solution)/shard_map/finish/pallas_call | solution.py:604
  (27 shorter events, 0.2 us)
Async XLA Ops:
  2.2 3.9 %collective-permute-start.1 = (bf16[2,144,128]{2,1,0:T(8,128)(2,1)}, bf16[2,144,128]{2,1,0:T(8,128)(2,1)S(1)}, u32[]{:S(2)}, u32[]{:S(2)}) collective-permute-start(bf16[2,144,128]{2,1,0:T(8,128)(2,1)} %pack.1.refs_0_), channel_id=1, source_target_pairs={{1,2},{2,1},{5,6},{6,5},{9,10},{10,9},{13,14},{14,13},{17,18},{18,... | collective-permute-start | bytes 221192 | tf_op jit(solution)/shard_map/ppermute | solution.py:496
  2.8 7.0 %collective-permute-start = (bf16[2,144,128]{2,1,0:T(8,128)(2,1)}, bf16[2,144,128]{2,1,0:T(8,128)(2,1)S(1)}, u32[]{:S(2)}, u32[]{:S(2)}) collective-permute-start(bf16[2,144,128]{2,1,0:T(8,128)(2,1)} %pack.1.refs_0_), channel_id=1, source_target_pairs={{0,1},{2,3},{1,0},{3,2},{4,5},{6,7},{5,4},{7,6},{8,9},{10,11},{9,8... | collective-permute-start | bytes 221192 | tf_op jit(solution)/shard_map/ppermute | solution.py:496
  9.8 0.9 %copy-start = (bf16[2,144,128]{2,1,0:T(8,128)(2,1)S(1)}, bf16[2,144,128]{2,1,0:T(8,128)(2,1)}, u32[]{:S(2)}) copy-start(bf16[2,144,128]{2,1,0:T(8,128)(2,1)} %pack.1.refs_0_) | copy-start | bytes 221188
  10.7 11.7 %copy-start.1 = (bf16[1024,128]{1,0:T(8,128)(2,1)S(1)}, bf16[1024,128]{1,0:T(8,128)(2,1)}, u32[]{:S(2)}) copy-start(bf16[1024,128]{1,0:T(8,128)(2,1)} %mixing_ref.1) | copy-start | bytes 786436
  10.7 8.0 %collective-permute-start.3 = (bf16[6,144,128]{2,1,0:T(8,128)(2,1)S(1)}, bf16[6,144,128]{2,1,0:T(8,128)(2,1)S(1)}, u32[]{:S(2)}, u32[]{:S(2)}) collective-permute-start(bf16[6,144,128]{2,1,0:T(8,128)(2,1)S(1)} %join.1.refs_0_), channel_id=1, source_target_pairs={{4,8},{8,4},{5,9},{9,5},{6,10},{10,6},{7,11},{11,7},{20,24},{24,20... | collective-permute-start | bytes 663560 | tf_op jit(solution)/shard_map/ppermute | solution.py:496
  14.3 6.0 %collective-permute-start.2 = (bf16[6,144,128]{2,1,0:T(8,128)(2,1)S(1)}, bf16[6,144,128]{2,1,0:T(8,128)(2,1)S(1)}, u32[]{:S(2)}, u32[]{:S(2)}) collective-permute-start(bf16[6,144,128]{2,1,0:T(8,128)(2,1)S(1)} %join.1.refs_0_), channel_id=1, source_target_pairs={{0,4},{8,12},{4,0},{12,8},{1,5},{9,13},{5,1},{13,9},{2,6},{10,14},... | collective-permute-start | bytes 663560 | tf_op jit(solution)/shard_map/ppermute | solution.py:496
  14.4 7.9 %collective-permute-start.4 = (bf16[6,144,128]{2,1,0:T(8,128)(2,1)S(1)}, bf16[6,144,128]{2,1,0:T(8,128)(2,1)S(1)}, u32[]{:S(2)}, u32[]{:S(2)}) collective-permute-start(bf16[6,144,128]{2,1,0:T(8,128)(2,1)S(1)} %join.1.refs_0_), channel_id=1, source_target_pairs={{0,16},{16,0},{1,17},{17,1},{2,18},{18,2},{3,19},{19,3},{4,20},{20... | collective-permute-start | bytes 663560 | tf_op jit(solution)/shard_map/ppermute | solution.py:535
  18.7 3.6 %collective-permute-start.6 = (bf16[6,144,128]{2,1,0:T(8,128)(2,1)S(1)}, bf16[6,144,128]{2,1,0:T(8,128)(2,1)S(1)}, u32[]{:S(2)}, u32[]{:S(2)}) collective-permute-start(bf16[6,144,128]{2,1,0:T(8,128)(2,1)S(1)} %collective-permute-done.3.refs_2_), channel_id=1, source_target_pairs={{0,16},{16,0},{1,17},{17,1},{2,18},{18,2},{3,19},{19,3},{4,20},{20... | collective-permute-start | bytes 663560 | tf_op jit(solution)/shard_map/ppermute | solution.py:536
  20.3 2.0 %collective-permute-start.5 = (bf16[6,144,128]{2,1,0:T(8,128)(2,1)S(1)}, bf16[6,144,128]{2,1,0:T(8,128)(2,1)S(1)}, u32[]{:S(2)}, u32[]{:S(2)}) collective-permute-start(bf16[6,144,128]{2,1,0:T(8,128)(2,1)S(1)} %collective-permute-done.2.refs_1_), channel_id=1, source_target_pairs={{0,16},{16,0},{1,17},{17,1},{2,18},{18,2},{3,19},{19,3},{4,20},{20... | collective-permute-start | bytes 663560 | tf_op jit(solution)/shard_map/ppermute | solution.py:536
  20.3 0.7 %copy-start.5 = (f32[4]{0:T(128)S(1)}, f32[4]{0:T(128)}, u32[]{:S(2)}) copy-start(f32[4]{0:T(128)} %rates_ref.1) | copy-start | bytes 52
  20.3 0.7 %copy-start.6 = (f32[128]{0:T(128)S(1)}, f32[128]{0:T(128)}, u32[]{:S(2)}) copy-start(f32[128]{0:T(128)} %param.12) | copy-start | bytes 1540
  20.3 0.7 %copy-start.2 = (f32[1,1,1,2,3,128]{5,3,4,2,1,0:T(2,128)S(1)}, f32[1,1,1,2,3,128]{5,3,4,2,1,0:T(2,128)}, u32[]{:S(2)}) copy-start(f32[1,1,1,2,3,128]{5,3,4,2,1,0:T(2,128)} %param.7) | copy-start | bytes 9220
  20.3 0.7 %copy-start.3 = (s32[1,1,1,2]{3,2,1,0:T(1,128)S(1)}, s32[1,1,1,2]{3,2,1,0:T(1,128)}, u32[]{:S(2)}) copy-start(s32[1,1,1,2]{3,2,1,0:T(1,128)} %param.9) | copy-start | bytes 28
  20.3 0.7 %copy-start.4 = (s32[1,1,1,2,8]{4,3,2,1,0:T(2,128)S(1)}, s32[1,1,1,2,8]{4,3,2,1,0:T(2,128)}, u32[]{:S(2)}) copy-start(s32[1,1,1,2,8]{4,3,2,1,0:T(2,128)} %param.10) | copy-start | bytes 196
  38.5 1.8 %collective-permute-start.8 = (f32[6,136,128]{2,1,0:T(8,128)S(1)}, f32[6,136,128]{2,1,0:T(8,128)S(1)}, u32[]{:S(2)}, u32[]{:S(2)}) collective-permute-start(f32[6,136,128]{2,1,0:T(8,128)S(1)} %get-tuple-element.26), channel_id=1, source_target_pairs={{0,16},{16,0},{1,17},{17,1},{2,18},{18,2},{3,19},{19,3},{4,20},{20... | collective-permute-start | bytes 1253384 | tf_op jit(solution)/shard_map/ppermute | solution.py:589
  38.6 2.3 %collective-permute-start.10 = (f32[6,136,128]{2,1,0:T(8,128)S(1)}, f32[6,136,128]{2,1,0:T(8,128)S(1)}, u32[]{:S(2)}, u32[]{:S(2)}) collective-permute-start(f32[6,136,128]{2,1,0:T(8,128)S(1)} %get-tuple-element.28), channel_id=1, source_target_pairs={{0,16},{16,0},{1,17},{17,1},{2,18},{18,2},{3,19},{19,3},{4,20},{20... | collective-permute-start | bytes 1253384 | tf_op jit(solution)/shard_map/ppermute | solution.py:589
  39.1 11.1 %collective-permute-start.7 = (f32[6,136,128]{2,1,0:T(8,128)S(1)}, f32[6,136,128]{2,1,0:T(8,128)S(1)}, u32[]{:S(2)}, u32[]{:S(2)}) collective-permute-start(f32[6,136,128]{2,1,0:T(8,128)S(1)} %get-tuple-element.24), channel_id=1, source_target_pairs={{0,16},{16,0},{1,17},{17,1},{2,18},{18,2},{3,19},{19,3},{4,20},{20... | collective-permute-start | bytes 1253384 | tf_op jit(solution)/shard_map/ppermute | solution.py:589
  40.5 7.3 %collective-permute-start.9 = (f16[6,136,128]{2,1,0:T(8,128)(2,1)S(1)}, f16[6,136,128]{2,1,0:T(8,128)(2,1)S(1)}, u32[]{:S(2)}, u32[]{:S(2)}) collective-permute-start(f16[6,136,128]{2,1,0:T(8,128)(2,1)S(1)} %convert_element_type.24), channel_id=1, source_target_pairs={{0,4},{8,12},{4,0},{12,8},{1,5},{9,13},{5,1},{13,9},{2,6},{10,14},... | collective-permute-start | bytes 626696 | tf_op jit(solution)/shard_map/ppermute | solution.py:157
  41.1 9.1 %collective-permute-start.11 = (f16[6,136,128]{2,1,0:T(8,128)(2,1)S(1)}, f16[6,136,128]{2,1,0:T(8,128)(2,1)S(1)}, u32[]{:S(2)}, u32[]{:S(2)}) collective-permute-start(f16[6,136,128]{2,1,0:T(8,128)(2,1)S(1)} %convert_element_type.26), channel_id=1, source_target_pairs={{4,8},{8,4},{5,9},{9,5},{6,10},{10,6},{7,11},{11,7},{20,24},{24,20... | collective-permute-start | bytes 626696 | tf_op jit(solution)/shard_map/ppermute | solution.py:157
  50.4 0.8 %collective-permute-start.13 = (f16[2,136,128]{2,1,0:T(8,128)(2,1)S(1)}, f16[2,136,128]{2,1,0:T(8,128)(2,1)S(1)}, u32[]{:S(2)}, u32[]{:S(2)}) collective-permute-start(f16[2,136,128]{2,1,0:T(8,128)(2,1)S(1)} %convert_element_type.30), channel_id=1, source_target_pairs={{1,2},{2,1},{5,6},{6,5},{9,10},{10,9},{13,14},{14,13},{17,18},{18,... | collective-permute-start | bytes 208904 | tf_op jit(solution)/shard_map/ppermute | solution.py:157
  51.1 4.4 %collective-permute-start.12 = (f16[2,136,128]{2,1,0:T(8,128)(2,1)S(1)}, f16[2,136,128]{2,1,0:T(8,128)(2,1)S(1)}, u32[]{:S(2)}, u32[]{:S(2)}) collective-permute-start(f16[2,136,128]{2,1,0:T(8,128)(2,1)S(1)} %convert_element_type.28), channel_id=1, source_target_pairs={{0,1},{2,3},{1,0},{3,2},{4,5},{6,7},{5,4},{7,6},{8,9},{10,11},{9,8... | collective-permute-start | bytes 208904 | tf_op jit(solution)/shard_map/ppermute | solution.py:157

commit v3 on v2

--- a/solution.py
+++ b/solution.py
@@ -15,7 +15,7 @@
 GROUP = 8
 LOG2E = 1.4426950408889634
 SMALL = 8 << 20
-LARGE = 30 << 20
+LARGE = 20 << 20
 NT = (((1,), (1,)), ((), ()))
 
 
@@ -51,26 +51,52 @@
 
 
 def side_kernel(
+    sides,
+    axis_ref,
     counts_ref,
     neighbours_ref,
     rates_ref,
     points_ref,
     readout_ref,
+    packed_ref,
     out_counts_ref,
-    out_neighbours_ref,
+    out_table_ref,
     out_rates_ref,
     out_points_ref,
     out_readout_ref,
+    out_packed_ref,
 ):
     tiles, slots = neighbours_ref.shape
     for t in range(tiles):
         out_counts_ref[t] = counts_ref[t]
+        spots = []
         for k in range(slots):
-            out_neighbours_ref[t, k] = neighbours_ref[t, k]
+            target = jnp.maximum(neighbours_ref[t, k], 0)
+            block = lax.div(target, tiles)
+            steps = (lax.div(block, 9), lax.rem(lax.div(block, 3), 3), lax.rem(block, 3))
+            x, y, z = (side_of(steps[m] - 1, axis_ref[m], sides[m]) for m in range(3))
+            block = (x * (sides[1] + 1) + y) * (sides[2] + 1) + z
+            live = neighbours_ref[t, k] >= 0
+            spots.append((block * tiles + lax.rem(target, tiles), live, live & (y == 0)))
+            out_table_ref[t, k] = -1
+        near = sum(jnp.where(line, 1, 0) for _, _, line in spots)
+        total = sum(jnp.where(live, 1, 0) for _, live, _ in spots)
+        out_table_ref[t, slots] = near
+        out_table_ref[t, slots + 1] = total
+        at_near, at_far = jnp.zeros((), jnp.int32), near
+        for spot, live, line in spots:
+
+            def put(spot=spot, at=jnp.where(line, at_near, at_far)):
+                out_table_ref[t, at] = spot
+
+            pl.when(live)(put)
+            at_near = at_near + jnp.where(line, 1, 0)
+            at_far = at_far + jnp.where(live & ~line, 1, 0)
     for r in range(rates_ref.shape[0]):
         out_rates_ref[r] = rates_ref[r]
     out_points_ref[...] = points_ref[...]
     out_readout_ref[...] = readout_ref[...]
+    out_packed_ref[...] = packed_ref[...]
 
 
 def join_kernel(groups, *refs):
@@ -157,13 +183,161 @@
     return lax.ppermute(value.astype(jnp.float16), axis, pairs).astype(jnp.float32)
 
 
+class Pairs:
+    def __init__(self, rates_ref, own_ref, other_ref, channels, atoms):
+        self.rates = [rates_ref[r] for r in range(rates_ref.shape[0])]
+        self.powers = [-rate * LOG2E for rate in self.rates]
+        self.own_ref, self.other_ref = own_ref, other_ref
+        self.channels, self.atoms = channels, atoms
+        self.group_rows = 4 * len(self.rates) * GROUP
+        self.groups = ROWS // GROUP
+        self.chunk_rows = self.group_rows * self.groups
+
+    def geometry(self, t, slot, where):
+        offset = [self.other_ref[t, slot, m] - self.own_ref[t, m, where, :] for m in range(3)]
+        square = offset[0] * offset[0] + offset[1] * offset[1] + offset[2] * offset[2]
+        return offset, [jnp.exp2(power * square) for power in self.powers]
+
+    def backward(
+        self,
+        t,
+        chunks,
+        first,
+        last,
+        masked,
+        block,
+        couples,
+        seed_ref,
+        seed_t_ref,
+        features_ref,
+        basis_ref,
+        near_grad_ref,
+        near_force_ref,
+        own_force_ref,
+        grad_refs,
+    ):
+        atoms, group_rows, chunk_rows = self.atoms, self.group_rows, self.chunk_rows
+        near_grad_ref[...] = jnp.zeros_like(near_grad_ref)
+        near_force_ref[...] = jnp.zeros_like(near_force_ref)
+        steps = (last - first) * chunks
+
+        def following(place):
+            couple, chunk = place
+            wrap = chunk + 1 >= chunks
+            couple = jnp.where(wrap, couple + 1, couple)
+            return jnp.where(couple < last, couple, couples), jnp.where(wrap, 0, chunk + 1)
+
+        def multiply(place, grad_ref):
+            couple, chunk = place
+            base = pl.multiple_of(chunk * chunk_rows, chunk_rows)
+            where = pl.ds(base, chunk_rows)
+            spot = jnp.where(couple == masked, block, couple)
+            spot = pl.multiple_of(spot * 2 * atoms, 2 * atoms)
+            grad_ref[...] = lax.dot_general(
+                seed_ref[t, where, :],
+                features_ref[t, pl.ds(spot, 2 * atoms), :],
+                NT,
+                preferred_element_type=jnp.float32,
+            )
+            stored = jnp.minimum(couple, couples - 1)
+            basis = [basis_ref[t, 2 * stored + half, where, :] for half in range(2)]
+            near_grad_ref[couple] += jnp.dot(
+                seed_t_ref[t, chunk],
+                jnp.concatenate(basis, axis=1),
+                preferred_element_type=jnp.float32,
+            )
+
+        def pull(place, grad_ref):
+            couple, chunk = place
+            start = pl.multiple_of(chunk * ROWS, ROWS)
+            pulled = [[None] * 3 for _ in range(2)]
+            for g in range(self.groups):
+                rows = pl.ds(start + g * GROUP, GROUP)
+                total = [None] * 3
+                for half in range(2):
+                    lanes = slice(half * atoms, (half + 1) * atoms)
+                    offset, radial = self.geometry(t, 2 * couple + half, rows)
+                    direct = [None] * 3
+                    inner = None
+                    for r, rate in enumerate(self.rates):
+                        row = g * group_rows + 4 * r * GROUP
+                        grad = [
+                            grad_ref[row + m * GROUP : row + (m + 1) * GROUP, lanes]
+                            for m in range(4)
+                        ]
+                        along = grad[0]
+                        for m in range(3):
+                            along = along + grad[m + 1] * offset[m]
+                            part = radial[r] * grad[m + 1]
+                            direct[m] = part if r == 0 else direct[m] + part
+                        part = (radial[r] * (2.0 * rate)) * along
+                        inner = part if r == 0 else inner + part
+                    for m in range(3):
+                        force = direct[m] - offset[m] * inner
+                        total[m] = force if half == 0 else total[m] + force
+                        old = pulled[half][m]
+                        pulled[half][m] = force if g == 0 else old + force
+                for m in range(3):
+                    own_force_ref[t, m, rows, :] += total[m]
+            for half in range(2):
+                for m in range(3):
+                    near_force_ref[couple, half, m] += pulled[half][m]
+
+        one = (first, jnp.zeros((), jnp.int32))
+        two = following(one)
+        multiply(one, grad_refs[0])
+        multiply(two, grad_refs[1])
+
+        def loop(k, places):
+            one, two = places
+            three = following(two)
+            four = following(three)
+            five = following(four)
+            six = following(five)
+            pull(one, grad_refs[0])
+            multiply(three, grad_refs[2])
+            pull(two, grad_refs[1])
+            multiply(four, grad_refs[3])
+            pull(three, grad_refs[2])
+            multiply(five, grad_refs[0])
+            pull(four, grad_refs[3])
+            multiply(six, grad_refs[1])
+            return five, six
+
+        lax.fori_loop(0, (steps + 3) // 4, loop, (one, two))
+
+    def give(self, slot, tile, near_grad_ref, near_force_ref, ghost_ref):
+        couple, half = divmod(slot, 2)
+        channels, atoms = self.channels, self.atoms
+        lanes = slice(half * atoms, (half + 1) * atoms)
+        ghost_ref[tile, :channels, :] += near_grad_ref[couple, :, lanes]
+        for m in range(3):
+            ghost_ref[tile, channels + m : channels + m + 1, :] -= jnp.sum(
+                near_force_ref[couple, half, m], axis=0, keepdims=True
+            )
+
+
+def starts_of(piece_refs):
+    return [sum(ref.shape[0] for ref in piece_refs[:k]) for k in range(len(piece_refs))]
+
+
+def copies(pairs, sems):
+    result = [
+        pltpu.make_async_copy(source, target, sems.at[k])
+        for k, (source, target) in enumerate(pairs)
+    ]
+    for copy in result:
+        copy.start()
+    return result
+
+
 def main_kernel(
     pieces,
-    sides,
+    outs,
     slots,
-    axis_ref,
+    line,
     counts_ref,
-    neighbours_ref,
+    table_ref,
     rates_ref,
     points_ref,
     mixing_ref,
@@ -171,43 +345,36 @@
     *refs,
 ):
     piece_refs = refs[:pieces]
-    ghost_refs = refs[pieces : 2 * pieces]
+    ghost_refs = refs[pieces : pieces + outs]
     (
-        near_ref,
         own_ref,
         other_ref,
         features_ref,
         basis_ref,
-        sum_ref,
         seed_ref,
         seed_t_ref,
+        own_force_ref,
+        near_ref,
+        sum_ref,
         near_grad_ref,
         near_force_ref,
-        own_force_ref,
         ghost_ref,
         in_sems,
         out_sems,
         *grad_refs,
-    ) = refs[2 * pieces :]
+    ) = refs[pieces + outs :]
     _, tiles, atoms = points_ref.shape
     channels = readout_ref.shape[1]
-    radials = rates_ref.shape[0]
-    bases = 4 * radials
-    group_rows = bases * GROUP
-    groups = ROWS // GROUP
-    chunk_rows = bases * ROWS
     couples = (slots + 1) // 2
     scaling = (slots * atoms) ** (-0.5)
-    starts = [sum(ref.shape[0] for ref in piece_refs[:k]) for k in range(pieces)]
-
-    loads = [
-        pltpu.make_async_copy(
-            piece_refs[k], near_ref.at[pl.ds(starts[k], piece_refs[k].shape[0])], in_sems.at[k]
-        )
-        for k in range(pieces)
-    ]
-    for load in loads:
-        load.start()
+    starts = starts_of(piece_refs)
+    loads = copies(
+        [
+            (ref, near_ref.at[pl.ds(start, ref.shape[0])])
+            for ref, start in zip(piece_refs, starts)
+        ],
+        in_sems,
+    )
 
     for t in range(tiles):
         lines = [points_ref[m, t : t + 1, :] for m in range(3)]
@@ -221,51 +388,48 @@
     for load in loads:
         load.wait()
 
-    def located(target):
-        target = jnp.maximum(target, 0)
-        block = lax.div(target, tiles)
-        steps = (lax.div(block, 9), lax.rem(lax.div(block, 3), 3), lax.rem(block, 3))
-        x, y, z = (side_of(steps[k] - 1, axis_ref[k], sides[k]) for k in range(3))
-        block = (x * (sides[1] + 1) + y) * (sides[2] + 1) + z
-        return block * tiles + lax.rem(target, tiles)
-
-    rates = [rates_ref[r] for r in range(radials)]
-    powers = [-rate * LOG2E for rate in rates]
-
-    def geometry(t, slot, where):
-        offset = [other_ref[t, slot, m] - own_ref[t, m, where, :] for m in range(3)]
-        square = offset[0] * offset[0] + offset[1] * offset[1] + offset[2] * offset[2]
-        return offset, [jnp.exp2(power * square) for power in powers]
+    pairs = Pairs(rates_ref, own_ref, other_ref, channels, atoms)
+    radials, groups = len(pairs.rates), pairs.groups
+    group_rows, chunk_rows = pairs.group_rows, pairs.chunk_rows
 
     for t in range(tiles):
         count = counts_ref[t]
         chunks = (count + (ROWS - 1)) // ROWS
-
-        def work(t=t, count=count, chunks=chunks):
-            live = 0
+        near = table_ref[t, slots]
+        total_live = table_ref[t, slots + 1]
+
+        def work(t=t, count=count, chunks=chunks, near=near, total_live=total_live):
             for k in range(slots):
-                target = neighbours_ref[t, k]
-                live = live + jnp.where(target >= 0, 1, 0)
-                tile = located(target)
+                tile = table_ref[t, k]
+                live = tile >= 0
+                tile = jnp.maximum(tile, 0)
                 values = near_ref[tile, :atoms, :]
                 features_ref[t, k * atoms : (k + 1) * atoms] = jnp.where(
-                    target >= 0, values, jnp.zeros_like(values)
+                    live, values, jnp.zeros_like(values)
                 )
                 extra = near_ref[tile, atoms:, :].astype(jnp.float32)
                 total = extra[0:3] + extra[3:6] + extra[6:9]
                 for m in range(3):
                     other_ref[t, k, m] = jnp.broadcast_to(total[m : m + 1, :], (GROUP, atoms))
             for k in range(slots, 2 * couples + 2):
-                features_ref[t, k * atoms : (k + 1) * atoms] = jnp.zeros((atoms, channels), jnp.bfloat16)
                 for m in range(3):
                     other_ref[t, k, m] = jnp.zeros((GROUP, atoms), jnp.float32)
+            features_ref[t, slots * atoms :] = jnp.zeros(
+                ((2 * couples + 6 - slots) * atoms, channels), jnp.bfloat16
+            )
+            ahead = pl.ds(pl.multiple_of(near * atoms, atoms), atoms)
+            behind = pl.ds(pl.multiple_of((near - 1) * atoms, atoms), atoms)
+            spare = (2 * couples + 2) * atoms
+            features_ref[t, spare + atoms : spare + 2 * atoms] = features_ref[t, ahead, :]
+            features_ref[t, spare + 2 * atoms : spare + 3 * atoms] = features_ref[t, behind, :]
 
             def forward(chunk, carry):
                 start = pl.multiple_of(chunk * ROWS, ROWS)
                 base = pl.multiple_of(chunk * chunk_rows, chunk_rows)
                 for slot in range(2 * couples):
                     for g in range(groups):
-                        offset, radial = geometry(t, slot, pl.ds(start + g * GROUP, GROUP))
+                        where = pl.ds(start + g * GROUP, GROUP)
+                        offset, radial = pairs.geometry(t, slot, where)
                         for r in range(radials):
                             values = [radial[r]] + [radial[r] * offset[m] for m in range(3)]
                             for k in range(2):
@@ -341,127 +505,119 @@
                 rows = slice(chunk * chunk_rows, (chunk + 1) * chunk_rows)
                 seed_t_ref[t, chunk] = jnp.transpose(seed_ref[t, rows, :])
 
-            near_grad_ref[...] = jnp.zeros_like(near_grad_ref)
-            near_force_ref[...] = jnp.zeros_like(near_force_ref)
-            active = (live + 1) // 2
-            steps = active * chunks
-
-            def following(place):
-                couple, chunk = place
-                wrap = chunk + 1 >= chunks
-                couple = jnp.where(wrap, couple + 1, couple)
-                return jnp.where(couple < active, couple, couples), jnp.where(wrap, 0, chunk + 1)
-
-            def multiply(place, grad_ref):
-                couple, chunk = place
-                base = pl.multiple_of(chunk * chunk_rows, chunk_rows)
-                where = pl.ds(base, chunk_rows)
-                grad_ref[...] = lax.dot_general(
-                    seed_ref[t, where, :],
-                    features_ref[
-                        t, pl.ds(pl.multiple_of(couple * 2 * atoms, 2 * atoms), 2 * atoms), :
-                    ],
-                    NT,
-                    preferred_element_type=jnp.float32,
+            def distant():
+                first = near // 2
+                pairs.backward(
+                    t,
+                    chunks,
+                    first,
+                    (total_live + 1) // 2,
+                    jnp.where(near % 2 == 1, first, -1),
+                    couples + 1,
+                    couples,
+                    seed_ref,
+                    seed_t_ref,
+                    features_ref,
+                    basis_ref,
+                    near_grad_ref,
+                    near_force_ref,
+                    own_force_ref,
+                    grad_refs,
                 )
-                stored = jnp.minimum(couple, couples - 1)
-                basis = [basis_ref[t, 2 * stored + half, where, :] for half in range(2)]
-                near_grad_ref[couple] += jnp.dot(
-                    seed_t_ref[t, chunk],
-                    jnp.concatenate(basis, axis=1),
-                    preferred_element_type=jnp.float32,
-                )
-
-            def pull(place, grad_ref):
-                couple, chunk = place
-                start = pl.multiple_of(chunk * ROWS, ROWS)
-                pulled = [[None] * 3 for _ in range(2)]
-                for g in range(groups):
-                    rows = pl.ds(start + g * GROUP, GROUP)
-                    total = [None] * 3
-                    for half in range(2):
-                        lanes = slice(half * atoms, (half + 1) * atoms)
-                        offset, radial = geometry(t, 2 * couple + half, rows)
-                        direct = [None] * 3
-                        inner = None
-                        for r in range(radials):
-                            row = g * group_rows + 4 * r * GROUP
-                            grad = [
-                                grad_ref[row + m * GROUP : row + (m + 1) * GROUP, lanes]
-                                for m in range(4)
-                            ]
-                            along = grad[0]
-                            for m in range(3):
-                                along = along + grad[m + 1] * offset[m]
-                                part = radial[r] * grad[m + 1]
-                                direct[m] = part if r == 0 else direct[m] + part
-                            part = (radial[r] * (2.0 * rates[r])) * along
-                            inner = part if r == 0 else inner + part
-                        for m in range(3):
-                            force = direct[m] - offset[m] * inner
-                            total[m] = force if half == 0 else total[m] + force
-                            old = pulled[half][m]
-                            pulled[half][m] = force if g == 0 else old + force
-                    for m in range(3):
-                        own_force_ref[t, m, rows, :] += total[m]
-                for half in range(2):
-                    for m in range(3):
-                        near_force_ref[couple, half, m] += pulled[half][m]
-
-            zero = jnp.zeros((), jnp.int32)
-            first = (zero, zero)
-            places = (first, following(first))
-            multiply(places[0], grad_refs[0])
-            multiply(places[1], grad_refs[1])
-
-            def backward(k, places):
-                one, two = places
-                three = following(two)
-                four = following(three)
-                five = following(four)
-                six = following(five)
-                pull(one, grad_refs[0])
-                multiply(three, grad_refs[2])
-                pull(two, grad_refs[1])
-                multiply(four, grad_refs[3])
-                pull(three, grad_refs[2])
-                multiply(five, grad_refs[0])
-                pull(four, grad_refs[3])
-                multiply(six, grad_refs[1])
-                return five, six
-
-            lax.fori_loop(0, (steps + 3) // 4, backward, places)
-
+                for slot in range(1, slots):
+
+                    def give(slot=slot):
+                        tile = table_ref[t, slot]
+                        plane = lax.div(tile, line[1])
+                        tile = tile - line[0] * (plane + 1)
+                        pairs.give(slot, tile, near_grad_ref, near_force_ref, ghost_ref)
+
+                    pl.when((slot >= near) & (slot < total_live))(give)
+
+            pl.when(total_live > near)(distant)
+
+        pl.when(count > 0)(work)
+
+    starts = starts_of(ghost_refs)
+    for store in copies(
+        [
+            (ghost_ref.at[pl.ds(start, ref.shape[0])], ref)
+            for ref, start in zip(ghost_refs, starts)
+        ],
+        out_sems,
+    ):
+        store.wait()
+
+
+def line_kernel(
+    outs,
+    slots,
+    line,
+    counts_ref,
+    table_ref,
+    rates_ref,
+    own_ref,
+    other_ref,
+    features_ref,
+    basis_ref,
+    seed_ref,
+    seed_t_ref,
+    far_force_ref,
+    *refs,
+):
+    ghost_refs = refs[:outs]
+    near_grad_ref, near_force_ref, own_force_ref, ghost_ref, out_sems, *grad_refs = refs[outs:]
+    tiles, _, atoms, _ = own_ref.shape
+    channels = features_ref.shape[2]
+    couples = (slots + 1) // 2
+    pairs = Pairs(rates_ref, own_ref, other_ref, channels, atoms)
+    ghost_ref[...] = jnp.zeros_like(ghost_ref)
+    for t in range(tiles):
+        count = counts_ref[t]
+        chunks = (count + (ROWS - 1)) // ROWS
+        near = table_ref[t, slots]
+
+        def work(t=t, chunks=chunks, near=near):
+            own_force_ref[t] = far_force_ref[t]
+            pairs.backward(
+                t,
+                chunks,
+                jnp.zeros((), jnp.int32),
+                (near + 1) // 2,
+                jnp.where(near % 2 == 1, near // 2, -1),
+                couples + 2,
+                couples,
+                seed_ref,
+                seed_t_ref,
+                features_ref,
+                basis_ref,
+                near_grad_ref,
+                near_force_ref,
+                own_force_ref,
+                grad_refs,
+            )
             for slot in range(slots):
-                target = neighbours_ref[t, slot]
-
-                def give(slot=slot, target=target):
-                    tile = located(target)
-                    couple, half = divmod(slot, 2)
-                    lanes = slice(half * atoms, (half + 1) * atoms)
-                    ghost_ref[tile, :channels, :] += near_grad_ref[couple, :, lanes]
-                    for m in range(3):
-                        ghost_ref[tile, channels + m : channels + m + 1, :] -= jnp.sum(
-                            near_force_ref[couple, half, m], axis=0, keepdims=True
-                        )
-
-                pl.when(target >= 0)(give)
+
+                def give(slot=slot):
+                    tile = table_ref[t, slot]
+                    tile = tile - (line[1] - line[0]) * lax.div(tile, line[1])
+                    pairs.give(slot, tile, near_grad_ref, near_force_ref, ghost_ref)
+
+                pl.when(slot < near)(give)
             for m in range(3):
                 ghost_ref[t, channels + m : channels + m + 1, :] += jnp.sum(
                     jnp.transpose(own_force_ref[t, m]), axis=0, keepdims=True
                 )
 
         pl.when(count > 0)(work)
-
-    stores = [
-        pltpu.make_async_copy(
-            ghost_ref.at[pl.ds(starts[k], piece_refs[k].shape[0])], ghost_refs[k], out_sems.at[k]
-        )
-        for k in range(pieces)
-    ]
-    for store in stores:
-        store.start()
-    for store in stores:
+    starts = starts_of(ghost_refs)
+    for store in copies(
+        [
+            (ghost_ref.at[pl.ds(start, ref.shape[0])], ref)
+            for ref, start in zip(ghost_refs, starts)
+        ],
+        out_sems,
+    ):
         store.wait()
 
 
@@ -508,27 +664,30 @@
         name="pack",
     )(own_counts, features.reshape(tiles, atoms, channels), points)
     along_z = swap(packed, "gz")
-    own_counts, neighbours, rates, points, readout = pl.pallas_call(
-        side_kernel,
+    own_counts, table, rates, points, readout, local = pl.pallas_call(
+        functools.partial(side_kernel, sides),
         out_shape=[
             jax.ShapeDtypeStruct((tiles,), jnp.int32),
-            jax.ShapeDtypeStruct((tiles, slots), jnp.int32),
+            jax.ShapeDtypeStruct((tiles, slots + 2), jnp.int32),
             jax.ShapeDtypeStruct((radials,), jnp.float32),
             jax.ShapeDtypeStruct((3, tiles, atoms), jnp.float32),
             jax.ShapeDtypeStruct((1, channels), jnp.float32),
+            jax.ShapeDtypeStruct(packed.shape, packed.dtype),
         ],
-        in_specs=[smem, smem, smem, vmem, vmem],
-        out_specs=[smem, smem, smem, vmem, vmem],
+        in_specs=[smem, smem, smem, smem, vmem, vmem, vmem],
+        out_specs=[smem, smem, smem, vmem, vmem, vmem],
         compiler_params=small,
         name="sides",
     )(
+        jnp.stack([lax.axis_index(axis) % 2 for axis in ("gx", "gy", "gz")]),
         own_counts,
         neighbours.reshape(tiles, slots),
         radial_rates,
         points,
         readout.reshape(1, channels),
+        packed,
     )
-    (line,) = join([list(range(1 + len(along_z)))], packed, *along_z)
+    (line,) = join([list(range(1 + len(along_z)))], local, *along_z)
     lines = [line] + swap(line, "gy")
     pieces = [lines]
     for pairs in swaps("gx"):
@@ -541,47 +700,72 @@
     bases = 4 * radials
     chunks = atoms // ROWS
     ghost_rows = channels + EXTRA
-    position = jnp.stack([lax.axis_index(axis) % 2 for axis in ("gx", "gy", "gz")])
-    ghosts = pl.pallas_call(
-        functools.partial(main_kernel, len(flat), sides, slots),
-        out_shape=[
-            jax.ShapeDtypeStruct((piece.shape[0], ghost_rows, atoms), jnp.float32)
-            for piece in flat
-        ],
-        in_specs=[smem] * 4 + [vmem] * 3 + [hbm] * len(flat),
-        out_specs=[hbm] * len(flat),
+    counts_of = (line.shape[0], total // len(pieces))
+
+    def ghost_shapes(arrays):
+        return [
+            jax.ShapeDtypeStruct((array.shape[0], ghost_rows, atoms), jnp.float32)
+            for array in arrays
+        ]
+
+    far_shapes = ghost_shapes([piece for plane in pieces for piece in plane[1:]])
+    line_shapes = ghost_shapes([plane[0] for plane in pieces])
+    state_shapes = [
+        jax.ShapeDtypeStruct((tiles, 3, atoms, atoms), jnp.float32),
+        jax.ShapeDtypeStruct((tiles, 2 * couples + 2, 3, GROUP, atoms), jnp.float32),
+        jax.ShapeDtypeStruct((tiles, (2 * couples + 6) * atoms, channels), jnp.bfloat16),
+        jax.ShapeDtypeStruct((tiles, 2 * couples, bases * atoms, atoms), jnp.bfloat16),
+        jax.ShapeDtypeStruct((tiles, bases * atoms, channels), jnp.bfloat16),
+        jax.ShapeDtypeStruct((tiles, chunks, channels, bases * ROWS), jnp.bfloat16),
+        jax.ShapeDtypeStruct((tiles, 3, atoms, atoms), jnp.float32),
+    ]
+    sums = [
+        pltpu.VMEM((couples + 1, channels, 2 * atoms), jnp.float32),
+        pltpu.VMEM((couples + 1, 2, 3, GROUP, atoms), jnp.float32),
+    ]
+    buffers = [pltpu.VMEM((bases * ROWS, 2 * atoms), jnp.float32)] * 4
+    large = pltpu.CompilerParams(vmem_limit_bytes=LARGE)
+    results = pl.pallas_call(
+        functools.partial(main_kernel, len(flat), len(far_shapes), slots, counts_of),
+        out_shape=far_shapes + state_shapes,
+        in_specs=[smem] * 3 + [vmem] * 3 + [hbm] * len(flat),
+        out_specs=[hbm] * len(far_shapes) + [vmem] * len(state_shapes),
         scratch_shapes=[
             pltpu.VMEM((total, atoms + 16, channels), jnp.bfloat16),
+            pltpu.VMEM((tiles, bases * atoms, channels), jnp.float32),
+            *sums,
+            pltpu.VMEM(
+                (sum(shape.shape[0] for shape in far_shapes), ghost_rows, atoms), jnp.float32
+            ),
+            pltpu.SemaphoreType.DMA((len(flat),)),
+            pltpu.SemaphoreType.DMA((len(far_shapes),)),
+            *buffers,
+        ],
+        compiler_params=large,
+        name="pairs",
+    )(own_counts, table, rates, points, mix_weight, readout, *flat)
+    state = results[len(far_shapes) :]
+    line_ghosts = pl.pallas_call(
+        functools.partial(line_kernel, len(line_shapes), slots, counts_of),
+        out_shape=line_shapes,
+        in_specs=[smem] * 3 + [vmem] * len(state),
+        out_specs=[hbm] * len(line_shapes),
+        scratch_shapes=[
+            *sums,
             pltpu.VMEM((tiles, 3, atoms, atoms), jnp.float32),
-            pltpu.VMEM((tiles, 2 * couples + 2, 3, GROUP, atoms), jnp.float32),
-            pltpu.VMEM((tiles, (2 * couples + 2) * atoms, channels), jnp.bfloat16),
-            pltpu.VMEM((tiles, 2 * couples, bases * atoms, atoms), jnp.bfloat16),
-            pltpu.VMEM((tiles, bases * atoms, channels), jnp.float32),
-            pltpu.VMEM((tiles, bases * atoms, channels), jnp.bfloat16),
-            pltpu.VMEM((tiles, chunks, channels, bases * ROWS), jnp.bfloat16),
-            pltpu.VMEM((couples + 1, channels, 2 * atoms), jnp.float32),
-            pltpu.VMEM((couples + 1, 2, 3, GROUP, atoms), jnp.float32),
-            pltpu.VMEM((tiles, 3, atoms, atoms), jnp.float32),
-            pltpu.VMEM((total, ghost_rows, atoms), jnp.float32),
-            pltpu.SemaphoreType.DMA((len(flat),)),
-            pltpu.SemaphoreType.DMA((len(flat),)),
-        ]
-        + [pltpu.VMEM((bases * ROWS, 2 * atoms), jnp.float32)] * 4,
-        compiler_params=pltpu.CompilerParams(vmem_limit_bytes=LARGE),
-        name="pairs",
-    )(
-        position,
-        own_counts,
-        neighbours,
-        rates,
-        points,
-        mix_weight,
-        readout,
-        *flat,
-    )
-
-    width = len(pieces[0])
-    ghosts = [ghosts[k * width : (k + 1) * width] for k in range(len(pieces))]
+            pltpu.VMEM(
+                (sum(shape.shape[0] for shape in line_shapes), ghost_rows, atoms), jnp.float32
+            ),
+            pltpu.SemaphoreType.DMA((len(line_shapes),)),
+            *buffers,
+        ],
+        compiler_params=large,
+        name="lines",
+    )(own_counts, table, rates, *state)
+    width = len(pieces[0]) - 1
+    ghosts = [
+        [line_ghosts[k]] + list(results[k * width : (k + 1) * width]) for k in range(len(pieces))
+    ]
 
     def gather(k):
         arrays = [ghosts[0][k]]

time: 57.1 us -> 60.7 us (1.063)
  local copies, waits for them, and re-layouts: 1.6 us -> 5.16 us
  Pallas kernels: 20.6 us -> 23.6 us
  waiting for transfers between devices: 22.5 us -> 19.5 us
    unnamed x14, local copies, waits for them, and re-layouts: 1.6 us -> 5.16 us
    ppermute x4, waiting for transfers between devices: 9.52 us -> 6.24 us  [swap(): return [lax.ppermute(value, axis, pairs) for pairs in swaps(axis)]]
    pallas_call x2 -> x3, Pallas kernels: 17.4 us -> 20.4 us  [the longest x1 13.8 us: step(): pl.pallas_call(functools.partial(main_kernel, len(flat), len(far_shapes),...]
    ppermute x3, waiting for transfers between devices: 1.56 us -> 0.01 us  [gather(): arrays.append(lax.ppermute(plane[k], 'gx', pairs))]
    ppermute x2, waiting for transfers between devices: 0.01 us -> 1.47 us  [step(): lax.ppermute(piece, 'gx', pairs)]
  transfers between devices with their start and end apart: 14 -> 14, of which waited for: 8 -> 7; matrix products, arithmetic and copies ran while one was open for 0% -> 0% of each run, Pallas kernels for 2% -> 11%
where the time goes in v3:
time: 60.7 us; the launch traced here: 60.3 us
  Pallas kernels  23.6 us (39%)
  waiting for transfers between devices  19.5 us (32%)
  starting transfers between devices  10.9 us (18%)
  local copies, waits for them, and re-layouts  5.16 us (9%)
  between operations  0.87 us (1%)
    pallas_call x1, Pallas kernels, step(): pl.pallas_call(functools.partial(main_kernel, len(flat), len(far_shapes),...  13.8 us
    ppermute x4, waiting for transfers between devices, send(): lax.ppermute(value.astype(jnp.float16), axis, pairs).astype(jnp.float32)  11.8 us
    ppermute x4, starting transfers between devices, swap(): return [lax.ppermute(value, axis, pairs) for pairs in swaps(axis)]  7.49 us
    ppermute x4, waiting for transfers between devices, swap(): return [lax.ppermute(value, axis, pairs) for pairs in swaps(axis)]  6.24 us
    unnamed x14, local copies, waits for them, and re-layouts  5.16 us
    pallas_call x1, Pallas kernels, step(): pl.pallas_call(functools.partial(line_kernel, len(line_shapes), slots, co...  5 us
    ppermute x4, starting transfers between devices, send(): lax.ppermute(value.astype(jnp.float16), axis, pairs).astype(jnp.float32)  2.73 us
    pallas_call x1, Pallas kernels, step(): pl.pallas_call(functools.partial(side_kernel, sides), out_shape=[jax.Shap...  1.64 us
  transfers between devices with their start and end apart: 14, of which 7 were waited for; matrix products, arithmetic and copies ran while one was open for 0% of the time, Pallas kernels for 11%

profile of v3, /device:TPU:14, one launch (start us, length us, event | category | flops | bytes accessed | tf_op | source)
XLA Modules:
  0.0 60.3 jit_solution(6666275772440535790)
XLA Ops:
  0.6 1.5 %pack.1.packed_ref = bf16[2,144,128]{2,1,0:T(8,128)(2,1)} custom-call(s32[2]{0:T(128)} %bitcast.16, bf16[2,128,128]{2,1,0:T(8,128)(2,1)} %bitcast.20, f32[3,2,128]{2,1,0:T(2,128)} %bitcast.14), custom_call_target="tpu_custom_call" | custom-call | tf_op jit(solution)/shard_map/pack/pallas_call | solution.py:657
  2.2 0.7 %collective-permute-start.1 = (bf16[2,144,128]{2,1,0:T(8,128)(2,1)}, bf16[2,144,128]{2,1,0:T(8,128)(2,1)S(1)}, u32[]{:S(2)}, u32[]{:S(2)}) collective-permute-start(bf16[2,144,128]{2,1,0:T(8,128)(2,1)} %pack.1.packed_ref), channel_id=1, source_target_pairs={{1,2},{2,1},{5,6},{6,5},{9,10},{10,9},{13,14},{14,13},{17,18},{18,... | collective-permute-start | bytes 221192 | tf_op jit(solution)/shard_map/ppermute | solution.py:652
  2.8 3.3 %collective-permute-start = (bf16[2,144,128]{2,1,0:T(8,128)(2,1)}, bf16[2,144,128]{2,1,0:T(8,128)(2,1)S(1)}, u32[]{:S(2)}, u32[]{:S(2)}) collective-permute-start(bf16[2,144,128]{2,1,0:T(8,128)(2,1)} %pack.1.packed_ref), channel_id=1, source_target_pairs={{0,1},{2,3},{1,0},{3,2},{4,5},{6,7},{5,4},{7,6},{8,9},{10,11},{9,8... | collective-permute-start | bytes 221192 | tf_op jit(solution)/shard_map/ppermute | solution.py:652
  6.1 0.1 pad_add_fusion.axis_ref
  6.2 0.9 %copy-done = bf16[2,144,128]{2,1,0:T(8,128)(2,1)S(1)} copy-done((bf16[2,144,128]{2,1,0:T(8,128)(2,1)S(1)}, bf16[2,144,128]{2,1,0:T(8,128)(2,1)}, u32[]{:S(2)}) %copy-start) | copy-done | bytes 73752
  7.1 0.7 %copy-done.2 = f32[1,1,1,2,3,128]{5,3,4,2,1,0:T(2,128)S(1)} copy-done((f32[1,1,1,2,3,128]{5,3,4,2,1,0:T(2,128)S(1)}, f32[1,1,1,2,3,128]{5,3,4,2,1,0:T(2,128)}, u32[]{:S(2)}) %copy-start.2) | copy-done | bytes 3096
  7.7 0.7 %copy-done.3 = s32[1,1,1,2]{3,2,1,0:T(1,128)S(1)} copy-done((s32[1,1,1,2]{3,2,1,0:T(1,128)S(1)}, s32[1,1,1,2]{3,2,1,0:T(1,128)}, u32[]{:S(2)}) %copy-start.3) | copy-done | bytes 32
  8.4 0.7 %copy-done.4 = s32[1,1,1,2,8]{4,3,2,1,0:T(2,128)S(1)} copy-done((s32[1,1,1,2,8]{4,3,2,1,0:T(2,128)S(1)}, s32[1,1,1,2,8]{4,3,2,1,0:T(2,128)}, u32[]{:S(2)}) %copy-start.4) | copy-done | bytes 88
  9.1 0.7 %copy-done.5 = f32[4]{0:T(128)S(1)} copy-done((f32[4]{0:T(128)S(1)}, f32[4]{0:T(128)}, u32[]{:S(2)}) %copy-start.5) | copy-done | bytes 40
  9.7 0.7 %copy-done.6 = f32[128]{0:T(128)S(1)} copy-done((f32[128]{0:T(128)S(1)}, f32[128]{0:T(128)}, u32[]{:S(2)}) %copy-start.6) | copy-done | bytes 536
  10.4 1.6 %sides.1 = (s32[2]{0:T(128)S(1)}, s32[2,10]{1,0:T(2,128)S(1)}, f32[4]{0:T(128)S(1)}, f32[3,2,128]{2,1,0:T(2,128)S(1)}, f32[1,128]{1,0:T(1,128)S(1)}, /*index=5*/bf16[2,144,128]{2,1,0:T(8,128)(2,1)S(1)}) custom-call(s32[3]{0:T(128)S(1)} %pad_add_fusion.axis_ref, s32[2]{0:T(128)S(1)} %bitcast.17, s32[2,8]{1,0:T(2,128)S(1)} %bitcast.18, f32[4]{0:T(128)S(1)} %copy-done.5, ...), custom_call_target="tpu_custom_call" | custom-call | tf_op jit(solution)/shard_map/sides/pallas_call | solution.py:667
  12.1 3.5 %collective-permute-start.3 = (bf16[6,144,128]{2,1,0:T(8,128)(2,1)S(1)}, bf16[6,144,128]{2,1,0:T(8,128)(2,1)S(1)}, u32[]{:S(2)}, u32[]{:S(2)}) collective-permute-start(bf16[6,144,128]{2,1,0:T(8,128)(2,1)S(1)} %join.1.refs_0_), channel_id=1, source_target_pairs={{4,8},{8,4},{5,9},{9,5},{6,10},{10,6},{7,11},{11,7},{20,24},{24,20... | collective-permute-start | bytes 663560 | tf_op jit(solution)/shard_map/ppermute | solution.py:652
  15.7 0.1 collective-permute-start.4
  15.7 4.9 %collective-permute-done.3.refs_2_ = bf16[6,144,128]{2,1,0:T(8,128)(2,1)S(1)} collective-permute-done((bf16[6,144,128]{2,1,0:T(8,128)(2,1)S(1)}, bf16[6,144,128]{2,1,0:T(8,128)(2,1)S(1)}, u32[]{:S(2)}, u32[]{:S(2)}) %collective-permute-start.3) | collective-permute-done | bytes 221216 | tf_op jit(solution)/shard_map/ppermute | solution.py:652
  20.6 1.4 %collective-permute-done.2.refs_1_ = bf16[6,144,128]{2,1,0:T(8,128)(2,1)S(1)} collective-permute-done((bf16[6,144,128]{2,1,0:T(8,128)(2,1)S(1)}, bf16[6,144,128]{2,1,0:T(8,128)(2,1)S(1)}, u32[]{:S(2)}, u32[]{:S(2)}) %collective-permute-start.2) | collective-permute-done | bytes 221216 | tf_op jit(solution)/shard_map/ppermute | solution.py:652
  22.0 0.1 collective-permute-done.6.refs_5_
  22.1 1.4 %collective-permute-done.5.refs_4_ = bf16[6,144,128]{2,1,0:T(8,128)(2,1)S(1)} collective-permute-done((bf16[6,144,128]{2,1,0:T(8,128)(2,1)S(1)}, bf16[6,144,128]{2,1,0:T(8,128)(2,1)S(1)}, u32[]{:S(2)}, u32[]{:S(2)}) %collective-permute-start.5) | collective-permute-done | bytes 221216 | tf_op jit(solution)/shard_map/ppermute | solution.py:695
  23.5 0.9 %copy-done.1 = bf16[1024,128]{1,0:T(8,128)(2,1)S(1)} copy-done((bf16[1024,128]{1,0:T(8,128)(2,1)S(1)}, bf16[1024,128]{1,0:T(8,128)(2,1)}, u32[]{:S(2)}) %copy-start.1) | copy-done | bytes 262168
  24.4 13.8 %pairs.1 = (f32[6,136,128]{2,1,0:T(8,128)S(1)}, f32[6,136,128]{2,1,0:T(8,128)S(1)}, f32[6,136,128]{2,1,0:T(8,128)S(1)}, f32[6,136,128]{2,1,0:T(8,128)S(1)}, f32[...) custom-call(s32[2]{0:T(128)S(1)} %get-tuple-element.26.counts_ref, ...), custom_call_target="tpu_custom_call" | custom-call | tf_op jit(solution)/shard_map/pairs/pallas_call | solution.py:728
  38.2 0.1 collective-permute-start.8
  38.2 0.5 collective-permute-start.10
  38.7 5.0 %lines.1 = (f32[6,136,128]{2,1,0:T(8,128)S(1)}, f32[6,136,128]{2,1,0:T(8,128)S(1)}) custom-call(s32[2]{0:T(128)S(1)} %get-tuple-element.26.counts_ref, s32[2,10]{1,0:T(2,128)S(1)} %get-tuple-element.27.table_ref, f32[4]{0:T(128)S(1)} %get-tuple-element.28.rates_ref, f32[2,3,128,128]{3,2,1,0:T(8,128)S(1)} %get-tuple-element.32.own_ref, ...), custom_call_target="tpu_custom_call" | custom-call | tf_op jit(solution)/shard_map/lines/pallas_call | solution.py:748
  43.8 0.1 fold.3
  44.0 0.1 collective-permute-start.9
  44.1 0.1 fold.4
  44.2 1.9 %collective-permute-start.11 = (f16[6,136,128]{2,1,0:T(8,128)(2,1)S(1)}, f16[6,136,128]{2,1,0:T(8,128)(2,1)S(1)}, u32[]{:S(2)}, u32[]{:S(2)}) collective-permute-start(f16[6,136,128]{2,1,0:T(8,128)(2,1)S(1)} %convert_element_type.26), channel_id=1, source_target_pairs={{4,8},{8,4},{5,9},{9,5},{6,10},{10,6},{7,11},{11,7},{20,24},{24,20... | collective-permute-start | bytes 626696 | tf_op jit(solution)/shard_map/ppermute | solution.py:183
  46.1 5.5 %collective-permute-done.9 = f16[6,136,128]{2,1,0:T(8,128)(2,1)S(1)} collective-permute-done((f16[6,136,128]{2,1,0:T(8,128)(2,1)S(1)}, f16[6,136,128]{2,1,0:T(8,128)(2,1)S(1)}, u32[]{:S(2)}, u32[]{:S(2)}) %collective-permute-start.9) | collective-permute-done | bytes 208928 | tf_op jit(solution)/shard_map/ppermute | solution.py:183
  51.6 2.0 %collective-permute-done.11 = f16[6,136,128]{2,1,0:T(8,128)(2,1)S(1)} collective-permute-done((f16[6,136,128]{2,1,0:T(8,128)(2,1)S(1)}, f16[6,136,128]{2,1,0:T(8,128)(2,1)S(1)}, u32[]{:S(2)}, u32[]{:S(2)}) %collective-permute-start.11) | collective-permute-done | bytes 208928 | tf_op jit(solution)/shard_map/ppermute | solution.py:183
  53.7 0.2 fold.5
  53.9 0.7 %collective-permute-start.13 = (f16[2,136,128]{2,1,0:T(8,128)(2,1)S(1)}, f16[2,136,128]{2,1,0:T(8,128)(2,1)S(1)}, u32[]{:S(2)}, u32[]{:S(2)}) collective-permute-start(f16[2,136,128]{2,1,0:T(8,128)(2,1)S(1)} %convert_element_type.30), channel_id=1, source_target_pairs={{1,2},{2,1},{5,6},{6,5},{9,10},{10,9},{13,14},{14,13},{17,18},{18,... | collective-permute-start | bytes 208904 | tf_op jit(solution)/shard_map/ppermute | solution.py:183
  54.7 4.3 %collective-permute-done.12 = f16[2,136,128]{2,1,0:T(8,128)(2,1)S(1)} collective-permute-done((f16[2,136,128]{2,1,0:T(8,128)(2,1)S(1)}, f16[2,136,128]{2,1,0:T(8,128)(2,1)S(1)}, u32[]{:S(2)}, u32[]{:S(2)}) %collective-permute-start.12) | collective-permute-done | bytes 69664 | tf_op jit(solution)/shard_map/ppermute | solution.py:183
  59.0 1.3 %finish.1 = (f32[3,2,128]{2,1,0:T(2,128)}, f32[2,128,128]{2,1,0:T(8,128)}) custom-call(s32[2]{0:T(128)S(1)} %get-tuple-element.26.counts_ref, f32[2,136,128]{2,1,0:T(8,128)S(1)} %get-tuple-element.45.center_ref, f32[2,136,128]{2,1,0:T(8,128)S(1)} %convert_element_type.29.refs_0_, f32[2,136,128]{2,1,0:T(8,128)S(1)} %convert_element_type.31.refs_1_), custom_call_target="tpu_custom_call" | custom-call | tf_op jit(solution)/shard_map/finish/pallas_call | solution.py:788
  (28 shorter events, 0.4 us)
Async XLA Ops:
  2.2 9.9 %collective-permute-start.1 = (bf16[2,144,128]{2,1,0:T(8,128)(2,1)}, bf16[2,144,128]{2,1,0:T(8,128)(2,1)S(1)}, u32[]{:S(2)}, u32[]{:S(2)}) collective-permute-start(bf16[2,144,128]{2,1,0:T(8,128)(2,1)} %pack.1.packed_ref), channel_id=1, source_target_pairs={{1,2},{2,1},{5,6},{6,5},{9,10},{10,9},{13,14},{14,13},{17,18},{18,... | collective-permute-start | bytes 221192 | tf_op jit(solution)/shard_map/ppermute | solution.py:652
  2.8 9.2 %collective-permute-start = (bf16[2,144,128]{2,1,0:T(8,128)(2,1)}, bf16[2,144,128]{2,1,0:T(8,128)(2,1)S(1)}, u32[]{:S(2)}, u32[]{:S(2)}) collective-permute-start(bf16[2,144,128]{2,1,0:T(8,128)(2,1)} %pack.1.packed_ref), channel_id=1, source_target_pairs={{0,1},{2,3},{1,0},{3,2},{4,5},{6,7},{5,4},{7,6},{8,9},{10,11},{9,8... | collective-permute-start | bytes 221192 | tf_op jit(solution)/shard_map/ppermute | solution.py:652
  6.2 0.9 %copy-start = (bf16[2,144,128]{2,1,0:T(8,128)(2,1)S(1)}, bf16[2,144,128]{2,1,0:T(8,128)(2,1)}, u32[]{:S(2)}) copy-start(bf16[2,144,128]{2,1,0:T(8,128)(2,1)} %pack.1.packed_ref) | copy-start | bytes 221188
  7.1 0.7 %copy-start.2 = (f32[1,1,1,2,3,128]{5,3,4,2,1,0:T(2,128)S(1)}, f32[1,1,1,2,3,128]{5,3,4,2,1,0:T(2,128)}, u32[]{:S(2)}) copy-start(f32[1,1,1,2,3,128]{5,3,4,2,1,0:T(2,128)} %param.7) | copy-start | bytes 9220
  7.7 0.7 %copy-start.3 = (s32[1,1,1,2]{3,2,1,0:T(1,128)S(1)}, s32[1,1,1,2]{3,2,1,0:T(1,128)}, u32[]{:S(2)}) copy-start(s32[1,1,1,2]{3,2,1,0:T(1,128)} %param.9) | copy-start | bytes 28
  8.4 0.7 %copy-start.4 = (s32[1,1,1,2,8]{4,3,2,1,0:T(2,128)S(1)}, s32[1,1,1,2,8]{4,3,2,1,0:T(2,128)}, u32[]{:S(2)}) copy-start(s32[1,1,1,2,8]{4,3,2,1,0:T(2,128)} %param.10) | copy-start | bytes 196
  9.1 0.7 %copy-start.5 = (f32[4]{0:T(128)S(1)}, f32[4]{0:T(128)}, u32[]{:S(2)}) copy-start(f32[4]{0:T(128)} %rates_ref.1) | copy-start | bytes 52
  9.7 0.7 %copy-start.6 = (f32[128]{0:T(128)S(1)}, f32[128]{0:T(128)}, u32[]{:S(2)}) copy-start(f32[128]{0:T(128)} %param.12) | copy-start | bytes 1540
  12.1 8.5 %collective-permute-start.3 = (bf16[6,144,128]{2,1,0:T(8,128)(2,1)S(1)}, bf16[6,144,128]{2,1,0:T(8,128)(2,1)S(1)}, u32[]{:S(2)}, u32[]{:S(2)}) collective-permute-start(bf16[6,144,128]{2,1,0:T(8,128)(2,1)S(1)} %join.1.refs_0_), channel_id=1, source_target_pairs={{4,8},{8,4},{5,9},{9,5},{6,10},{10,6},{7,11},{11,7},{20,24},{24,20... | collective-permute-start | bytes 663560 | tf_op jit(solution)/shard_map/ppermute | solution.py:652
  15.6 6.4 %collective-permute-start.2 = (bf16[6,144,128]{2,1,0:T(8,128)(2,1)S(1)}, bf16[6,144,128]{2,1,0:T(8,128)(2,1)S(1)}, u32[]{:S(2)}, u32[]{:S(2)}) collective-permute-start(bf16[6,144,128]{2,1,0:T(8,128)(2,1)S(1)} %join.1.refs_0_), channel_id=1, source_target_pairs={{0,4},{8,12},{4,0},{12,8},{1,5},{9,13},{5,1},{13,9},{2,6},{10,14},... | collective-permute-start | bytes 663560 | tf_op jit(solution)/shard_map/ppermute | solution.py:652
  15.7 6.3 %collective-permute-start.4 = (bf16[6,144,128]{2,1,0:T(8,128)(2,1)S(1)}, bf16[6,144,128]{2,1,0:T(8,128)(2,1)S(1)}, u32[]{:S(2)}, u32[]{:S(2)}) collective-permute-start(bf16[6,144,128]{2,1,0:T(8,128)(2,1)S(1)} %join.1.refs_0_), channel_id=1, source_target_pairs={{0,16},{16,0},{1,17},{17,1},{2,18},{18,2},{3,19},{19,3},{4,20},{20... | collective-permute-start | bytes 663560 | tf_op jit(solution)/shard_map/ppermute | solution.py:694
  20.6 1.5 %collective-permute-start.6 = (bf16[6,144,128]{2,1,0:T(8,128)(2,1)S(1)}, bf16[6,144,128]{2,1,0:T(8,128)(2,1)S(1)}, u32[]{:S(2)}, u32[]{:S(2)}) collective-permute-start(bf16[6,144,128]{2,1,0:T(8,128)(2,1)S(1)} %collective-permute-done.3.refs_2_), channel_id=1, source_target_pairs={{0,16},{16,0},{1,17},{17,1},{2,18},{18,2},{3,19},{19,3},{4,20},{20... | collective-permute-start | bytes 663560 | tf_op jit(solution)/shard_map/ppermute | solution.py:695
  22.0 1.5 %collective-permute-start.5 = (bf16[6,144,128]{2,1,0:T(8,128)(2,1)S(1)}, bf16[6,144,128]{2,1,0:T(8,128)(2,1)S(1)}, u32[]{:S(2)}, u32[]{:S(2)}) collective-permute-start(bf16[6,144,128]{2,1,0:T(8,128)(2,1)S(1)} %collective-permute-done.2.refs_1_), channel_id=1, source_target_pairs={{0,16},{16,0},{1,17},{17,1},{2,18},{18,2},{3,19},{19,3},{4,20},{20... | collective-permute-start | bytes 663560 | tf_op jit(solution)/shard_map/ppermute | solution.py:695
  23.4 1.0 %copy-start.1 = (bf16[1024,128]{1,0:T(8,128)(2,1)S(1)}, bf16[1024,128]{1,0:T(8,128)(2,1)}, u32[]{:S(2)}) copy-start(bf16[1024,128]{1,0:T(8,128)(2,1)} %mixing_ref.1) | copy-start | bytes 786436
  38.2 5.7 %collective-permute-start.8 = (f32[6,136,128]{2,1,0:T(8,128)S(1)}, f32[6,136,128]{2,1,0:T(8,128)S(1)}, u32[]{:S(2)}, u32[]{:S(2)}) collective-permute-start(f32[6,136,128]{2,1,0:T(8,128)S(1)} %get-tuple-element.42), channel_id=1, source_target_pairs={{0,16},{16,0},{1,17},{17,1},{2,18},{18,2},{3,19},{19,3},{4,20},{20... | collective-permute-start | bytes 1253384 | tf_op jit(solution)/shard_map/ppermute | solution.py:773
  38.2 5.8 %collective-permute-start.10 = (f32[6,136,128]{2,1,0:T(8,128)S(1)}, f32[6,136,128]{2,1,0:T(8,128)S(1)}, u32[]{:S(2)}, u32[]{:S(2)}) collective-permute-start(f32[6,136,128]{2,1,0:T(8,128)S(1)} %get-tuple-element.44), channel_id=1, source_target_pairs={{0,16},{16,0},{1,17},{17,1},{2,18},{18,2},{3,19},{19,3},{4,20},{20... | collective-permute-start | bytes 1253384 | tf_op jit(solution)/shard_map/ppermute | solution.py:773
  43.7 9.9 %collective-permute-start.7 = (f32[6,136,128]{2,1,0:T(8,128)S(1)}, f32[6,136,128]{2,1,0:T(8,128)S(1)}, u32[]{:S(2)}, u32[]{:S(2)}) collective-permute-start(f32[6,136,128]{2,1,0:T(8,128)S(1)} %get-tuple-element.40), channel_id=1, source_target_pairs={{0,16},{16,0},{1,17},{17,1},{2,18},{18,2},{3,19},{19,3},{4,20},{20... | collective-permute-start | bytes 1253384 | tf_op jit(solution)/shard_map/ppermute | solution.py:773
  44.0 7.6 %collective-permute-start.9 = (f16[6,136,128]{2,1,0:T(8,128)(2,1)S(1)}, f16[6,136,128]{2,1,0:T(8,128)(2,1)S(1)}, u32[]{:S(2)}, u32[]{:S(2)}) collective-permute-start(f16[6,136,128]{2,1,0:T(8,128)(2,1)S(1)} %convert_element_type.24), channel_id=1, source_target_pairs={{0,4},{8,12},{4,0},{12,8},{1,5},{9,13},{5,1},{13,9},{2,6},{10,14},... | collective-permute-start | bytes 626696 | tf_op jit(solution)/shard_map/ppermute | solution.py:183
  44.2 9.5 %collective-permute-start.11 = (f16[6,136,128]{2,1,0:T(8,128)(2,1)S(1)}, f16[6,136,128]{2,1,0:T(8,128)(2,1)S(1)}, u32[]{:S(2)}, u32[]{:S(2)}) collective-permute-start(f16[6,136,128]{2,1,0:T(8,128)(2,1)S(1)} %convert_element_type.26), channel_id=1, source_target_pairs={{4,8},{8,4},{5,9},{9,5},{6,10},{10,6},{7,11},{11,7},{20,24},{24,20... | collective-permute-start | bytes 626696 | tf_op jit(solution)/shard_map/ppermute | solution.py:183
  53.9 0.8 %collective-permute-start.13 = (f16[2,136,128]{2,1,0:T(8,128)(2,1)S(1)}, f16[2,136,128]{2,1,0:T(8,128)(2,1)S(1)}, u32[]{:S(2)}, u32[]{:S(2)}) collective-permute-start(f16[2,136,128]{2,1,0:T(8,128)(2,1)S(1)} %convert_element_type.30), channel_id=1, source_target_pairs={{1,2},{2,1},{5,6},{6,5},{9,10},{10,9},{13,14},{14,13},{17,18},{18,... | collective-permute-start | bytes 208904 | tf_op jit(solution)/shard_map/ppermute | solution.py:183
  54.6 4.4 %collective-permute-start.12 = (f16[2,136,128]{2,1,0:T(8,128)(2,1)S(1)}, f16[2,136,128]{2,1,0:T(8,128)(2,1)S(1)}, u32[]{:S(2)}, u32[]{:S(2)}) collective-permute-start(f16[2,136,128]{2,1,0:T(8,128)(2,1)S(1)} %convert_element_type.28), channel_id=1, source_target_pairs={{0,1},{2,3},{1,0},{3,2},{4,5},{6,7},{5,4},{7,6},{8,9},{10,11},{9,8... | collective-permute-start | bytes 208904 | tf_op jit(solution)/shard_map/ppermute | solution.py:183

commit v4 on v3

--- a/solution.py
+++ b/solution.py
@@ -55,15 +55,9 @@
     axis_ref,
     counts_ref,
     neighbours_ref,
-    rates_ref,
-    points_ref,
-    readout_ref,
     packed_ref,
     out_counts_ref,
     out_table_ref,
-    out_rates_ref,
-    out_points_ref,
-    out_readout_ref,
     out_packed_ref,
 ):
     tiles, slots = neighbours_ref.shape
@@ -92,11 +86,15 @@
             pl.when(live)(put)
             at_near = at_near + jnp.where(line, 1, 0)
             at_far = at_far + jnp.where(live & ~line, 1, 0)
+    out_packed_ref[...] = packed_ref[...]
+
+
+def stage_kernel(rates_ref, points_ref, readout_ref, mixing_ref, *out_refs):
     for r in range(rates_ref.shape[0]):
-        out_rates_ref[r] = rates_ref[r]
-    out_points_ref[...] = points_ref[...]
-    out_readout_ref[...] = readout_ref[...]
-    out_packed_ref[...] = packed_ref[...]
+        out_refs[0][r] = rates_ref[r]
+    out_refs[1][...] = points_ref[...]
+    out_refs[2][...] = readout_ref[...]
+    out_refs[3][...] = mixing_ref[...]
 
 
 def join_kernel(groups, *refs):
@@ -200,10 +198,9 @@
 
     def backward(
         self,
-        t,
         chunks,
-        first,
-        last,
+        firsts,
+        lasts,
         masked,
         block,
         couples,
@@ -219,19 +216,42 @@
         atoms, group_rows, chunk_rows = self.atoms, self.group_rows, self.chunk_rows
         near_grad_ref[...] = jnp.zeros_like(near_grad_ref)
         near_force_ref[...] = jnp.zeros_like(near_force_ref)
-        steps = (last - first) * chunks
+        tiles = len(chunks)
+        lengths = [(lasts[k] - firsts[k]) * chunks[k] for k in range(tiles)]
+        steps = sum(lengths)
+        zero = jnp.zeros((), jnp.int32)
+
+        def of(values, t):
+            result = values[-1]
+            for k in reversed(range(tiles - 1)):
+                result = jnp.where(t == k, values[k], result)
+            return result
+
+        def enter(start):
+            t = jnp.full((), tiles, jnp.int32)
+            for k in reversed(range(tiles)):
+                t = jnp.where((start <= k) & (lengths[k] > 0), k, t)
+            found = t < tiles
+            t = jnp.minimum(t, tiles - 1)
+            return t, jnp.where(found, of(firsts, t), couples), zero
 
         def following(place):
-            couple, chunk = place
-            wrap = chunk + 1 >= chunks
-            couple = jnp.where(wrap, couple + 1, couple)
-            return jnp.where(couple < last, couple, couples), jnp.where(wrap, 0, chunk + 1)
+            t, couple, chunk = place
+            wrap = chunk + 1 >= of(chunks, t)
+            end = wrap & (couple + 1 >= of(lasts, t))
+            tile, start, _ = enter(t + 1)
+            inside = jnp.where(wrap, couple + 1, couple)
+            return (
+                jnp.where(end, tile, t),
+                jnp.where(end, start, inside),
+                jnp.where(wrap, 0, chunk + 1),
+            )
 
         def multiply(place, grad_ref):
-            couple, chunk = place
+            t, couple, chunk = place
             base = pl.multiple_of(chunk * chunk_rows, chunk_rows)
             where = pl.ds(base, chunk_rows)
-            spot = jnp.where(couple == masked, block, couple)
+            spot = jnp.where(couple == of(masked, t), block, couple)
             spot = pl.multiple_of(spot * 2 * atoms, 2 * atoms)
             grad_ref[...] = lax.dot_general(
                 seed_ref[t, where, :],
@@ -241,14 +261,14 @@
             )
             stored = jnp.minimum(couple, couples - 1)
             basis = [basis_ref[t, 2 * stored + half, where, :] for half in range(2)]
-            near_grad_ref[couple] += jnp.dot(
+            near_grad_ref[t * (couples + 1) + couple] += jnp.dot(
                 seed_t_ref[t, chunk],
                 jnp.concatenate(basis, axis=1),
                 preferred_element_type=jnp.float32,
             )
 
         def pull(place, grad_ref):
-            couple, chunk = place
+            t, couple, chunk = place
             start = pl.multiple_of(chunk * ROWS, ROWS)
             pulled = [[None] * 3 for _ in range(2)]
             for g in range(self.groups):
@@ -281,9 +301,9 @@
                     own_force_ref[t, m, rows, :] += total[m]
             for half in range(2):
                 for m in range(3):
-                    near_force_ref[couple, half, m] += pulled[half][m]
-
-        one = (first, jnp.zeros((), jnp.int32))
+                    near_force_ref[t * (couples + 1) + couple, half, m] += pulled[half][m]
+
+        one = enter(zero)
         two = following(one)
         multiply(one, grad_refs[0])
         multiply(two, grad_refs[1])
@@ -306,14 +326,13 @@
 
         lax.fori_loop(0, (steps + 3) // 4, loop, (one, two))
 
-    def give(self, slot, tile, near_grad_ref, near_force_ref, ghost_ref):
-        couple, half = divmod(slot, 2)
+    def give(self, row, half, tile, near_grad_ref, near_force_ref, ghost_ref):
         channels, atoms = self.channels, self.atoms
         lanes = slice(half * atoms, (half + 1) * atoms)
-        ghost_ref[tile, :channels, :] += near_grad_ref[couple, :, lanes]
+        ghost_ref[tile, :channels, :] += near_grad_ref[row, :, lanes]
         for m in range(3):
             ghost_ref[tile, channels + m : channels + m + 1, :] -= jnp.sum(
-                near_force_ref[couple, half, m], axis=0, keepdims=True
+                near_force_ref[row, half, m], axis=0, keepdims=True
             )
 
 
@@ -396,9 +415,8 @@
         count = counts_ref[t]
         chunks = (count + (ROWS - 1)) // ROWS
         near = table_ref[t, slots]
-        total_live = table_ref[t, slots + 1]
-
-        def work(t=t, count=count, chunks=chunks, near=near, total_live=total_live):
+
+        def work(t=t, count=count, chunks=chunks, near=near):
             for k in range(slots):
                 tile = table_ref[t, k]
                 live = tile >= 0
@@ -505,38 +523,48 @@
                 rows = slice(chunk * chunk_rows, (chunk + 1) * chunk_rows)
                 seed_t_ref[t, chunk] = jnp.transpose(seed_ref[t, rows, :])
 
-            def distant():
-                first = near // 2
-                pairs.backward(
-                    t,
-                    chunks,
-                    first,
-                    (total_live + 1) // 2,
-                    jnp.where(near % 2 == 1, first, -1),
-                    couples + 1,
-                    couples,
-                    seed_ref,
-                    seed_t_ref,
-                    features_ref,
-                    basis_ref,
-                    near_grad_ref,
-                    near_force_ref,
-                    own_force_ref,
-                    grad_refs,
-                )
-                for slot in range(1, slots):
-
-                    def give(slot=slot):
-                        tile = table_ref[t, slot]
-                        plane = lax.div(tile, line[1])
-                        tile = tile - line[0] * (plane + 1)
-                        pairs.give(slot, tile, near_grad_ref, near_force_ref, ghost_ref)
-
-                    pl.when((slot >= near) & (slot < total_live))(give)
-
-            pl.when(total_live > near)(distant)
-
         pl.when(count > 0)(work)
+
+    counts = [counts_ref[t] for t in range(tiles)]
+    nears = [table_ref[t, slots] for t in range(tiles)]
+    totals = [table_ref[t, slots + 1] for t in range(tiles)]
+    active = [(counts[t] > 0) & (totals[t] > nears[t]) for t in range(tiles)]
+    firsts = [nears[t] // 2 for t in range(tiles)]
+    lasts = [jnp.where(active[t], (totals[t] + 1) // 2, firsts[t]) for t in range(tiles)]
+
+    def distant():
+        pairs.backward(
+            [(count + (ROWS - 1)) // ROWS for count in counts],
+            firsts,
+            lasts,
+            [jnp.where(nears[t] % 2 == 1, firsts[t], -1) for t in range(tiles)],
+            couples + 1,
+            couples,
+            seed_ref,
+            seed_t_ref,
+            features_ref,
+            basis_ref,
+            near_grad_ref,
+            near_force_ref,
+            own_force_ref,
+            grad_refs,
+        )
+        for t in range(tiles):
+            for slot in range(1, slots):
+
+                def give(t=t, slot=slot):
+                    tile = table_ref[t, slot]
+                    plane = lax.div(tile, line[1])
+                    tile = tile - line[0] * (plane + 1)
+                    row = t * (couples + 1) + slot // 2
+                    pairs.give(row, slot % 2, tile, near_grad_ref, near_force_ref, ghost_ref)
+
+                pl.when(active[t] & (slot >= nears[t]) & (slot < totals[t]))(give)
+
+    some = active[0]
+    for t in range(1, tiles):
+        some = some | active[t]
+    pl.when(some)(distant)
 
     starts = starts_of(ghost_refs)
     for store in copies(
@@ -572,44 +600,51 @@
     couples = (slots + 1) // 2
     pairs = Pairs(rates_ref, own_ref, other_ref, channels, atoms)
     ghost_ref[...] = jnp.zeros_like(ghost_ref)
-    for t in range(tiles):
-        count = counts_ref[t]
-        chunks = (count + (ROWS - 1)) // ROWS
-        near = table_ref[t, slots]
-
-        def work(t=t, chunks=chunks, near=near):
-            own_force_ref[t] = far_force_ref[t]
-            pairs.backward(
-                t,
-                chunks,
-                jnp.zeros((), jnp.int32),
-                (near + 1) // 2,
-                jnp.where(near % 2 == 1, near // 2, -1),
-                couples + 2,
-                couples,
-                seed_ref,
-                seed_t_ref,
-                features_ref,
-                basis_ref,
-                near_grad_ref,
-                near_force_ref,
-                own_force_ref,
-                grad_refs,
-            )
+    own_force_ref[...] = far_force_ref[...]
+    counts = [counts_ref[t] for t in range(tiles)]
+    nears = [table_ref[t, slots] for t in range(tiles)]
+    zero = jnp.zeros((), jnp.int32)
+
+    def linear():
+        pairs.backward(
+            [(count + (ROWS - 1)) // ROWS for count in counts],
+            [zero] * tiles,
+            [jnp.where(counts[t] > 0, (nears[t] + 1) // 2, 0) for t in range(tiles)],
+            [jnp.where(nears[t] % 2 == 1, nears[t] // 2, -1) for t in range(tiles)],
+            couples + 2,
+            couples,
+            seed_ref,
+            seed_t_ref,
+            features_ref,
+            basis_ref,
+            near_grad_ref,
+            near_force_ref,
+            own_force_ref,
+            grad_refs,
+        )
+        for t in range(tiles):
             for slot in range(slots):
 
-                def give(slot=slot):
+                def give(t=t, slot=slot):
                     tile = table_ref[t, slot]
                     tile = tile - (line[1] - line[0]) * lax.div(tile, line[1])
-                    pairs.give(slot, tile, near_grad_ref, near_force_ref, ghost_ref)
-
-                pl.when(slot < near)(give)
-            for m in range(3):
-                ghost_ref[t, channels + m : channels + m + 1, :] += jnp.sum(
-                    jnp.transpose(own_force_ref[t, m]), axis=0, keepdims=True
-                )
-
-        pl.when(count > 0)(work)
+                    row = t * (couples + 1) + slot // 2
+                    pairs.give(row, slot % 2, tile, near_grad_ref, near_force_ref, ghost_ref)
+
+                pl.when((counts[t] > 0) & (slot < nears[t]))(give)
+
+            def own(t=t):
+                for m in range(3):
+                    ghost_ref[t, channels + m : channels + m + 1, :] += jnp.sum(
+                        jnp.transpose(own_force_ref[t, m]), axis=0, keepdims=True
+                    )
+
+            pl.when(counts[t] > 0)(own)
+
+    some = counts[0] > 0
+    for t in range(1, tiles):
+        some = some | (counts[t] > 0)
+    pl.when(some)(linear)
     starts = starts_of(ghost_refs)
     for store in copies(
         [
@@ -664,31 +699,38 @@
         name="pack",
     )(own_counts, features.reshape(tiles, atoms, channels), points)
     along_z = swap(packed, "gz")
-    own_counts, table, rates, points, readout, local = pl.pallas_call(
+    own_counts, table, local = pl.pallas_call(
         functools.partial(side_kernel, sides),
         out_shape=[
             jax.ShapeDtypeStruct((tiles,), jnp.int32),
             jax.ShapeDtypeStruct((tiles, slots + 2), jnp.int32),
-            jax.ShapeDtypeStruct((radials,), jnp.float32),
-            jax.ShapeDtypeStruct((3, tiles, atoms), jnp.float32),
-            jax.ShapeDtypeStruct((1, channels), jnp.float32),
             jax.ShapeDtypeStruct(packed.shape, packed.dtype),
         ],
-        in_specs=[smem, smem, smem, smem, vmem, vmem, vmem],
-        out_specs=[smem, smem, smem, vmem, vmem, vmem],
+        in_specs=[smem, smem, smem, vmem],
+        out_specs=[smem, smem, vmem],
         compiler_params=small,
         name="sides",
     )(
         jnp.stack([lax.axis_index(axis) % 2 for axis in ("gx", "gy", "gz")]),
         own_counts,
         neighbours.reshape(tiles, slots),
-        radial_rates,
-        points,
-        readout.reshape(1, channels),
         packed,
     )
     (line,) = join([list(range(1 + len(along_z)))], local, *along_z)
     lines = [line] + swap(line, "gy")
+    rates, points, readout, mix_weight = pl.pallas_call(
+        stage_kernel,
+        out_shape=[
+            jax.ShapeDtypeStruct((radials,), jnp.float32),
+            jax.ShapeDtypeStruct((3, tiles, atoms), jnp.float32),
+            jax.ShapeDtypeStruct((1, channels), jnp.float32),
+            jax.ShapeDtypeStruct(mix_weight.shape, mix_weight.dtype),
+        ],
+        in_specs=[smem, vmem, vmem, vmem],
+        out_specs=[smem, vmem, vmem, vmem],
+        compiler_params=small,
+        name="stage",
+    )(radial_rates, points, readout.reshape(1, channels), mix_weight)
     pieces = [lines]
     for pairs in swaps("gx"):
         plane = [lax.ppermute(line, "gx", pairs)]
@@ -720,8 +762,8 @@
         jax.ShapeDtypeStruct((tiles, 3, atoms, atoms), jnp.float32),
     ]
     sums = [
-        pltpu.VMEM((couples + 1, channels, 2 * atoms), jnp.float32),
-        pltpu.VMEM((couples + 1, 2, 3, GROUP, atoms), jnp.float32),
+        pltpu.VMEM((tiles * (couples + 1), channels, 2 * atoms), jnp.float32),
+        pltpu.VMEM((tiles * (couples + 1), 2, 3, GROUP, atoms), jnp.float32),
     ]
     buffers = [pltpu.VMEM((bases * ROWS, 2 * atoms), jnp.float32)] * 4
     large = pltpu.CompilerParams(vmem_limit_bytes=LARGE)

time: 60.7 us -> 59.7 us (0.984)
  waiting for transfers between devices: 19.5 us -> 18 us
    ppermute x2, waiting for transfers between devices: 1.47 us -> 0.01 us  [step(): lax.ppermute(piece, 'gx', pairs)]
    pallas_call x0 -> x1, Pallas kernels: none -> 1.14 us  [step(): pl.pallas_call(stage_kernel, out_shape=[jax.ShapeDtypeStruct((radials,),...]
  transfers between devices with their start and end apart: 14 -> 14, of which waited for: 7 -> 5; matrix products, arithmetic and copies ran while one was open for 0% -> 0% of each run, Pallas kernels for 11% -> 13%
where the time goes in v4:
time: 59.7 us; the launch traced here: 59.3 us
  Pallas kernels  24.1 us (40%)
  waiting for transfers between devices  18 us (30%)
  starting transfers between devices  10.9 us (18%)
  local copies, waits for them, and re-layouts  5.16 us (9%)
  between operations  0.9 us (2%)
    pallas_call x1, Pallas kernels, step(): pl.pallas_call(functools.partial(main_kernel, len(flat), len(far_shapes),...  13.4 us
    ppermute x4, waiting for transfers between devices, send(): lax.ppermute(value.astype(jnp.float16), axis, pairs).astype(jnp.float32)  11.8 us
    ppermute x4, starting transfers between devices, swap(): return [lax.ppermute(value, axis, pairs) for pairs in swaps(axis)]  7.49 us
    ppermute x4, waiting for transfers between devices, swap(): return [lax.ppermute(value, axis, pairs) for pairs in swaps(axis)]  6.24 us
    unnamed x14, local copies, waits for them, and re-layouts  5.16 us
    pallas_call x1, Pallas kernels, step(): pl.pallas_call(functools.partial(line_kernel, len(line_shapes), slots, co...  4.69 us
    ppermute x4, starting transfers between devices, send(): lax.ppermute(value.astype(jnp.float16), axis, pairs).astype(jnp.float32)  2.73 us
    pallas_call x1, Pallas kernels, step(): pl.pallas_call(functools.partial(side_kernel, sides), out_shape=[jax.Shap...  1.61 us
  transfers between devices with their start and end apart: 14, of which 5 were waited for; matrix products, arithmetic and copies ran while one was open for 0% of the time, Pallas kernels for 13%

profile of v4, /device:TPU:14, one launch (start us, length us, event | category | flops | bytes accessed | tf_op | source)
XLA Modules:
  0.0 59.3 jit_solution(12212602649703694375)
XLA Ops:
  0.6 1.5 %pack.1.packed_ref = bf16[2,144,128]{2,1,0:T(8,128)(2,1)} custom-call(s32[2]{0:T(128)} %bitcast.16, bf16[2,128,128]{2,1,0:T(8,128)(2,1)} %bitcast.20, f32[3,2,128]{2,1,0:T(2,128)} %bitcast.14), custom_call_target="tpu_custom_call" | custom-call | tf_op jit(solution)/shard_map/pack/pallas_call | solution.py:692
  2.2 0.7 %collective-permute-start.1 = (bf16[2,144,128]{2,1,0:T(8,128)(2,1)}, bf16[2,144,128]{2,1,0:T(8,128)(2,1)S(1)}, u32[]{:S(2)}, u32[]{:S(2)}) collective-permute-start(bf16[2,144,128]{2,1,0:T(8,128)(2,1)} %pack.1.packed_ref), channel_id=1, source_target_pairs={{1,2},{2,1},{5,6},{6,5},{9,10},{10,9},{13,14},{14,13},{17,18},{18,... | collective-permute-start | bytes 221192 | tf_op jit(solution)/shard_map/ppermute | solution.py:687
  2.8 3.3 %collective-permute-start = (bf16[2,144,128]{2,1,0:T(8,128)(2,1)}, bf16[2,144,128]{2,1,0:T(8,128)(2,1)S(1)}, u32[]{:S(2)}, u32[]{:S(2)}) collective-permute-start(bf16[2,144,128]{2,1,0:T(8,128)(2,1)} %pack.1.packed_ref), channel_id=1, source_target_pairs={{0,1},{2,3},{1,0},{3,2},{4,5},{6,7},{5,4},{7,6},{8,9},{10,11},{9,8... | collective-permute-start | bytes 221192 | tf_op jit(solution)/shard_map/ppermute | solution.py:687
  6.1 0.1 pad_add_fusion.axis_ref
  6.2 0.9 %copy-done = bf16[2,144,128]{2,1,0:T(8,128)(2,1)S(1)} copy-done((bf16[2,144,128]{2,1,0:T(8,128)(2,1)S(1)}, bf16[2,144,128]{2,1,0:T(8,128)(2,1)}, u32[]{:S(2)}) %copy-start) | copy-done | bytes 73752
  7.1 0.7 %copy-done.3 = s32[1,1,1,2]{3,2,1,0:T(1,128)S(1)} copy-done((s32[1,1,1,2]{3,2,1,0:T(1,128)S(1)}, s32[1,1,1,2]{3,2,1,0:T(1,128)}, u32[]{:S(2)}) %copy-start.3) | copy-done | bytes 32
  7.7 0.7 %copy-done.4 = s32[1,1,1,2,8]{4,3,2,1,0:T(2,128)S(1)} copy-done((s32[1,1,1,2,8]{4,3,2,1,0:T(2,128)S(1)}, s32[1,1,1,2,8]{4,3,2,1,0:T(2,128)}, u32[]{:S(2)}) %copy-start.4) | copy-done | bytes 88
  8.4 1.6 %sides.1 = (s32[2]{0:T(128)S(1)}, s32[2,10]{1,0:T(2,128)S(1)}, bf16[2,144,128]{2,1,0:T(8,128)(2,1)S(1)}) custom-call(s32[3]{0:T(128)S(1)} %pad_add_fusion.axis_ref, s32[2]{0:T(128)S(1)} %bitcast.17, s32[2,8]{1,0:T(2,128)S(1)} %bitcast.18, bf16[2,144,128]{2,1,0:T(8,128)(2,1)S(1)} %copy-done), custom_call_target="tpu_custom_call" | custom-call | tf_op jit(solution)/shard_map/sides/pallas_call | solution.py:702
  10.1 3.5 %collective-permute-start.3 = (bf16[6,144,128]{2,1,0:T(8,128)(2,1)S(1)}, bf16[6,144,128]{2,1,0:T(8,128)(2,1)S(1)}, u32[]{:S(2)}, u32[]{:S(2)}) collective-permute-start(bf16[6,144,128]{2,1,0:T(8,128)(2,1)S(1)} %join.1.refs_0_), channel_id=1, source_target_pairs={{4,8},{8,4},{5,9},{9,5},{6,10},{10,6},{7,11},{11,7},{20,24},{24,20... | collective-permute-start | bytes 663560 | tf_op jit(solution)/shard_map/ppermute | solution.py:687
  13.6 0.1 collective-permute-start.4
  13.7 4.9 %collective-permute-done.3.refs_2_ = bf16[6,144,128]{2,1,0:T(8,128)(2,1)S(1)} collective-permute-done((bf16[6,144,128]{2,1,0:T(8,128)(2,1)S(1)}, bf16[6,144,128]{2,1,0:T(8,128)(2,1)S(1)}, u32[]{:S(2)}, u32[]{:S(2)}) %collective-permute-start.3) | collective-permute-done | bytes 221216 | tf_op jit(solution)/shard_map/ppermute | solution.py:687
  18.6 1.4 %collective-permute-done.2.refs_1_ = bf16[6,144,128]{2,1,0:T(8,128)(2,1)S(1)} collective-permute-done((bf16[6,144,128]{2,1,0:T(8,128)(2,1)S(1)}, bf16[6,144,128]{2,1,0:T(8,128)(2,1)S(1)}, u32[]{:S(2)}, u32[]{:S(2)}) %collective-permute-start.2) | collective-permute-done | bytes 221216 | tf_op jit(solution)/shard_map/ppermute | solution.py:687
  19.9 0.9 %copy-done.1 = bf16[1024,128]{1,0:T(8,128)(2,1)S(1)} copy-done((bf16[1024,128]{1,0:T(8,128)(2,1)S(1)}, bf16[1024,128]{1,0:T(8,128)(2,1)}, u32[]{:S(2)}) %copy-start.1) | copy-done | bytes 262168
  20.9 0.7 %copy-done.2 = f32[1,1,1,2,3,128]{5,3,4,2,1,0:T(2,128)S(1)} copy-done((f32[1,1,1,2,3,128]{5,3,4,2,1,0:T(2,128)S(1)}, f32[1,1,1,2,3,128]{5,3,4,2,1,0:T(2,128)}, u32[]{:S(2)}) %copy-start.2) | copy-done | bytes 3096
  21.6 0.7 %copy-done.5 = f32[4]{0:T(128)S(1)} copy-done((f32[4]{0:T(128)S(1)}, f32[4]{0:T(128)}, u32[]{:S(2)}) %copy-start.5) | copy-done | bytes 40
  22.2 0.7 %copy-done.6 = f32[128]{0:T(128)S(1)} copy-done((f32[128]{0:T(128)S(1)}, f32[128]{0:T(128)}, u32[]{:S(2)}) %copy-start.6) | copy-done | bytes 536
  22.9 1.1 %stage.1 = (f32[4]{0:T(128)S(1)}, f32[3,2,128]{2,1,0:T(2,128)S(1)}, f32[1,128]{1,0:T(1,128)S(1)}, bf16[1024,128]{1,0:T(8,128)(2,1)S(1)}) custom-call(f32[4]{0:T(128)S(1)} %copy-done.5, f32[3,2,128]{2,1,0:T(2,128)S(1)} %bitcast.15, f32[1,128]{1,0:T(1,128)S(1)} %bitcast.19, bf16[1024,128]{1,0:T(8,128)(2,1)S(1)} %copy-done.1), custom_call_target="tpu_custom_call" | custom-call | tf_op jit(solution)/shard_map/stage/pallas_call | solution.py:721
  24.1 13.4 %pairs.1 = (f32[6,136,128]{2,1,0:T(8,128)S(1)}, f32[6,136,128]{2,1,0:T(8,128)S(1)}, f32[6,136,128]{2,1,0:T(8,128)S(1)}, f32[6,136,128]{2,1,0:T(8,128)S(1)}, f32[...) custom-call(s32[2]{0:T(128)S(1)} %get-tuple-element.27.counts_ref, ...), custom_call_target="tpu_custom_call" | custom-call | tf_op jit(solution)/shard_map/pairs/pallas_call | solution.py:770
  37.6 0.5 collective-permute-start.10
  38.1 4.7 %lines.1 = (f32[6,136,128]{2,1,0:T(8,128)S(1)}, f32[6,136,128]{2,1,0:T(8,128)S(1)}) custom-call(s32[2]{0:T(128)S(1)} %get-tuple-element.27.counts_ref, s32[2,10]{1,0:T(2,128)S(1)} %get-tuple-element.28.table_ref, f32[4]{0:T(128)S(1)} %get-tuple-element.29.rates_ref, f32[2,3,128,128]{3,2,1,0:T(8,128)S(1)} %get-tuple-element.34.own_ref, ...), custom_call_target="tpu_custom_call" | custom-call | tf_op jit(solution)/shard_map/lines/pallas_call | solution.py:790
  42.8 0.1 collective-permute-start.7
  42.9 0.1 fold.3
  43.0 0.1 collective-permute-start.9
  43.1 0.1 fold.4
  43.3 1.9 %collective-permute-start.11 = (f16[6,136,128]{2,1,0:T(8,128)(2,1)S(1)}, f16[6,136,128]{2,1,0:T(8,128)(2,1)S(1)}, u32[]{:S(2)}, u32[]{:S(2)}) collective-permute-start(f16[6,136,128]{2,1,0:T(8,128)(2,1)S(1)} %convert_element_type.26), channel_id=1, source_target_pairs={{4,8},{8,4},{5,9},{9,5},{6,10},{10,6},{7,11},{11,7},{20,24},{24,20... | collective-permute-start | bytes 626696 | tf_op jit(solution)/shard_map/ppermute | solution.py:181
  45.2 5.5 %collective-permute-done.9 = f16[6,136,128]{2,1,0:T(8,128)(2,1)S(1)} collective-permute-done((f16[6,136,128]{2,1,0:T(8,128)(2,1)S(1)}, f16[6,136,128]{2,1,0:T(8,128)(2,1)S(1)}, u32[]{:S(2)}, u32[]{:S(2)}) %collective-permute-start.9) | collective-permute-done | bytes 208928 | tf_op jit(solution)/shard_map/ppermute | solution.py:181
  50.7 2.0 %collective-permute-done.11 = f16[6,136,128]{2,1,0:T(8,128)(2,1)S(1)} collective-permute-done((f16[6,136,128]{2,1,0:T(8,128)(2,1)S(1)}, f16[6,136,128]{2,1,0:T(8,128)(2,1)S(1)}, u32[]{:S(2)}, u32[]{:S(2)}) %collective-permute-start.11) | collective-permute-done | bytes 208928 | tf_op jit(solution)/shard_map/ppermute | solution.py:181
  52.8 0.2 fold.5
  52.9 0.7 %collective-permute-start.13 = (f16[2,136,128]{2,1,0:T(8,128)(2,1)S(1)}, f16[2,136,128]{2,1,0:T(8,128)(2,1)S(1)}, u32[]{:S(2)}, u32[]{:S(2)}) collective-permute-start(f16[2,136,128]{2,1,0:T(8,128)(2,1)S(1)} %convert_element_type.30), channel_id=1, source_target_pairs={{1,2},{2,1},{5,6},{6,5},{9,10},{10,9},{13,14},{14,13},{17,18},{18,... | collective-permute-start | bytes 208904 | tf_op jit(solution)/shard_map/ppermute | solution.py:181
  53.6 0.1 collective-permute-start.12
  53.8 4.3 %collective-permute-done.12 = f16[2,136,128]{2,1,0:T(8,128)(2,1)S(1)} collective-permute-done((f16[2,136,128]{2,1,0:T(8,128)(2,1)S(1)}, f16[2,136,128]{2,1,0:T(8,128)(2,1)S(1)}, u32[]{:S(2)}, u32[]{:S(2)}) %collective-permute-start.12) | collective-permute-done | bytes 69664 | tf_op jit(solution)/shard_map/ppermute | solution.py:181
  58.0 1.3 %finish.1 = (f32[3,2,128]{2,1,0:T(2,128)}, f32[2,128,128]{2,1,0:T(8,128)}) custom-call(s32[2]{0:T(128)S(1)} %get-tuple-element.27.counts_ref, f32[2,136,128]{2,1,0:T(8,128)S(1)} %get-tuple-element.47.center_ref, f32[2,136,128]{2,1,0:T(8,128)S(1)} %convert_element_type.29.refs_0_, f32[2,136,128]{2,1,0:T(8,128)S(1)} %convert_element_type.31.refs_1_), custom_call_target="tpu_custom_call" | custom-call | tf_op jit(solution)/shard_map/finish/pallas_call | solution.py:830
  (29 shorter events, 0.4 us)
Async XLA Ops:
  2.2 7.9 %collective-permute-start.1 = (bf16[2,144,128]{2,1,0:T(8,128)(2,1)}, bf16[2,144,128]{2,1,0:T(8,128)(2,1)S(1)}, u32[]{:S(2)}, u32[]{:S(2)}) collective-permute-start(bf16[2,144,128]{2,1,0:T(8,128)(2,1)} %pack.1.packed_ref), channel_id=1, source_target_pairs={{1,2},{2,1},{5,6},{6,5},{9,10},{10,9},{13,14},{14,13},{17,18},{18,... | collective-permute-start | bytes 221192 | tf_op jit(solution)/shard_map/ppermute | solution.py:687
  2.8 7.2 %collective-permute-start = (bf16[2,144,128]{2,1,0:T(8,128)(2,1)}, bf16[2,144,128]{2,1,0:T(8,128)(2,1)S(1)}, u32[]{:S(2)}, u32[]{:S(2)}) collective-permute-start(bf16[2,144,128]{2,1,0:T(8,128)(2,1)} %pack.1.packed_ref), channel_id=1, source_target_pairs={{0,1},{2,3},{1,0},{3,2},{4,5},{6,7},{5,4},{7,6},{8,9},{10,11},{9,8... | collective-permute-start | bytes 221192 | tf_op jit(solution)/shard_map/ppermute | solution.py:687
  6.2 0.9 %copy-start = (bf16[2,144,128]{2,1,0:T(8,128)(2,1)S(1)}, bf16[2,144,128]{2,1,0:T(8,128)(2,1)}, u32[]{:S(2)}) copy-start(bf16[2,144,128]{2,1,0:T(8,128)(2,1)} %pack.1.packed_ref) | copy-start | bytes 221188
  7.1 0.7 %copy-start.3 = (s32[1,1,1,2]{3,2,1,0:T(1,128)S(1)}, s32[1,1,1,2]{3,2,1,0:T(1,128)}, u32[]{:S(2)}) copy-start(s32[1,1,1,2]{3,2,1,0:T(1,128)} %param.9) | copy-start | bytes 28
  7.7 0.7 %copy-start.4 = (s32[1,1,1,2,8]{4,3,2,1,0:T(2,128)S(1)}, s32[1,1,1,2,8]{4,3,2,1,0:T(2,128)}, u32[]{:S(2)}) copy-start(s32[1,1,1,2,8]{4,3,2,1,0:T(2,128)} %param.10) | copy-start | bytes 196
  10.1 8.5 %collective-permute-start.3 = (bf16[6,144,128]{2,1,0:T(8,128)(2,1)S(1)}, bf16[6,144,128]{2,1,0:T(8,128)(2,1)S(1)}, u32[]{:S(2)}, u32[]{:S(2)}) collective-permute-start(bf16[6,144,128]{2,1,0:T(8,128)(2,1)S(1)} %join.1.refs_0_), channel_id=1, source_target_pairs={{4,8},{8,4},{5,9},{9,5},{6,10},{10,6},{7,11},{11,7},{20,24},{24,20... | collective-permute-start | bytes 663560 | tf_op jit(solution)/shard_map/ppermute | solution.py:687
  13.6 6.4 %collective-permute-start.2 = (bf16[6,144,128]{2,1,0:T(8,128)(2,1)S(1)}, bf16[6,144,128]{2,1,0:T(8,128)(2,1)S(1)}, u32[]{:S(2)}, u32[]{:S(2)}) collective-permute-start(bf16[6,144,128]{2,1,0:T(8,128)(2,1)S(1)} %join.1.refs_0_), channel_id=1, source_target_pairs={{0,4},{8,12},{4,0},{12,8},{1,5},{9,13},{5,1},{13,9},{2,6},{10,14},... | collective-permute-start | bytes 663560 | tf_op jit(solution)/shard_map/ppermute | solution.py:687
  13.6 10.4 %collective-permute-start.4 = (bf16[6,144,128]{2,1,0:T(8,128)(2,1)S(1)}, bf16[6,144,128]{2,1,0:T(8,128)(2,1)S(1)}, u32[]{:S(2)}, u32[]{:S(2)}) collective-permute-start(bf16[6,144,128]{2,1,0:T(8,128)(2,1)S(1)} %join.1.refs_0_), channel_id=1, source_target_pairs={{0,16},{16,0},{1,17},{17,1},{2,18},{18,2},{3,19},{19,3},{4,20},{20... | collective-permute-start | bytes 663560 | tf_op jit(solution)/shard_map/ppermute | solution.py:736
  18.6 5.5 %collective-permute-start.6 = (bf16[6,144,128]{2,1,0:T(8,128)(2,1)S(1)}, bf16[6,144,128]{2,1,0:T(8,128)(2,1)S(1)}, u32[]{:S(2)}, u32[]{:S(2)}) collective-permute-start(bf16[6,144,128]{2,1,0:T(8,128)(2,1)S(1)} %collective-permute-done.3.refs_2_), channel_id=1, source_target_pairs={{0,16},{16,0},{1,17},{17,1},{2,18},{18,2},{3,19},{19,3},{4,20},{20... | collective-permute-start | bytes 663560 | tf_op jit(solution)/shard_map/ppermute | solution.py:737
  19.9 4.1 %collective-permute-start.5 = (bf16[6,144,128]{2,1,0:T(8,128)(2,1)S(1)}, bf16[6,144,128]{2,1,0:T(8,128)(2,1)S(1)}, u32[]{:S(2)}, u32[]{:S(2)}) collective-permute-start(bf16[6,144,128]{2,1,0:T(8,128)(2,1)S(1)} %collective-permute-done.2.refs_1_), channel_id=1, source_target_pairs={{0,16},{16,0},{1,17},{17,1},{2,18},{18,2},{3,19},{19,3},{4,20},{20... | collective-permute-start | bytes 663560 | tf_op jit(solution)/shard_map/ppermute | solution.py:737
  19.9 1.0 %copy-start.1 = (bf16[1024,128]{1,0:T(8,128)(2,1)S(1)}, bf16[1024,128]{1,0:T(8,128)(2,1)}, u32[]{:S(2)}) copy-start(bf16[1024,128]{1,0:T(8,128)(2,1)} %mixing_ref.1) | copy-start | bytes 786436
  20.9 0.7 %copy-start.2 = (f32[1,1,1,2,3,128]{5,3,4,2,1,0:T(2,128)S(1)}, f32[1,1,1,2,3,128]{5,3,4,2,1,0:T(2,128)}, u32[]{:S(2)}) copy-start(f32[1,1,1,2,3,128]{5,3,4,2,1,0:T(2,128)} %param.7) | copy-start | bytes 9220
  21.6 0.7 %copy-start.5 = (f32[4]{0:T(128)S(1)}, f32[4]{0:T(128)}, u32[]{:S(2)}) copy-start(f32[4]{0:T(128)} %rates_ref.1) | copy-start | bytes 52
  22.2 0.7 %copy-start.6 = (f32[128]{0:T(128)S(1)}, f32[128]{0:T(128)}, u32[]{:S(2)}) copy-start(f32[128]{0:T(128)} %param.12) | copy-start | bytes 1540
  37.5 5.4 %collective-permute-start.8 = (f32[6,136,128]{2,1,0:T(8,128)S(1)}, f32[6,136,128]{2,1,0:T(8,128)S(1)}, u32[]{:S(2)}, u32[]{:S(2)}) collective-permute-start(f32[6,136,128]{2,1,0:T(8,128)S(1)} %get-tuple-element.44), channel_id=1, source_target_pairs={{0,16},{16,0},{1,17},{17,1},{2,18},{18,2},{3,19},{19,3},{4,20},{20... | collective-permute-start | bytes 1253384 | tf_op jit(solution)/shard_map/ppermute | solution.py:815
  37.6 5.5 %collective-permute-start.10 = (f32[6,136,128]{2,1,0:T(8,128)S(1)}, f32[6,136,128]{2,1,0:T(8,128)S(1)}, u32[]{:S(2)}, u32[]{:S(2)}) collective-permute-start(f32[6,136,128]{2,1,0:T(8,128)S(1)} %get-tuple-element.46), channel_id=1, source_target_pairs={{0,16},{16,0},{1,17},{17,1},{2,18},{18,2},{3,19},{19,3},{4,20},{20... | collective-permute-start | bytes 1253384 | tf_op jit(solution)/shard_map/ppermute | solution.py:815
  42.8 9.9 %collective-permute-start.7 = (f32[6,136,128]{2,1,0:T(8,128)S(1)}, f32[6,136,128]{2,1,0:T(8,128)S(1)}, u32[]{:S(2)}, u32[]{:S(2)}) collective-permute-start(f32[6,136,128]{2,1,0:T(8,128)S(1)} %get-tuple-element.42), channel_id=1, source_target_pairs={{0,16},{16,0},{1,17},{17,1},{2,18},{18,2},{3,19},{19,3},{4,20},{20... | collective-permute-start | bytes 1253384 | tf_op jit(solution)/shard_map/ppermute | solution.py:815
  43.0 7.6 %collective-permute-start.9 = (f16[6,136,128]{2,1,0:T(8,128)(2,1)S(1)}, f16[6,136,128]{2,1,0:T(8,128)(2,1)S(1)}, u32[]{:S(2)}, u32[]{:S(2)}) collective-permute-start(f16[6,136,128]{2,1,0:T(8,128)(2,1)S(1)} %convert_element_type.24), channel_id=1, source_target_pairs={{0,4},{8,12},{4,0},{12,8},{1,5},{9,13},{5,1},{13,9},{2,6},{10,14},... | collective-permute-start | bytes 626696 | tf_op jit(solution)/shard_map/ppermute | solution.py:181
  43.3 9.5 %collective-permute-start.11 = (f16[6,136,128]{2,1,0:T(8,128)(2,1)S(1)}, f16[6,136,128]{2,1,0:T(8,128)(2,1)S(1)}, u32[]{:S(2)}, u32[]{:S(2)}) collective-permute-start(f16[6,136,128]{2,1,0:T(8,128)(2,1)S(1)} %convert_element_type.26), channel_id=1, source_target_pairs={{4,8},{8,4},{5,9},{9,5},{6,10},{10,6},{7,11},{11,7},{20,24},{24,20... | collective-permute-start | bytes 626696 | tf_op jit(solution)/shard_map/ppermute | solution.py:181
  52.9 0.8 %collective-permute-start.13 = (f16[2,136,128]{2,1,0:T(8,128)(2,1)S(1)}, f16[2,136,128]{2,1,0:T(8,128)(2,1)S(1)}, u32[]{:S(2)}, u32[]{:S(2)}) collective-permute-start(f16[2,136,128]{2,1,0:T(8,128)(2,1)S(1)} %convert_element_type.30), channel_id=1, source_target_pairs={{1,2},{2,1},{5,6},{6,5},{9,10},{10,9},{13,14},{14,13},{17,18},{18,... | collective-permute-start | bytes 208904 | tf_op jit(solution)/shard_map/ppermute | solution.py:181
  53.6 4.4 %collective-permute-start.12 = (f16[2,136,128]{2,1,0:T(8,128)(2,1)S(1)}, f16[2,136,128]{2,1,0:T(8,128)(2,1)S(1)}, u32[]{:S(2)}, u32[]{:S(2)}) collective-permute-start(f16[2,136,128]{2,1,0:T(8,128)(2,1)S(1)} %convert_element_type.28), channel_id=1, source_target_pairs={{0,1},{2,3},{1,0},{3,2},{4,5},{6,7},{5,4},{7,6},{8,9},{10,11},{9,8... | collective-permute-start | bytes 208904 | tf_op jit(solution)/shard_map/ppermute | solution.py:181

commit v5 on v4

--- a/solution.py
+++ b/solution.py
@@ -810,19 +810,20 @@
     ]
 
     def gather(k):
-        arrays = [ghosts[0][k]]
+        coded = []
         for plane, pairs in zip(ghosts[1:], swaps("gx")):
-            arrays.append(lax.ppermute(plane[k], "gx", pairs))
-        return arrays
+            (value,) = fold([(0, plane[k].shape[0], True)], [plane[k]], [])
+            coded.append(send(value, "gx", pairs))
+        return [ghosts[0][k]], coded
 
     received = []
     for k, pairs in enumerate(swaps("gy")):
-        arrays = gather(k + 1)
-        (value,) = fold([(0, arrays[0].shape[0], True)], arrays, [])
+        plain, coded = gather(k + 1)
+        (value,) = fold([(0, plain[0].shape[0], True)], plain, coded)
         received.append(send(value, "gy", pairs))
-    arrays = gather(0)
+    plain, coded = gather(0)
     cuts = [(k * tiles, (k + 1) * tiles, k > 0) for k in range(sides[2] + 1)]
-    center, *along_z = fold(cuts, arrays, received)
+    center, *along_z = fold(cuts, plain, coded + received)
     parts = [center]
     for value, pairs in zip(along_z, swaps("gz")):
         parts.append(send(value, "gz", pairs))

time: 59.7 us -> 60.2 us (level)
    ppermute x4 -> x7, starting transfers between devices: 2.73 us -> 3.43 us  [send(): lax.ppermute(value.astype(jnp.float16), axis, pairs).astype(jnp.float32)]
    ppermute x3 -> x0, starting transfers between devices: 0.64 us -> none  [gather(): arrays.append(lax.ppermute(plane[k], 'gx', pairs))]
    ppermute x4 -> x7, waiting for transfers between devices: 11.8 us -> 11.7 us  [send(): lax.ppermute(value.astype(jnp.float16), axis, pairs).astype(jnp.float32)]
  transfers between devices with their start and end apart: 14 -> 14, of which waited for: 5 -> 5; matrix products, arithmetic and copies ran while one was open for 0% -> 1% of each run, Pallas kernels for 13% -> 13%
where the time goes in v5:
time: 60.2 us; the launch traced here: 59.9 us
  Pallas kernels  24.3 us (40%)
  waiting for transfers between devices  18 us (30%)
  starting transfers between devices  11 us (18%)
  local copies, waits for them, and re-layouts  5.16 us (9%)
  between operations  0.97 us (2%)
    pallas_call x1, Pallas kernels, step(): pl.pallas_call(functools.partial(main_kernel, len(flat), len(far_shapes),...  13.4 us
    ppermute x7, waiting for transfers between devices, send(): lax.ppermute(value.astype(jnp.float16), axis, pairs).astype(jnp.float32)  11.7 us
    ppermute x4, starting transfers between devices, swap(): return [lax.ppermute(value, axis, pairs) for pairs in swaps(axis)]  7.49 us
    ppermute x4, waiting for transfers between devices, swap(): return [lax.ppermute(value, axis, pairs) for pairs in swaps(axis)]  6.24 us
    unnamed x14, local copies, waits for them, and re-layouts  5.16 us
    pallas_call x1, Pallas kernels, step(): pl.pallas_call(functools.partial(line_kernel, len(line_shapes), slots, co...  4.69 us
    ppermute x7, starting transfers between devices, send(): lax.ppermute(value.astype(jnp.float16), axis, pairs).astype(jnp.float32)  3.43 us
    pallas_call x1, Pallas kernels, step(): pl.pallas_call(functools.partial(side_kernel, sides), out_shape=[jax.Shap...  1.61 us
  transfers between devices with their start and end apart: 14, of which 5 were waited for; matrix products, arithmetic and copies ran while one was open for 1% of the time, Pallas kernels for 13%

profile of v5, /device:TPU:14, one launch (start us, length us, event | category | flops | bytes accessed | tf_op | source)
XLA Modules:
  0.0 59.9 jit_solution(10115765024149963151)
XLA Ops:
  0.6 1.5 %pack.1.packed_ref = bf16[2,144,128]{2,1,0:T(8,128)(2,1)} custom-call(s32[2]{0:T(128)} %bitcast.16, bf16[2,128,128]{2,1,0:T(8,128)(2,1)} %bitcast.20, f32[3,2,128]{2,1,0:T(2,128)} %bitcast.14), custom_call_target="tpu_custom_call" | custom-call | tf_op jit(solution)/shard_map/pack/pallas_call | solution.py:692
  2.2 0.7 %collective-permute-start.1 = (bf16[2,144,128]{2,1,0:T(8,128)(2,1)}, bf16[2,144,128]{2,1,0:T(8,128)(2,1)S(1)}, u32[]{:S(2)}, u32[]{:S(2)}) collective-permute-start(bf16[2,144,128]{2,1,0:T(8,128)(2,1)} %pack.1.packed_ref), channel_id=1, source_target_pairs={{1,2},{2,1},{5,6},{6,5},{9,10},{10,9},{13,14},{14,13},{17,18},{18,... | collective-permute-start | bytes 221192 | tf_op jit(solution)/shard_map/ppermute | solution.py:687
  2.8 3.3 %collective-permute-start = (bf16[2,144,128]{2,1,0:T(8,128)(2,1)}, bf16[2,144,128]{2,1,0:T(8,128)(2,1)S(1)}, u32[]{:S(2)}, u32[]{:S(2)}) collective-permute-start(bf16[2,144,128]{2,1,0:T(8,128)(2,1)} %pack.1.packed_ref), channel_id=1, source_target_pairs={{0,1},{2,3},{1,0},{3,2},{4,5},{6,7},{5,4},{7,6},{8,9},{10,11},{9,8... | collective-permute-start | bytes 221192 | tf_op jit(solution)/shard_map/ppermute | solution.py:687
  6.1 0.1 pad_add_fusion.axis_ref
  6.2 0.9 %copy-done = bf16[2,144,128]{2,1,0:T(8,128)(2,1)S(1)} copy-done((bf16[2,144,128]{2,1,0:T(8,128)(2,1)S(1)}, bf16[2,144,128]{2,1,0:T(8,128)(2,1)}, u32[]{:S(2)}) %copy-start) | copy-done | bytes 73752
  7.1 0.7 %copy-done.3 = s32[1,1,1,2]{3,2,1,0:T(1,128)S(1)} copy-done((s32[1,1,1,2]{3,2,1,0:T(1,128)S(1)}, s32[1,1,1,2]{3,2,1,0:T(1,128)}, u32[]{:S(2)}) %copy-start.3) | copy-done | bytes 32
  7.7 0.7 %copy-done.4 = s32[1,1,1,2,8]{4,3,2,1,0:T(2,128)S(1)} copy-done((s32[1,1,1,2,8]{4,3,2,1,0:T(2,128)S(1)}, s32[1,1,1,2,8]{4,3,2,1,0:T(2,128)}, u32[]{:S(2)}) %copy-start.4) | copy-done | bytes 88
  8.4 1.6 %sides.1 = (s32[2]{0:T(128)S(1)}, s32[2,10]{1,0:T(2,128)S(1)}, bf16[2,144,128]{2,1,0:T(8,128)(2,1)S(1)}) custom-call(s32[3]{0:T(128)S(1)} %pad_add_fusion.axis_ref, s32[2]{0:T(128)S(1)} %bitcast.17, s32[2,8]{1,0:T(2,128)S(1)} %bitcast.18, bf16[2,144,128]{2,1,0:T(8,128)(2,1)S(1)} %copy-done), custom_call_target="tpu_custom_call" | custom-call | tf_op jit(solution)/shard_map/sides/pallas_call | solution.py:702
  10.1 3.5 %collective-permute-start.3 = (bf16[6,144,128]{2,1,0:T(8,128)(2,1)S(1)}, bf16[6,144,128]{2,1,0:T(8,128)(2,1)S(1)}, u32[]{:S(2)}, u32[]{:S(2)}) collective-permute-start(bf16[6,144,128]{2,1,0:T(8,128)(2,1)S(1)} %join.1.refs_0_), channel_id=1, source_target_pairs={{4,8},{8,4},{5,9},{9,5},{6,10},{10,6},{7,11},{11,7},{20,24},{24,20... | collective-permute-start | bytes 663560 | tf_op jit(solution)/shard_map/ppermute | solution.py:687
  13.6 0.1 collective-permute-start.4
  13.7 4.9 %collective-permute-done.3.refs_2_ = bf16[6,144,128]{2,1,0:T(8,128)(2,1)S(1)} collective-permute-done((bf16[6,144,128]{2,1,0:T(8,128)(2,1)S(1)}, bf16[6,144,128]{2,1,0:T(8,128)(2,1)S(1)}, u32[]{:S(2)}, u32[]{:S(2)}) %collective-permute-start.3) | collective-permute-done | bytes 221216 | tf_op jit(solution)/shard_map/ppermute | solution.py:687
  18.6 1.4 %collective-permute-done.2.refs_1_ = bf16[6,144,128]{2,1,0:T(8,128)(2,1)S(1)} collective-permute-done((bf16[6,144,128]{2,1,0:T(8,128)(2,1)S(1)}, bf16[6,144,128]{2,1,0:T(8,128)(2,1)S(1)}, u32[]{:S(2)}, u32[]{:S(2)}) %collective-permute-start.2) | collective-permute-done | bytes 221216 | tf_op jit(solution)/shard_map/ppermute | solution.py:687
  19.9 0.9 %copy-done.1 = bf16[1024,128]{1,0:T(8,128)(2,1)S(1)} copy-done((bf16[1024,128]{1,0:T(8,128)(2,1)S(1)}, bf16[1024,128]{1,0:T(8,128)(2,1)}, u32[]{:S(2)}) %copy-start.1) | copy-done | bytes 262168
  20.9 0.7 %copy-done.2 = f32[1,1,1,2,3,128]{5,3,4,2,1,0:T(2,128)S(1)} copy-done((f32[1,1,1,2,3,128]{5,3,4,2,1,0:T(2,128)S(1)}, f32[1,1,1,2,3,128]{5,3,4,2,1,0:T(2,128)}, u32[]{:S(2)}) %copy-start.2) | copy-done | bytes 3096
  21.6 0.7 %copy-done.5 = f32[4]{0:T(128)S(1)} copy-done((f32[4]{0:T(128)S(1)}, f32[4]{0:T(128)}, u32[]{:S(2)}) %copy-start.5) | copy-done | bytes 40
  22.2 0.7 %copy-done.6 = f32[128]{0:T(128)S(1)} copy-done((f32[128]{0:T(128)S(1)}, f32[128]{0:T(128)}, u32[]{:S(2)}) %copy-start.6) | copy-done | bytes 536
  22.9 1.1 %stage.1 = (f32[4]{0:T(128)S(1)}, f32[3,2,128]{2,1,0:T(2,128)S(1)}, f32[1,128]{1,0:T(1,128)S(1)}, bf16[1024,128]{1,0:T(8,128)(2,1)S(1)}) custom-call(f32[4]{0:T(128)S(1)} %copy-done.5, f32[3,2,128]{2,1,0:T(2,128)S(1)} %bitcast.15, f32[1,128]{1,0:T(1,128)S(1)} %bitcast.19, bf16[1024,128]{1,0:T(8,128)(2,1)S(1)} %copy-done.1), custom_call_target="tpu_custom_call" | custom-call | tf_op jit(solution)/shard_map/stage/pallas_call | solution.py:721
  24.1 13.4 %pairs.1 = (f32[6,136,128]{2,1,0:T(8,128)S(1)}, f32[6,136,128]{2,1,0:T(8,128)S(1)}, f32[6,136,128]{2,1,0:T(8,128)S(1)}, f32[6,136,128]{2,1,0:T(8,128)S(1)}, f32[...) custom-call(s32[2]{0:T(128)S(1)} %get-tuple-element.27.counts_ref, ...), custom_call_target="tpu_custom_call" | custom-call | tf_op jit(solution)/shard_map/pairs/pallas_call | solution.py:770
  37.6 0.1 collective-permute-start.8
  37.8 0.6 collective-permute-start.10
  38.4 4.7 %lines.1 = (f32[6,136,128]{2,1,0:T(8,128)S(1)}, f32[6,136,128]{2,1,0:T(8,128)S(1)}) custom-call(s32[2]{0:T(128)S(1)} %get-tuple-element.27.counts_ref, s32[2,10]{1,0:T(2,128)S(1)} %get-tuple-element.28.table_ref, f32[4]{0:T(128)S(1)} %get-tuple-element.29.rates_ref, f32[2,3,128,128]{3,2,1,0:T(8,128)S(1)} %get-tuple-element.34.own_ref, ...), custom_call_target="tpu_custom_call" | custom-call | tf_op jit(solution)/shard_map/lines/pallas_call | solution.py:790
  43.2 0.1 collective-permute-start.7
  43.3 0.1 fold.8
  43.5 0.1 collective-permute-start.9
  43.6 0.1 fold.10
  43.8 1.9 %collective-permute-start.11 = (f16[6,136,128]{2,1,0:T(8,128)(2,1)S(1)}, f16[6,136,128]{2,1,0:T(8,128)(2,1)S(1)}, u32[]{:S(2)}, u32[]{:S(2)}) collective-permute-start(f16[6,136,128]{2,1,0:T(8,128)(2,1)S(1)} %convert_element_type.50), channel_id=1, source_target_pairs={{4,8},{8,4},{5,9},{9,5},{6,10},{10,6},{7,11},{11,7},{20,24},{24,20... | collective-permute-start | bytes 626696 | tf_op jit(solution)/shard_map/ppermute | solution.py:181
  45.7 5.4 %collective-permute-done.9 = f16[6,136,128]{2,1,0:T(8,128)(2,1)S(1)} collective-permute-done((f16[6,136,128]{2,1,0:T(8,128)(2,1)S(1)}, f16[6,136,128]{2,1,0:T(8,128)(2,1)S(1)}, u32[]{:S(2)}, u32[]{:S(2)}) %collective-permute-start.9) | collective-permute-done | bytes 208928 | tf_op jit(solution)/shard_map/ppermute | solution.py:181
  51.1 2.1 %collective-permute-done.11 = f16[6,136,128]{2,1,0:T(8,128)(2,1)S(1)} collective-permute-done((f16[6,136,128]{2,1,0:T(8,128)(2,1)S(1)}, f16[6,136,128]{2,1,0:T(8,128)(2,1)S(1)}, u32[]{:S(2)}, u32[]{:S(2)}) %collective-permute-start.11) | collective-permute-done | bytes 208928 | tf_op jit(solution)/shard_map/ppermute | solution.py:181
  53.2 0.2 fold.11
  53.5 0.7 %collective-permute-start.13 = (f16[2,136,128]{2,1,0:T(8,128)(2,1)S(1)}, f16[2,136,128]{2,1,0:T(8,128)(2,1)S(1)}, u32[]{:S(2)}, u32[]{:S(2)}) collective-permute-start(f16[2,136,128]{2,1,0:T(8,128)(2,1)S(1)} %convert_element_type.54), channel_id=1, source_target_pairs={{1,2},{2,1},{5,6},{6,5},{9,10},{10,9},{13,14},{14,13},{17,18},{18,... | collective-permute-start | bytes 208904 | tf_op jit(solution)/shard_map/ppermute | solution.py:181
  54.3 4.3 %collective-permute-done.12 = f16[2,136,128]{2,1,0:T(8,128)(2,1)S(1)} collective-permute-done((f16[2,136,128]{2,1,0:T(8,128)(2,1)S(1)}, f16[2,136,128]{2,1,0:T(8,128)(2,1)S(1)}, u32[]{:S(2)}, u32[]{:S(2)}) %collective-permute-start.12) | collective-permute-done | bytes 69664 | tf_op jit(solution)/shard_map/ppermute | solution.py:181
  58.5 1.3 %finish.1 = (f32[3,2,128]{2,1,0:T(2,128)}, f32[2,128,128]{2,1,0:T(8,128)}) custom-call(s32[2]{0:T(128)S(1)} %get-tuple-element.27.counts_ref, f32[2,136,128]{2,1,0:T(8,128)S(1)} %get-tuple-element.47.center_ref, f32[2,136,128]{2,1,0:T(8,128)S(1)} %convert_element_type.53.refs_0_, f32[2,136,128]{2,1,0:T(8,128)S(1)} %convert_element_type.55.refs_1_), custom_call_target="tpu_custom_call" | custom-call | tf_op jit(solution)/shard_map/finish/pallas_call | solution.py:831
  (38 shorter events, 0.7 us)
Async XLA Ops:
  2.2 7.9 %collective-permute-start.1 = (bf16[2,144,128]{2,1,0:T(8,128)(2,1)}, bf16[2,144,128]{2,1,0:T(8,128)(2,1)S(1)}, u32[]{:S(2)}, u32[]{:S(2)}) collective-permute-start(bf16[2,144,128]{2,1,0:T(8,128)(2,1)} %pack.1.packed_ref), channel_id=1, source_target_pairs={{1,2},{2,1},{5,6},{6,5},{9,10},{10,9},{13,14},{14,13},{17,18},{18,... | collective-permute-start | bytes 221192 | tf_op jit(solution)/shard_map/ppermute | solution.py:687
  2.8 7.2 %collective-permute-start = (bf16[2,144,128]{2,1,0:T(8,128)(2,1)}, bf16[2,144,128]{2,1,0:T(8,128)(2,1)S(1)}, u32[]{:S(2)}, u32[]{:S(2)}) collective-permute-start(bf16[2,144,128]{2,1,0:T(8,128)(2,1)} %pack.1.packed_ref), channel_id=1, source_target_pairs={{0,1},{2,3},{1,0},{3,2},{4,5},{6,7},{5,4},{7,6},{8,9},{10,11},{9,8... | collective-permute-start | bytes 221192 | tf_op jit(solution)/shard_map/ppermute | solution.py:687
  6.2 0.9 %copy-start = (bf16[2,144,128]{2,1,0:T(8,128)(2,1)S(1)}, bf16[2,144,128]{2,1,0:T(8,128)(2,1)}, u32[]{:S(2)}) copy-start(bf16[2,144,128]{2,1,0:T(8,128)(2,1)} %pack.1.packed_ref) | copy-start | bytes 221188
  7.1 0.7 %copy-start.3 = (s32[1,1,1,2]{3,2,1,0:T(1,128)S(1)}, s32[1,1,1,2]{3,2,1,0:T(1,128)}, u32[]{:S(2)}) copy-start(s32[1,1,1,2]{3,2,1,0:T(1,128)} %param.9) | copy-start | bytes 28
  7.7 0.7 %copy-start.4 = (s32[1,1,1,2,8]{4,3,2,1,0:T(2,128)S(1)}, s32[1,1,1,2,8]{4,3,2,1,0:T(2,128)}, u32[]{:S(2)}) copy-start(s32[1,1,1,2,8]{4,3,2,1,0:T(2,128)} %param.10) | copy-start | bytes 196
  10.1 8.5 %collective-permute-start.3 = (bf16[6,144,128]{2,1,0:T(8,128)(2,1)S(1)}, bf16[6,144,128]{2,1,0:T(8,128)(2,1)S(1)}, u32[]{:S(2)}, u32[]{:S(2)}) collective-permute-start(bf16[6,144,128]{2,1,0:T(8,128)(2,1)S(1)} %join.1.refs_0_), channel_id=1, source_target_pairs={{4,8},{8,4},{5,9},{9,5},{6,10},{10,6},{7,11},{11,7},{20,24},{24,20... | collective-permute-start | bytes 663560 | tf_op jit(solution)/shard_map/ppermute | solution.py:687
  13.6 6.4 %collective-permute-start.2 = (bf16[6,144,128]{2,1,0:T(8,128)(2,1)S(1)}, bf16[6,144,128]{2,1,0:T(8,128)(2,1)S(1)}, u32[]{:S(2)}, u32[]{:S(2)}) collective-permute-start(bf16[6,144,128]{2,1,0:T(8,128)(2,1)S(1)} %join.1.refs_0_), channel_id=1, source_target_pairs={{0,4},{8,12},{4,0},{12,8},{1,5},{9,13},{5,1},{13,9},{2,6},{10,14},... | collective-permute-start | bytes 663560 | tf_op jit(solution)/shard_map/ppermute | solution.py:687
  13.6 10.4 %collective-permute-start.4 = (bf16[6,144,128]{2,1,0:T(8,128)(2,1)S(1)}, bf16[6,144,128]{2,1,0:T(8,128)(2,1)S(1)}, u32[]{:S(2)}, u32[]{:S(2)}) collective-permute-start(bf16[6,144,128]{2,1,0:T(8,128)(2,1)S(1)} %join.1.refs_0_), channel_id=1, source_target_pairs={{0,16},{16,0},{1,17},{17,1},{2,18},{18,2},{3,19},{19,3},{4,20},{20... | collective-permute-start | bytes 663560 | tf_op jit(solution)/shard_map/ppermute | solution.py:736
  18.6 5.5 %collective-permute-start.6 = (bf16[6,144,128]{2,1,0:T(8,128)(2,1)S(1)}, bf16[6,144,128]{2,1,0:T(8,128)(2,1)S(1)}, u32[]{:S(2)}, u32[]{:S(2)}) collective-permute-start(bf16[6,144,128]{2,1,0:T(8,128)(2,1)S(1)} %collective-permute-done.3.refs_2_), channel_id=1, source_target_pairs={{0,16},{16,0},{1,17},{17,1},{2,18},{18,2},{3,19},{19,3},{4,20},{20... | collective-permute-start | bytes 663560 | tf_op jit(solution)/shard_map/ppermute | solution.py:737
  19.9 4.1 %collective-permute-start.5 = (bf16[6,144,128]{2,1,0:T(8,128)(2,1)S(1)}, bf16[6,144,128]{2,1,0:T(8,128)(2,1)S(1)}, u32[]{:S(2)}, u32[]{:S(2)}) collective-permute-start(bf16[6,144,128]{2,1,0:T(8,128)(2,1)S(1)} %collective-permute-done.2.refs_1_), channel_id=1, source_target_pairs={{0,16},{16,0},{1,17},{17,1},{2,18},{18,2},{3,19},{19,3},{4,20},{20... | collective-permute-start | bytes 663560 | tf_op jit(solution)/shard_map/ppermute | solution.py:737
  19.9 1.0 %copy-start.1 = (bf16[1024,128]{1,0:T(8,128)(2,1)S(1)}, bf16[1024,128]{1,0:T(8,128)(2,1)}, u32[]{:S(2)}) copy-start(bf16[1024,128]{1,0:T(8,128)(2,1)} %mixing_ref.1) | copy-start | bytes 786436
  20.9 0.7 %copy-start.2 = (f32[1,1,1,2,3,128]{5,3,4,2,1,0:T(2,128)S(1)}, f32[1,1,1,2,3,128]{5,3,4,2,1,0:T(2,128)}, u32[]{:S(2)}) copy-start(f32[1,1,1,2,3,128]{5,3,4,2,1,0:T(2,128)} %param.7) | copy-start | bytes 9220
  21.6 0.7 %copy-start.5 = (f32[4]{0:T(128)S(1)}, f32[4]{0:T(128)}, u32[]{:S(2)}) copy-start(f32[4]{0:T(128)} %rates_ref.1) | copy-start | bytes 52
  22.2 0.7 %copy-start.6 = (f32[128]{0:T(128)S(1)}, f32[128]{0:T(128)}, u32[]{:S(2)}) copy-start(f32[128]{0:T(128)} %param.12) | copy-start | bytes 1540
  37.6 5.6 %collective-permute-start.8 = (f16[6,136,128]{2,1,0:T(8,128)(2,1)S(1)}, f16[6,136,128]{2,1,0:T(8,128)(2,1)S(1)}, u32[]{:S(2)}, u32[]{:S(2)}) collective-permute-start(f16[6,136,128]{2,1,0:T(8,128)(2,1)S(1)} %convert_element_type.44), channel_id=1, source_target_pairs={{0,16},{16,0},{1,17},{17,1},{2,18},{18,2},{3,19},{19,3},{4,20},{20... | collective-permute-start | bytes 626696 | tf_op jit(solution)/shard_map/ppermute | solution.py:181
  37.8 5.7 %collective-permute-start.10 = (f16[6,136,128]{2,1,0:T(8,128)(2,1)S(1)}, f16[6,136,128]{2,1,0:T(8,128)(2,1)S(1)}, u32[]{:S(2)}, u32[]{:S(2)}) collective-permute-start(f16[6,136,128]{2,1,0:T(8,128)(2,1)S(1)} %convert_element_type.48), channel_id=1, source_target_pairs={{0,16},{16,0},{1,17},{17,1},{2,18},{18,2},{3,19},{19,3},{4,20},{20... | collective-permute-start | bytes 626696 | tf_op jit(solution)/shard_map/ppermute | solution.py:181
  43.2 2.5 %collective-permute-start.7 = (f16[6,136,128]{2,1,0:T(8,128)(2,1)S(1)}, f16[6,136,128]{2,1,0:T(8,128)(2,1)S(1)}, u32[]{:S(2)}, u32[]{:S(2)}) collective-permute-start(f16[6,136,128]{2,1,0:T(8,128)(2,1)S(1)} %convert_element_type.42), channel_id=1, source_target_pairs={{0,16},{16,0},{1,17},{17,1},{2,18},{18,2},{3,19},{19,3},{4,20},{20... | collective-permute-start | bytes 626696 | tf_op jit(solution)/shard_map/ppermute | solution.py:181
  43.5 7.6 %collective-permute-start.9 = (f16[6,136,128]{2,1,0:T(8,128)(2,1)S(1)}, f16[6,136,128]{2,1,0:T(8,128)(2,1)S(1)}, u32[]{:S(2)}, u32[]{:S(2)}) collective-permute-start(f16[6,136,128]{2,1,0:T(8,128)(2,1)S(1)} %convert_element_type.46), channel_id=1, source_target_pairs={{0,4},{8,12},{4,0},{12,8},{1,5},{9,13},{5,1},{13,9},{2,6},{10,14},... | collective-permute-start | bytes 626696 | tf_op jit(solution)/shard_map/ppermute | solution.py:181
  43.8 9.4 %collective-permute-start.11 = (f16[6,136,128]{2,1,0:T(8,128)(2,1)S(1)}, f16[6,136,128]{2,1,0:T(8,128)(2,1)S(1)}, u32[]{:S(2)}, u32[]{:S(2)}) collective-permute-start(f16[6,136,128]{2,1,0:T(8,128)(2,1)S(1)} %convert_element_type.50), channel_id=1, source_target_pairs={{4,8},{8,4},{5,9},{9,5},{6,10},{10,6},{7,11},{11,7},{20,24},{24,20... | collective-permute-start | bytes 626696 | tf_op jit(solution)/shard_map/ppermute | solution.py:181
  53.5 0.8 %collective-permute-start.13 = (f16[2,136,128]{2,1,0:T(8,128)(2,1)S(1)}, f16[2,136,128]{2,1,0:T(8,128)(2,1)S(1)}, u32[]{:S(2)}, u32[]{:S(2)}) collective-permute-start(f16[2,136,128]{2,1,0:T(8,128)(2,1)S(1)} %convert_element_type.54), channel_id=1, source_target_pairs={{1,2},{2,1},{5,6},{6,5},{9,10},{10,9},{13,14},{14,13},{17,18},{18,... | collective-permute-start | bytes 208904 | tf_op jit(solution)/shard_map/ppermute | solution.py:181
  54.1 4.4 %collective-permute-start.12 = (f16[2,136,128]{2,1,0:T(8,128)(2,1)S(1)}, f16[2,136,128]{2,1,0:T(8,128)(2,1)S(1)}, u32[]{:S(2)}, u32[]{:S(2)}) collective-permute-start(f16[2,136,128]{2,1,0:T(8,128)(2,1)S(1)} %convert_element_type.52), channel_id=1, source_target_pairs={{0,1},{2,3},{1,0},{3,2},{4,5},{6,7},{5,4},{7,6},{8,9},{10,11},{9,8... | collective-permute-start | bytes 208904 | tf_op jit(solution)/shard_map/ppermute | solution.py:181

commit v6 on v5

--- a/solution.py
+++ b/solution.py
@@ -441,10 +441,10 @@
             features_ref[t, spare + atoms : spare + 2 * atoms] = features_ref[t, ahead, :]
             features_ref[t, spare + 2 * atoms : spare + 3 * atoms] = features_ref[t, behind, :]
 
-            def forward(chunk, carry):
+            def forward(used, chunk, carry):
                 start = pl.multiple_of(chunk * ROWS, ROWS)
                 base = pl.multiple_of(chunk * chunk_rows, chunk_rows)
-                for slot in range(2 * couples):
+                for slot in range(2 * used):
                     for g in range(groups):
                         where = pl.ds(start + g * GROUP, GROUP)
                         offset, radial = pairs.geometry(t, slot, where)
@@ -457,18 +457,23 @@
                                     jnp.bfloat16
                                 )
                 where = pl.ds(base, chunk_rows)
-                basis = [basis_ref[t, slot, where, :] for slot in range(2 * couples)]
+                basis = [basis_ref[t, slot, where, :] for slot in range(2 * used)]
                 sum_ref[t, where, :] = (
                     jnp.dot(
                         jnp.concatenate(basis, axis=1),
-                        features_ref[t, : 2 * couples * atoms],
+                        features_ref[t, : 2 * used * atoms],
                         preferred_element_type=jnp.float32,
                     )
                     * scaling
                 )
                 return carry
 
-            lax.fori_loop(0, chunks, forward, 0)
+            for used in range(1, couples + 1):
+
+                def run(used=used):
+                    lax.fori_loop(0, chunks, functools.partial(forward, used), 0)
+
+                pl.when((table_ref[t, slots + 1] + 1) // 2 == used)(run)
 
             def clear(chunk, carry):
                 where = pl.ds(pl.multiple_of(chunk * chunk_rows, chunk_rows), chunk_rows)

time: 60.2 us -> 60.3 us (level)
  no operation moved by 1% of the time
where the time goes in v6:
time: 60.3 us; the launch traced here: 59.9 us
  Pallas kernels  24.4 us (40%)
  waiting for transfers between devices  18 us (30%)
  starting transfers between devices  11 us (18%)
  local copies, waits for them, and re-layouts  5.16 us (9%)
  between operations  0.97 us (2%)
    pallas_call x1, Pallas kernels, step(): pl.pallas_call(functools.partial(main_kernel, len(flat), len(far_shapes),...  13.5 us
    ppermute x7, waiting for transfers between devices, send(): lax.ppermute(value.astype(jnp.float16), axis, pairs).astype(jnp.float32)  11.7 us
    ppermute x4, starting transfers between devices, swap(): return [lax.ppermute(value, axis, pairs) for pairs in swaps(axis)]  7.49 us
    ppermute x4, waiting for transfers between devices, swap(): return [lax.ppermute(value, axis, pairs) for pairs in swaps(axis)]  6.24 us
    unnamed x14, local copies, waits for them, and re-layouts  5.16 us
    pallas_call x1, Pallas kernels, step(): pl.pallas_call(functools.partial(line_kernel, len(line_shapes), slots, co...  4.69 us
    ppermute x7, starting transfers between devices, send(): lax.ppermute(value.astype(jnp.float16), axis, pairs).astype(jnp.float32)  3.43 us
    pallas_call x1, Pallas kernels, step(): pl.pallas_call(functools.partial(side_kernel, sides), out_shape=[jax.Shap...  1.61 us
  transfers between devices with their start and end apart: 14, of which 5 were waited for; matrix products, arithmetic and copies ran while one was open for 1% of the time, Pallas kernels for 13%

profile of v6, /device:TPU:14, one launch (start us, length us, event | category | flops | bytes accessed | tf_op | source)
XLA Modules:
  0.0 59.9 jit_solution(10672559664165966229)
XLA Ops:
  0.6 1.5 %pack.1.packed_ref = bf16[2,144,128]{2,1,0:T(8,128)(2,1)} custom-call(s32[2]{0:T(128)} %bitcast.16, bf16[2,128,128]{2,1,0:T(8,128)(2,1)} %bitcast.20, f32[3,2,128]{2,1,0:T(2,128)} %bitcast.14), custom_call_target="tpu_custom_call" | custom-call | tf_op jit(solution)/shard_map/pack/pallas_call | solution.py:697
  2.2 0.7 %collective-permute-start.1 = (bf16[2,144,128]{2,1,0:T(8,128)(2,1)}, bf16[2,144,128]{2,1,0:T(8,128)(2,1)S(1)}, u32[]{:S(2)}, u32[]{:S(2)}) collective-permute-start(bf16[2,144,128]{2,1,0:T(8,128)(2,1)} %pack.1.packed_ref), channel_id=1, source_target_pairs={{1,2},{2,1},{5,6},{6,5},{9,10},{10,9},{13,14},{14,13},{17,18},{18,... | collective-permute-start | bytes 221192 | tf_op jit(solution)/shard_map/ppermute | solution.py:692
  2.8 3.3 %collective-permute-start = (bf16[2,144,128]{2,1,0:T(8,128)(2,1)}, bf16[2,144,128]{2,1,0:T(8,128)(2,1)S(1)}, u32[]{:S(2)}, u32[]{:S(2)}) collective-permute-start(bf16[2,144,128]{2,1,0:T(8,128)(2,1)} %pack.1.packed_ref), channel_id=1, source_target_pairs={{0,1},{2,3},{1,0},{3,2},{4,5},{6,7},{5,4},{7,6},{8,9},{10,11},{9,8... | collective-permute-start | bytes 221192 | tf_op jit(solution)/shard_map/ppermute | solution.py:692
  6.1 0.1 pad_add_fusion.axis_ref
  6.2 0.9 %copy-done = bf16[2,144,128]{2,1,0:T(8,128)(2,1)S(1)} copy-done((bf16[2,144,128]{2,1,0:T(8,128)(2,1)S(1)}, bf16[2,144,128]{2,1,0:T(8,128)(2,1)}, u32[]{:S(2)}) %copy-start) | copy-done | bytes 73752
  7.1 0.7 %copy-done.3 = s32[1,1,1,2]{3,2,1,0:T(1,128)S(1)} copy-done((s32[1,1,1,2]{3,2,1,0:T(1,128)S(1)}, s32[1,1,1,2]{3,2,1,0:T(1,128)}, u32[]{:S(2)}) %copy-start.3) | copy-done | bytes 32
  7.7 0.7 %copy-done.4 = s32[1,1,1,2,8]{4,3,2,1,0:T(2,128)S(1)} copy-done((s32[1,1,1,2,8]{4,3,2,1,0:T(2,128)S(1)}, s32[1,1,1,2,8]{4,3,2,1,0:T(2,128)}, u32[]{:S(2)}) %copy-start.4) | copy-done | bytes 88
  8.4 1.6 %sides.1 = (s32[2]{0:T(128)S(1)}, s32[2,10]{1,0:T(2,128)S(1)}, bf16[2,144,128]{2,1,0:T(8,128)(2,1)S(1)}) custom-call(s32[3]{0:T(128)S(1)} %pad_add_fusion.axis_ref, s32[2]{0:T(128)S(1)} %bitcast.17, s32[2,8]{1,0:T(2,128)S(1)} %bitcast.18, bf16[2,144,128]{2,1,0:T(8,128)(2,1)S(1)} %copy-done), custom_call_target="tpu_custom_call" | custom-call | tf_op jit(solution)/shard_map/sides/pallas_call | solution.py:707
  10.1 3.5 %collective-permute-start.3 = (bf16[6,144,128]{2,1,0:T(8,128)(2,1)S(1)}, bf16[6,144,128]{2,1,0:T(8,128)(2,1)S(1)}, u32[]{:S(2)}, u32[]{:S(2)}) collective-permute-start(bf16[6,144,128]{2,1,0:T(8,128)(2,1)S(1)} %join.1.refs_0_), channel_id=1, source_target_pairs={{4,8},{8,4},{5,9},{9,5},{6,10},{10,6},{7,11},{11,7},{20,24},{24,20... | collective-permute-start | bytes 663560 | tf_op jit(solution)/shard_map/ppermute | solution.py:692
  13.6 0.1 collective-permute-start.4
  13.7 4.9 %collective-permute-done.3.refs_2_ = bf16[6,144,128]{2,1,0:T(8,128)(2,1)S(1)} collective-permute-done((bf16[6,144,128]{2,1,0:T(8,128)(2,1)S(1)}, bf16[6,144,128]{2,1,0:T(8,128)(2,1)S(1)}, u32[]{:S(2)}, u32[]{:S(2)}) %collective-permute-start.3) | collective-permute-done | bytes 221216 | tf_op jit(solution)/shard_map/ppermute | solution.py:692
  18.6 1.4 %collective-permute-done.2.refs_1_ = bf16[6,144,128]{2,1,0:T(8,128)(2,1)S(1)} collective-permute-done((bf16[6,144,128]{2,1,0:T(8,128)(2,1)S(1)}, bf16[6,144,128]{2,1,0:T(8,128)(2,1)S(1)}, u32[]{:S(2)}, u32[]{:S(2)}) %collective-permute-start.2) | collective-permute-done | bytes 221216 | tf_op jit(solution)/shard_map/ppermute | solution.py:692
  19.9 0.9 %copy-done.1 = bf16[1024,128]{1,0:T(8,128)(2,1)S(1)} copy-done((bf16[1024,128]{1,0:T(8,128)(2,1)S(1)}, bf16[1024,128]{1,0:T(8,128)(2,1)}, u32[]{:S(2)}) %copy-start.1) | copy-done | bytes 262168
  20.9 0.7 %copy-done.2 = f32[1,1,1,2,3,128]{5,3,4,2,1,0:T(2,128)S(1)} copy-done((f32[1,1,1,2,3,128]{5,3,4,2,1,0:T(2,128)S(1)}, f32[1,1,1,2,3,128]{5,3,4,2,1,0:T(2,128)}, u32[]{:S(2)}) %copy-start.2) | copy-done | bytes 3096
  21.6 0.7 %copy-done.5 = f32[4]{0:T(128)S(1)} copy-done((f32[4]{0:T(128)S(1)}, f32[4]{0:T(128)}, u32[]{:S(2)}) %copy-start.5) | copy-done | bytes 40
  22.2 0.7 %copy-done.6 = f32[128]{0:T(128)S(1)} copy-done((f32[128]{0:T(128)S(1)}, f32[128]{0:T(128)}, u32[]{:S(2)}) %copy-start.6) | copy-done | bytes 536
  22.9 1.1 %stage.1 = (f32[4]{0:T(128)S(1)}, f32[3,2,128]{2,1,0:T(2,128)S(1)}, f32[1,128]{1,0:T(1,128)S(1)}, bf16[1024,128]{1,0:T(8,128)(2,1)S(1)}) custom-call(f32[4]{0:T(128)S(1)} %copy-done.5, f32[3,2,128]{2,1,0:T(2,128)S(1)} %bitcast.15, f32[1,128]{1,0:T(1,128)S(1)} %bitcast.19, bf16[1024,128]{1,0:T(8,128)(2,1)S(1)} %copy-done.1), custom_call_target="tpu_custom_call" | custom-call | tf_op jit(solution)/shard_map/stage/pallas_call | solution.py:726
  24.1 13.5 %pairs.1 = (f32[6,136,128]{2,1,0:T(8,128)S(1)}, f32[6,136,128]{2,1,0:T(8,128)S(1)}, f32[6,136,128]{2,1,0:T(8,128)S(1)}, f32[6,136,128]{2,1,0:T(8,128)S(1)}, f32[...) custom-call(s32[2]{0:T(128)S(1)} %get-tuple-element.27.counts_ref, ...), custom_call_target="tpu_custom_call" | custom-call | tf_op jit(solution)/shard_map/pairs/pallas_call | solution.py:775
  37.7 0.1 collective-permute-start.8
  37.9 0.6 collective-permute-start.10
  38.5 4.7 %lines.1 = (f32[6,136,128]{2,1,0:T(8,128)S(1)}, f32[6,136,128]{2,1,0:T(8,128)S(1)}) custom-call(s32[2]{0:T(128)S(1)} %get-tuple-element.27.counts_ref, s32[2,10]{1,0:T(2,128)S(1)} %get-tuple-element.28.table_ref, f32[4]{0:T(128)S(1)} %get-tuple-element.29.rates_ref, f32[2,3,128,128]{3,2,1,0:T(8,128)S(1)} %get-tuple-element.34.own_ref, ...), custom_call_target="tpu_custom_call" | custom-call | tf_op jit(solution)/shard_map/lines/pallas_call | solution.py:795
  43.3 0.1 collective-permute-start.7
  43.4 0.1 fold.8
  43.6 0.1 collective-permute-start.9
  43.7 0.1 fold.10
  43.9 1.9 %collective-permute-start.11 = (f16[6,136,128]{2,1,0:T(8,128)(2,1)S(1)}, f16[6,136,128]{2,1,0:T(8,128)(2,1)S(1)}, u32[]{:S(2)}, u32[]{:S(2)}) collective-permute-start(f16[6,136,128]{2,1,0:T(8,128)(2,1)S(1)} %convert_element_type.50), channel_id=1, source_target_pairs={{4,8},{8,4},{5,9},{9,5},{6,10},{10,6},{7,11},{11,7},{20,24},{24,20... | collective-permute-start | bytes 626696 | tf_op jit(solution)/shard_map/ppermute | solution.py:181
  45.8 5.4 %collective-permute-done.9 = f16[6,136,128]{2,1,0:T(8,128)(2,1)S(1)} collective-permute-done((f16[6,136,128]{2,1,0:T(8,128)(2,1)S(1)}, f16[6,136,128]{2,1,0:T(8,128)(2,1)S(1)}, u32[]{:S(2)}, u32[]{:S(2)}) %collective-permute-start.9) | collective-permute-done | bytes 208928 | tf_op jit(solution)/shard_map/ppermute | solution.py:181
  51.2 2.1 %collective-permute-done.11 = f16[6,136,128]{2,1,0:T(8,128)(2,1)S(1)} collective-permute-done((f16[6,136,128]{2,1,0:T(8,128)(2,1)S(1)}, f16[6,136,128]{2,1,0:T(8,128)(2,1)S(1)}, u32[]{:S(2)}, u32[]{:S(2)}) %collective-permute-start.11) | collective-permute-done | bytes 208928 | tf_op jit(solution)/shard_map/ppermute | solution.py:181
  53.3 0.2 fold.11
  53.5 0.7 %collective-permute-start.13 = (f16[2,136,128]{2,1,0:T(8,128)(2,1)S(1)}, f16[2,136,128]{2,1,0:T(8,128)(2,1)S(1)}, u32[]{:S(2)}, u32[]{:S(2)}) collective-permute-start(f16[2,136,128]{2,1,0:T(8,128)(2,1)S(1)} %convert_element_type.54), channel_id=1, source_target_pairs={{1,2},{2,1},{5,6},{6,5},{9,10},{10,9},{13,14},{14,13},{17,18},{18,... | collective-permute-start | bytes 208904 | tf_op jit(solution)/shard_map/ppermute | solution.py:181
  54.3 4.3 %collective-permute-done.12 = f16[2,136,128]{2,1,0:T(8,128)(2,1)S(1)} collective-permute-done((f16[2,136,128]{2,1,0:T(8,128)(2,1)S(1)}, f16[2,136,128]{2,1,0:T(8,128)(2,1)S(1)}, u32[]{:S(2)}, u32[]{:S(2)}) %collective-permute-start.12) | collective-permute-done | bytes 69664 | tf_op jit(solution)/shard_map/ppermute | solution.py:181
  58.6 1.3 %finish.1 = (f32[3,2,128]{2,1,0:T(2,128)}, f32[2,128,128]{2,1,0:T(8,128)}) custom-call(s32[2]{0:T(128)S(1)} %get-tuple-element.27.counts_ref, f32[2,136,128]{2,1,0:T(8,128)S(1)} %get-tuple-element.47.center_ref, f32[2,136,128]{2,1,0:T(8,128)S(1)} %convert_element_type.53.refs_0_, f32[2,136,128]{2,1,0:T(8,128)S(1)} %convert_element_type.55.refs_1_), custom_call_target="tpu_custom_call" | custom-call | tf_op jit(solution)/shard_map/finish/pallas_call | solution.py:836
  (38 shorter events, 0.7 us)
Async XLA Ops:
  2.2 7.9 %collective-permute-start.1 = (bf16[2,144,128]{2,1,0:T(8,128)(2,1)}, bf16[2,144,128]{2,1,0:T(8,128)(2,1)S(1)}, u32[]{:S(2)}, u32[]{:S(2)}) collective-permute-start(bf16[2,144,128]{2,1,0:T(8,128)(2,1)} %pack.1.packed_ref), channel_id=1, source_target_pairs={{1,2},{2,1},{5,6},{6,5},{9,10},{10,9},{13,14},{14,13},{17,18},{18,... | collective-permute-start | bytes 221192 | tf_op jit(solution)/shard_map/ppermute | solution.py:692
  2.8 7.2 %collective-permute-start = (bf16[2,144,128]{2,1,0:T(8,128)(2,1)}, bf16[2,144,128]{2,1,0:T(8,128)(2,1)S(1)}, u32[]{:S(2)}, u32[]{:S(2)}) collective-permute-start(bf16[2,144,128]{2,1,0:T(8,128)(2,1)} %pack.1.packed_ref), channel_id=1, source_target_pairs={{0,1},{2,3},{1,0},{3,2},{4,5},{6,7},{5,4},{7,6},{8,9},{10,11},{9,8... | collective-permute-start | bytes 221192 | tf_op jit(solution)/shard_map/ppermute | solution.py:692
  6.2 0.9 %copy-start = (bf16[2,144,128]{2,1,0:T(8,128)(2,1)S(1)}, bf16[2,144,128]{2,1,0:T(8,128)(2,1)}, u32[]{:S(2)}) copy-start(bf16[2,144,128]{2,1,0:T(8,128)(2,1)} %pack.1.packed_ref) | copy-start | bytes 221188
  7.1 0.7 %copy-start.3 = (s32[1,1,1,2]{3,2,1,0:T(1,128)S(1)}, s32[1,1,1,2]{3,2,1,0:T(1,128)}, u32[]{:S(2)}) copy-start(s32[1,1,1,2]{3,2,1,0:T(1,128)} %param.9) | copy-start | bytes 28
  7.7 0.7 %copy-start.4 = (s32[1,1,1,2,8]{4,3,2,1,0:T(2,128)S(1)}, s32[1,1,1,2,8]{4,3,2,1,0:T(2,128)}, u32[]{:S(2)}) copy-start(s32[1,1,1,2,8]{4,3,2,1,0:T(2,128)} %param.10) | copy-start | bytes 196
  10.1 8.5 %collective-permute-start.3 = (bf16[6,144,128]{2,1,0:T(8,128)(2,1)S(1)}, bf16[6,144,128]{2,1,0:T(8,128)(2,1)S(1)}, u32[]{:S(2)}, u32[]{:S(2)}) collective-permute-start(bf16[6,144,128]{2,1,0:T(8,128)(2,1)S(1)} %join.1.refs_0_), channel_id=1, source_target_pairs={{4,8},{8,4},{5,9},{9,5},{6,10},{10,6},{7,11},{11,7},{20,24},{24,20... | collective-permute-start | bytes 663560 | tf_op jit(solution)/shard_map/ppermute | solution.py:692
  13.6 6.4 %collective-permute-start.2 = (bf16[6,144,128]{2,1,0:T(8,128)(2,1)S(1)}, bf16[6,144,128]{2,1,0:T(8,128)(2,1)S(1)}, u32[]{:S(2)}, u32[]{:S(2)}) collective-permute-start(bf16[6,144,128]{2,1,0:T(8,128)(2,1)S(1)} %join.1.refs_0_), channel_id=1, source_target_pairs={{0,4},{8,12},{4,0},{12,8},{1,5},{9,13},{5,1},{13,9},{2,6},{10,14},... | collective-permute-start | bytes 663560 | tf_op jit(solution)/shard_map/ppermute | solution.py:692
  13.6 10.4 %collective-permute-start.4 = (bf16[6,144,128]{2,1,0:T(8,128)(2,1)S(1)}, bf16[6,144,128]{2,1,0:T(8,128)(2,1)S(1)}, u32[]{:S(2)}, u32[]{:S(2)}) collective-permute-start(bf16[6,144,128]{2,1,0:T(8,128)(2,1)S(1)} %join.1.refs_0_), channel_id=1, source_target_pairs={{0,16},{16,0},{1,17},{17,1},{2,18},{18,2},{3,19},{19,3},{4,20},{20... | collective-permute-start | bytes 663560 | tf_op jit(solution)/shard_map/ppermute | solution.py:741
  18.6 5.5 %collective-permute-start.6 = (bf16[6,144,128]{2,1,0:T(8,128)(2,1)S(1)}, bf16[6,144,128]{2,1,0:T(8,128)(2,1)S(1)}, u32[]{:S(2)}, u32[]{:S(2)}) collective-permute-start(bf16[6,144,128]{2,1,0:T(8,128)(2,1)S(1)} %collective-permute-done.3.refs_2_), channel_id=1, source_target_pairs={{0,16},{16,0},{1,17},{17,1},{2,18},{18,2},{3,19},{19,3},{4,20},{20... | collective-permute-start | bytes 663560 | tf_op jit(solution)/shard_map/ppermute | solution.py:742
  19.9 4.1 %collective-permute-start.5 = (bf16[6,144,128]{2,1,0:T(8,128)(2,1)S(1)}, bf16[6,144,128]{2,1,0:T(8,128)(2,1)S(1)}, u32[]{:S(2)}, u32[]{:S(2)}) collective-permute-start(bf16[6,144,128]{2,1,0:T(8,128)(2,1)S(1)} %collective-permute-done.2.refs_1_), channel_id=1, source_target_pairs={{0,16},{16,0},{1,17},{17,1},{2,18},{18,2},{3,19},{19,3},{4,20},{20... | collective-permute-start | bytes 663560 | tf_op jit(solution)/shard_map/ppermute | solution.py:742
  19.9 1.0 %copy-start.1 = (bf16[1024,128]{1,0:T(8,128)(2,1)S(1)}, bf16[1024,128]{1,0:T(8,128)(2,1)}, u32[]{:S(2)}) copy-start(bf16[1024,128]{1,0:T(8,128)(2,1)} %mixing_ref.1) | copy-start | bytes 786436
  20.9 0.7 %copy-start.2 = (f32[1,1,1,2,3,128]{5,3,4,2,1,0:T(2,128)S(1)}, f32[1,1,1,2,3,128]{5,3,4,2,1,0:T(2,128)}, u32[]{:S(2)}) copy-start(f32[1,1,1,2,3,128]{5,3,4,2,1,0:T(2,128)} %param.7) | copy-start | bytes 9220
  21.6 0.7 %copy-start.5 = (f32[4]{0:T(128)S(1)}, f32[4]{0:T(128)}, u32[]{:S(2)}) copy-start(f32[4]{0:T(128)} %rates_ref.1) | copy-start | bytes 52
  22.2 0.7 %copy-start.6 = (f32[128]{0:T(128)S(1)}, f32[128]{0:T(128)}, u32[]{:S(2)}) copy-start(f32[128]{0:T(128)} %param.12) | copy-start | bytes 1540
  37.7 5.6 %collective-permute-start.8 = (f16[6,136,128]{2,1,0:T(8,128)(2,1)S(1)}, f16[6,136,128]{2,1,0:T(8,128)(2,1)S(1)}, u32[]{:S(2)}, u32[]{:S(2)}) collective-permute-start(f16[6,136,128]{2,1,0:T(8,128)(2,1)S(1)} %convert_element_type.44), channel_id=1, source_target_pairs={{0,16},{16,0},{1,17},{17,1},{2,18},{18,2},{3,19},{19,3},{4,20},{20... | collective-permute-start | bytes 626696 | tf_op jit(solution)/shard_map/ppermute | solution.py:181
  37.9 5.7 %collective-permute-start.10 = (f16[6,136,128]{2,1,0:T(8,128)(2,1)S(1)}, f16[6,136,128]{2,1,0:T(8,128)(2,1)S(1)}, u32[]{:S(2)}, u32[]{:S(2)}) collective-permute-start(f16[6,136,128]{2,1,0:T(8,128)(2,1)S(1)} %convert_element_type.48), channel_id=1, source_target_pairs={{0,16},{16,0},{1,17},{17,1},{2,18},{18,2},{3,19},{19,3},{4,20},{20... | collective-permute-start | bytes 626696 | tf_op jit(solution)/shard_map/ppermute | solution.py:181
  43.3 2.5 %collective-permute-start.7 = (f16[6,136,128]{2,1,0:T(8,128)(2,1)S(1)}, f16[6,136,128]{2,1,0:T(8,128)(2,1)S(1)}, u32[]{:S(2)}, u32[]{:S(2)}) collective-permute-start(f16[6,136,128]{2,1,0:T(8,128)(2,1)S(1)} %convert_element_type.42), channel_id=1, source_target_pairs={{0,16},{16,0},{1,17},{17,1},{2,18},{18,2},{3,19},{19,3},{4,20},{20... | collective-permute-start | bytes 626696 | tf_op jit(solution)/shard_map/ppermute | solution.py:181
  43.6 7.6 %collective-permute-start.9 = (f16[6,136,128]{2,1,0:T(8,128)(2,1)S(1)}, f16[6,136,128]{2,1,0:T(8,128)(2,1)S(1)}, u32[]{:S(2)}, u32[]{:S(2)}) collective-permute-start(f16[6,136,128]{2,1,0:T(8,128)(2,1)S(1)} %convert_element_type.46), channel_id=1, source_target_pairs={{0,4},{8,12},{4,0},{12,8},{1,5},{9,13},{5,1},{13,9},{2,6},{10,14},... | collective-permute-start | bytes 626696 | tf_op jit(solution)/shard_map/ppermute | solution.py:181
  43.9 9.4 %collective-permute-start.11 = (f16[6,136,128]{2,1,0:T(8,128)(2,1)S(1)}, f16[6,136,128]{2,1,0:T(8,128)(2,1)S(1)}, u32[]{:S(2)}, u32[]{:S(2)}) collective-permute-start(f16[6,136,128]{2,1,0:T(8,128)(2,1)S(1)} %convert_element_type.50), channel_id=1, source_target_pairs={{4,8},{8,4},{5,9},{9,5},{6,10},{10,6},{7,11},{11,7},{20,24},{24,20... | collective-permute-start | bytes 626696 | tf_op jit(solution)/shard_map/ppermute | solution.py:181
  53.5 0.8 %collective-permute-start.13 = (f16[2,136,128]{2,1,0:T(8,128)(2,1)S(1)}, f16[2,136,128]{2,1,0:T(8,128)(2,1)S(1)}, u32[]{:S(2)}, u32[]{:S(2)}) collective-permute-start(f16[2,136,128]{2,1,0:T(8,128)(2,1)S(1)} %convert_element_type.54), channel_id=1, source_target_pairs={{1,2},{2,1},{5,6},{6,5},{9,10},{10,9},{13,14},{14,13},{17,18},{18,... | collective-permute-start | bytes 208904 | tf_op jit(solution)/shard_map/ppermute | solution.py:181
  54.2 4.4 %collective-permute-start.12 = (f16[2,136,128]{2,1,0:T(8,128)(2,1)S(1)}, f16[2,136,128]{2,1,0:T(8,128)(2,1)S(1)}, u32[]{:S(2)}, u32[]{:S(2)}) collective-permute-start(f16[2,136,128]{2,1,0:T(8,128)(2,1)S(1)} %convert_element_type.52), channel_id=1, source_target_pairs={{0,1},{2,3},{1,0},{3,2},{4,5},{6,7},{5,4},{7,6},{8,9},{10,11},{9,8... | collective-permute-start | bytes 208904 | tf_op jit(solution)/shard_map/ppermute | solution.py:181
